TPU v7x, 32 devices: a whole 2x2x4 slice. The times are simulated.
32 devices in a mesh: ctx: 2 (over y), section: 4 (over x, core), tp: 4 (over z).
Axes of the slice: x: 2, y: 2, z: 4, core: 2. Of those that a mesh axis runs over, the one named last changes fastest.
Arguments:
- queries: bfloat16 [256, 8192], P('ctx', ('section', 'tp')), may hold values from -140 to 140
- keys: bfloat16 [256, 1024], P('ctx', 'section'), may hold values from -6 to 6
- values: bfloat16 [256, 1024], P('ctx', 'section'), may hold values from -36 to 36
- out_grad: bfloat16 [256, 8192], P('ctx', ('section', 'tp')), may hold values from -6 to 6
- enc_weight: bfloat16 [8192, 65536], P(('section', 'tp'), 'ctx'), may hold values from -0.0625 to 0.0625
- enc_bias: float32 [65536], P(('ctx', 'section', 'tp')), may hold values from -3 to 3
- dec_weight: bfloat16 [65536, 8192], P('ctx', ('section', 'tp')), may hold values from -0.0625 to 0.0625
Outputs:
- query_grad: bfloat16 [256, 8192], P('ctx', ('section', 'tp'))
- gradient_keys: bfloat16 [256, 1024], P('ctx', 'section')
- gradient_values: bfloat16 [256, 1024], P('ctx', 'section')
- feature_scores: float32 [65536], P(('ctx', 'section', 'tp'))
All inputs are finite; a program needn't handle non-finite values.
Results may differ from a plain program's by a relative error of at most 0.015.
Values may be sent and summed in bfloat16 or wider, within the bound.
No kernel may reach another device: no remote copies, remote signals or barrier semaphores. Data moves between devices by JAX's collectives and lax.ppermute only.
A program may use at most 256 MiB of HBM per device.

v0:
```python
import math

import jax
import jax.numpy as jnp
from jax import lax
from jax.sharding import PartitionSpec as P

QUERY_HEADS = 64
KEY_VALUE_HEADS = 8
HEAD_SIZE = 128
D_Z = 8192


NEGATIVE = -1e30


def passed_along(value, axis, steps):
    count = lax.axis_size(axis)
    pairs = [(source, (source + steps) % count) for source in range(count)]
    return lax.ppermute(value, axis, pairs)


def spread(value, axis, root):
    mine = lax.axis_index(axis) == root
    return lax.psum(jnp.where(mine, value, jnp.zeros_like(value)), axis)


def token_positions(device, row_count, cycle_size):
    half = row_count // 2
    local = jnp.arange(row_count, dtype=jnp.int32)
    block = jnp.where(local >= half, 2 * cycle_size - 1 - device, device)
    return block * half + local % half


def causal_block(query_pos, anchor, row_count, cycle_size):
    key_pos = token_positions(anchor, row_count, cycle_size)
    return query_pos[:, None] >= key_pos[None, :]


def pass_gradients(key_acc, value_acc):
    return passed_along((key_acc, value_acc), "ctx", -1)


def body(queries, keys, values, out_grad, enc_weight, enc_bias, dec_weight):
    row_count = queries.shape[0]
    heads_here = queries.shape[1] // HEAD_SIZE
    kv_here = keys.shape[1] // HEAD_SIZE
    group_width = QUERY_HEADS // KEY_VALUE_HEADS
    score_scale = 1.0 / math.sqrt(HEAD_SIZE)
    cycle_size = lax.axis_size("ctx")
    cycle_index = lax.axis_index("ctx")
    local_kv = lax.axis_index("tp") * heads_here // group_width
    key_own = lax.dynamic_slice_in_dim(keys, local_kv * HEAD_SIZE, HEAD_SIZE, 1)
    value_own = lax.dynamic_slice_in_dim(values, local_kv * HEAD_SIZE, HEAD_SIZE, 1)
    query_heads = queries.reshape(row_count, heads_here, HEAD_SIZE)
    grad_heads = out_grad.reshape(row_count, heads_here, HEAD_SIZE)
    query_pos = token_positions(cycle_index, row_count, cycle_size)
    store_count = 1

    def block_logits(turn, key_blk):
        anchor = (cycle_index + turn) % cycle_size
        causal_mask = causal_block(query_pos, anchor, row_count, cycle_size)
        logits = (
            jnp.einsum("qhd,kd->hqk", query_heads, key_blk, preferred_element_type=jnp.float32)
            * score_scale
        )
        return (causal_mask, logits)

    def forward_turn(turn, loop_state):
        key_blk, value_blk, running_max, running_sum, running_out, key_store, value_store = (
            loop_state
        )
        causal_mask, logits = block_logits(turn, key_blk)
        logits = jnp.where(causal_mask[None], logits, NEGATIVE)
        new_max = jnp.maximum(running_max, jnp.max(logits, axis=2))
        weights = jnp.where(causal_mask[None], jnp.exp(logits - new_max[:, :, None]), 0.0)
        factor = jnp.exp(running_max - new_max)
        running_sum = running_sum * factor + jnp.sum(weights, axis=2)
        weights_high = weights.astype(jnp.bfloat16)
        weights_low = (weights - weights_high.astype(jnp.float32)).astype(jnp.bfloat16)
        block_out = jnp.einsum(
            "hqk,kd->hqd", weights_high, value_blk, preferred_element_type=jnp.float32
        )
        block_out = block_out + jnp.einsum(
            "hqk,kd->hqd", weights_low, value_blk, preferred_element_type=jnp.float32
        )
        running_out = running_out * factor[:, :, None] + block_out
        key_blk, value_blk = passed_along((key_blk, value_blk), "ctx", -1)
        return (key_blk, value_blk, new_max, running_sum, running_out, key_store, value_store)

    empty_store = jnp.zeros((store_count, row_count, HEAD_SIZE), jnp.bfloat16)
    start_state = (
        key_own,
        value_own,
        jnp.full((heads_here, row_count), NEGATIVE, jnp.float32),
        jnp.zeros((heads_here, row_count), jnp.float32),
        jnp.zeros((heads_here, row_count, HEAD_SIZE), jnp.float32),
        empty_store,
        empty_store,
    )
    final_state = lax.fori_loop(0, cycle_size, forward_turn, start_state)
    running_max, running_sum, running_out, key_store, value_store = final_state[2:]
    log_total = running_max + jnp.log(running_sum)
    head_out = jnp.transpose(
        (running_out / running_sum[:, :, None]).astype(jnp.bfloat16), (1, 0, 2)
    )
    attn_flat = head_out.reshape(row_count, heads_here * HEAD_SIZE)
    row_dots = jnp.sum(grad_heads.astype(jnp.float32) * head_out.astype(jnp.float32), axis=2).T

    def gradient_terms(turn, key_blk, value_blk):
        causal_mask, logits = block_logits(turn, key_blk)
        weights = jnp.where(causal_mask[None], jnp.exp(logits - log_total[:, :, None]), 0.0)
        value_term = jnp.einsum(
            "hqk,qhd->kd",
            weights.astype(jnp.bfloat16),
            grad_heads,
            preferred_element_type=jnp.float32,
        )
        weight_grad = jnp.einsum(
            "qhd,kd->hqk", grad_heads, value_blk, preferred_element_type=jnp.float32
        )
        logit_half = (weights * (weight_grad - row_dots[:, :, None])).astype(jnp.bfloat16)
        query_term = jnp.einsum(
            "hqk,kd->qhd", logit_half, key_blk, preferred_element_type=jnp.float32
        )
        key_term = jnp.einsum(
            "hqk,qhd->kd", logit_half, query_heads, preferred_element_type=jnp.float32
        )
        return (query_term, key_term, value_term)

    zero_block = jnp.zeros((row_count, HEAD_SIZE), jnp.float32)
    zero_query = jnp.zeros((row_count, heads_here, HEAD_SIZE), jnp.float32)

    def moving_turn(turn, loop_state):
        key_blk, value_blk, key_acc, value_acc, query_acc = loop_state
        query_term, key_term, value_term = gradient_terms(turn, key_blk, value_blk)
        key_blk, value_blk = passed_along((key_blk, value_blk), "ctx", -1)
        key_acc, value_acc = pass_gradients(key_acc + key_term, value_acc + value_term)
        return (key_blk, value_blk, key_acc, value_acc, query_acc + query_term)

    moved_state = lax.fori_loop(
        0, cycle_size, moving_turn, (key_own, value_own, zero_block, zero_block, zero_query)
    )
    key_acc, value_acc, query_acc = moved_state[2:]
    query_grad = (
        (query_acc * score_scale).reshape(row_count, heads_here * HEAD_SIZE).astype(jnp.bfloat16)
    )
    head_slot = (jnp.arange(kv_here, dtype=jnp.int32) == local_kv)[None, :, None]
    key_full = jnp.where(head_slot, (key_acc * score_scale)[:, None, :], 0.0).reshape(
        row_count, kv_here * HEAD_SIZE
    )
    value_full = jnp.where(head_slot, value_acc[:, None, :], 0.0).reshape(
        row_count, kv_here * HEAD_SIZE
    )
    key_sum, value_sum = lax.psum((key_full, value_full), "tp")
    last_index = cycle_size - 1
    scored_out, scored_grad = (
        spread(attn_flat, "ctx", last_index),
        spread(out_grad, "ctx", last_index),
    )
    wide_out = scored_out.astype(jnp.float32)
    squares = lax.psum(jnp.sum(wide_out * wide_out, axis=1), ("section", "tp"))
    row_norm = jnp.sqrt(squares / D_Z + 1e-06)
    encoded_part = jnp.dot(scored_out, enc_weight, preferred_element_type=jnp.float32)
    attrib_part = lax.dot_general(
        scored_grad, dec_weight, (((1,), (1,)), ((), ())), preferred_element_type=jnp.float32
    )
    encoded, attrib = (
        lax.psum_scatter(encoded_part, ("section", "tp"), scatter_dimension=1, tiled=True),
        lax.psum_scatter(attrib_part, ("section", "tp"), scatter_dimension=1, tiled=True),
    )
    active = jnp.maximum(encoded / row_norm[:, None] + enc_bias[None, :], 0.0)
    feature_scores = jnp.sum(active * attrib, axis=0)
    return (
        query_grad,
        key_sum.astype(jnp.bfloat16),
        value_sum.astype(jnp.bfloat16),
        feature_scores,
    )


def solution(mesh):
    placed = (
        P("ctx", ("section", "tp")),
        P("ctx", "section"),
        P("ctx", "section"),
        P("ctx", ("section", "tp")),
        P(("section", "tp"), "ctx"),
        P(("ctx", "section", "tp")),
        P("ctx", ("section", "tp")),
    )
    return jax.shard_map(
        body,
        mesh=mesh,
        in_specs=placed,
        out_specs=(
            P("ctx", ("section", "tp")),
            P("ctx", "section"),
            P("ctx", "section"),
            P(("ctx", "section", "tp")),
        ),
        check_vma=False,
    )
```

profile of v0, /device:TPU:0, one launch (start us, length us, event | category | flops | bytes accessed | tf_op | source)
XLA Modules:
  0.0 448.3 jit_solution(17951976722139428715)
XLA Ops:
  7.3 0.8 constant_dynamic-slice_fusion
  8.1 1.0 copy.18
  9.2 11.2 %while.54 = (s32[]{:T(128)}, bf16[128,128]{1,0:T(8,128)(2,1)S(1)}, bf16[128,128]{1,0:T(8,128)(2,1)S(1)}, f32[4,128]{1,0:T(4,128)S(1)}, f32[4,128]{1,0:T(4,128)S(...) while((s32[]{:T(128)}, bf16[128,128]{1,0:T(8,128)(2,1)S(1)}, ...), condition=%wide.region_3.4_spmd.clone.clone.clone, body=%wide.region_0.3_spmd.clone.clone.clone.sunk | while | flops 51598352 | bytes 2838894 | solution.py:101
  9.3 3.0 collective-permute-start
  12.5 0.2 fusion.96
  12.8 0.2 fusion.99
  13.0 0.3 fusion.100
  13.3 0.9 collective-permute-done
  14.2 2.0 collective-permute-done.1
  16.2 0.3 collective-permute-start
  16.6 1.7 collective-permute-start.1
  18.4 0.2 fusion.96
  18.7 0.2 fusion.99
  18.9 0.3 fusion.100
  19.2 1.0 collective-permute-done
  20.1 0.4 collective-permute-done.1
  20.6 0.7 broadcast_select_fusion
  21.3 0.7 broadcast_select_fusion.1
  22.1 25.8 %all-reduce.5.cloned.1.call-done = (bf16[128,512]{1,0:T(8,128)(2,1)}, bf16[128,512]{0,1:T(8,128)(2,1)}) async-done(((bf16[128,512]{1,0:T(8,128)(2,1)}, bf16[128,512]{0,1:T(8,128)(2,1)}), (bf16[128,512]{1,0:T(8,128)(2,1)}, bf16[128,512]{0,1:T(8,128)(2,1)})) %all-reduce.5.cloned.1.call-update) | async-done | bytes 262160 | tf_op jit(solution)/shard_map/psum | solution.py:25
  47.8 21.1 %fusion.48 = f32[128,32768]{1,0:T(8,128)} fusion(bf16[128,512]{0,1:T(8,128)(2,1)} %get-tuple-element.839, bf16[512,32768]{1,0:T(8,128)(2,1)} %param.15), kind=kOutput, calls=%fused_computation.83 | convolution fusion | flops 4294967296 | bytes 50462720 | tf_op jit(solution)/shard_map/dot_general | solution.py:164
  69.1 24.8 %fusion.49 = f32[128,32768]{1,0:T(8,128)} fusion(bf16[128,512]{1,0:T(8,128)(2,1)S(1)} %copy-done.2, bf16[32768,512]{1,0:T(8,128)(2,1)} %param.17), kind=kOutput, calls=%fused_computation.84 | convolution fusion | flops 4294967296 | bytes 50462720 | tf_op jit(solution)/shard_map/dot_general | solution.py:165
  94.3 16.7 %while.55 = (s32[]{:T(128)}, bf16[128,128]{1,0:T(8,128)(2,1)S(1)}, bf16[128,128]{1,0:T(8,128)(2,1)S(1)}, f32[128,128]{1,0:T(8,128)S(1)}, f32[128,128]{1,0:T(8,12...) while((s32[]{:T(128)}, bf16[128,128]{1,0:T(8,128)(2,1)S(1)}, ...), condition=%wide.region_6.7_spmd.clone.clone.clone, body=%wide.region_5.6_spmd.clone.clone.clone.sunk | while | flops 84527632 | bytes 3545556 | solution.py:141
  94.3 0.2 collective-permute-start.3
  94.6 1.9 collective-permute-start.2
  96.5 0.2 fusion.113
  96.7 0.2 fusion.114
  96.9 0.2 fusion.115
  97.1 0.2 collective-permute-start.4
  97.5 1.9 collective-permute-start.5
  99.5 0.2 fusion.117
  99.7 1.7 collective-permute-done.4
  101.5 0.7 collective-permute-done.5
  102.2 1.6 collective-permute-start.3
  103.7 0.5 collective-permute-start.2
  104.3 0.2 fusion.113
  104.5 0.2 fusion.114
  104.7 0.2 fusion.115
  104.9 1.6 collective-permute-start.4
  106.7 0.5 collective-permute-start.5
  107.2 0.2 fusion.117
  107.7 1.6 collective-permute-done.4
  109.2 1.8 collective-permute-done.5
  111.2 33.0 %all-reduce.6 = (bf16[128,256]{1,0:T(8,128)(2,1)}, bf16[128,256]{1,0:T(8,128)(2,1)}) all-reduce(f32[128,256]{1,0:T(8,128)S(1)} %get-tuple-element.845, f32[128,256]{1,0:T(8,128)S(1)} %get-tuple-element.844), channel_id=1, replica_groups=mesh['ctx'=2,'section'=4,'tp'=4] {'tp'}, use_global_device_ids=true, to_apply=%region_7.8 | all-reduce | flops 65536 | bytes 393216 | tf_op jit(solution)/shard_map/psum | solution.py:155
  144.3 0.7 copy_bitcast_fusion
  145.0 32.5 %psum.38 = f32[128]{0:T(128)S(1)} all-reduce(f32[128]{0:T(128)S(1)} %multiply_reduce_fusion.1), channel_id=1, replica_groups=mesh['ctx'=2,'section'=4,'tp'=4] {'section','tp'}, use_global_device_ids=true, to_apply=%region_12.13 | all-reduce | flops 128 | bytes 1024 | tf_op jit(solution)/shard_map/psum | solution.py:162
  177.5 79.6 %reduce-scatter.3.cloned.1.call-done = f32[128,2048]{1,0:T(8,128)} async-done(((f32[128,32768]{1,0:T(8,128)}), f32[128,2048]{1,0:T(8,128)}) %reduce-scatter.3.cloned.1.call-update) | async-done | bytes 1048592 | tf_op jit(solution)/shard_map/reduce_scatter | solution.py:169
  257.1 182.2 %reduce-scatter.5.cloned.1.call-done = f32[128,2048]{1,0:T(8,128)} async-done(((f32[128,32768]{1,0:T(8,128)}), f32[128,2048]{1,0:T(8,128)}) %reduce-scatter.5.cloned.1.call-update) | async-done | bytes 1048592 | tf_op jit(solution)/shard_map/reduce_scatter | solution.py:170
  439.4 2.4 multiply_reduce_fusion
  (71 shorter events, 2.3 us)
Async XLA Ops:
  7.2 40.6 %all-reduce.5.cloned.1.call-start = ((), (), s32[]{:S(2)}) async-start(), calls=%async_computation.4 | async-start | bytes 524288 | tf_op jit(solution)/shard_map/psum | solution.py:25
  9.3 4.9 %collective-permute-start = (bf16[128,128]{1,0:T(8,128)(2,1)S(1)}, bf16[128,128]{1,0:T(8,128)(2,1)S(1)}, u32[]{:S(2)}, u32[]{:S(2)}) collective-permute-start(bf16[128,128]{1,0:T(8,128)(2,1)S(1)} %copy.41), channel_id=1, source_target_pairs={{0,16},{16,0},{1,17},{17,1},{2,18},{18,2},{3,19},{19,3},{4,20},{20... | collective-permute-start | bytes 98312 | tf_op jit(solution)/shard_map/while/body/eval_jaxpr/ppermute | solution.py:20
  12.3 3.9 collective-permute-start.1
  16.2 3.9 collective-permute-start
  16.6 3.9 collective-permute-start.1
  22.0 235.1 %reduce-scatter.3.cloned.1.call-start = ((), (), s32[]{:S(2)}) async-start(), calls=%async_computation.2 | async-start | bytes 17825792 | tf_op jit(solution)/shard_map/reduce_scatter | solution.py:169
  47.8 21.2 %copy-start.2 = (bf16[128,512]{1,0:T(8,128)(2,1)S(1)}, bf16[128,512]{1,0:T(8,128)(2,1)}, u32[]{:S(2)}) copy-start(bf16[128,512]{1,0:T(8,128)(2,1)} %get-tuple-element.838) | copy-start | bytes 393220
  69.0 370.4 %reduce-scatter.5.cloned.1.call-start = ((), (), s32[]{:S(2)}) async-start(), calls=%async_computation.3 | async-start | bytes 17825792 | tf_op jit(solution)/shard_map/reduce_scatter | solution.py:170
  69.0 24.8 %copy-start.1 = (bf16[128,512]{1,0:T(8,128)(2,1)S(1)}, bf16[128,512]{1,0:T(8,128)(2,1)}, u32[]{:S(2)}) copy-start(bf16[128,512]{1,0:T(8,128)(2,1)} %param.14) | copy-start | bytes 393220
  69.0 75.9 %copy-start = (bf16[128,512]{0,1:T(8,128)(2,1)S(1)}, bf16[128,512]{0,1:T(8,128)(2,1)}, u32[]{:S(2)}) copy-start(bf16[128,512]{0,1:T(8,128)(2,1)} %get-tuple-element.839) | copy-start | bytes 393220
  69.1 370.3 %copy-start.3 = (f32[2048]{0:T(1024)S(1)}, f32[2048]{0:T(1024)}, u32[]{:S(2)}) copy-start(f32[2048]{0:T(1024)} %param.16) | copy-start | bytes 24580
  94.3 5.4 %collective-permute-start.3 = (bf16[128,128]{1,0:T(8,128)(2,1)S(1)}, bf16[128,128]{1,0:T(8,128)(2,1)S(1)}, u32[]{:S(2)}, u32[]{:S(2)}) collective-permute-start(bf16[128,128]{1,0:T(8,128)(2,1)S(1)} %copy.60), channel_id=1, source_target_pairs={{0,16},{16,0},{1,17},{17,1},{2,18},{18,2},{3,19},{19,3},{4,20},{20... | collective-permute-start | bytes 98312 | tf_op jit(solution)/shard_map/while/body/eval_jaxpr/ppermute | solution.py:20
  94.6 5.2 %collective-permute-start.2 = (bf16[128,128]{1,0:T(8,128)(2,1)S(1)}, bf16[128,128]{1,0:T(8,128)(2,1)S(1)}, u32[]{:S(2)}, u32[]{:S(2)}) collective-permute-start(bf16[128,128]{1,0:T(8,128)(2,1)S(1)} %copy.59), channel_id=1, source_target_pairs={{0,16},{16,0},{1,17},{17,1},{2,18},{18,2},{3,19},{19,3},{4,20},{20... | collective-permute-start | bytes 98312 | tf_op jit(solution)/shard_map/while/body/eval_jaxpr/ppermute | solution.py:20
  97.1 4.3 collective-permute-start.4
  97.5 4.6 %collective-permute-start.5 = (f32[128,128]{1,0:T(8,128)S(1)}, f32[128,128]{1,0:T(8,128)S(1)}, u32[]{:S(2)}, u32[]{:S(2)}) collective-permute-start(f32[128,128]{1,0:T(8,128)S(1)} %fusion.116), channel_id=1, source_target_pairs={{0,16},{16,0},{1,17},{17,1},{2,18},{18,2},{3,19},{19,3},{4,20},{20... | collective-permute-start | bytes 196616 | tf_op jit(solution)/shard_map/while/body/eval_jaxpr/ppermute | solution.py:20
  102.2 5.3 %collective-permute-start.3 = (bf16[128,128]{1,0:T(8,128)(2,1)S(1)}, bf16[128,128]{1,0:T(8,128)(2,1)S(1)}, u32[]{:S(2)}, u32[]{:S(2)}) collective-permute-start(bf16[128,128]{1,0:T(8,128)(2,1)S(1)} %copy.60), channel_id=1, source_target_pairs={{0,16},{16,0},{1,17},{17,1},{2,18},{18,2},{3,19},{19,3},{4,20},{20... | collective-permute-start | bytes 98312 | tf_op jit(solution)/shard_map/while/body/eval_jaxpr/ppermute | solution.py:20
  103.7 3.9 collective-permute-start.2
  104.9 4.3 collective-permute-start.4
  106.7 4.3 collective-permute-start.5
Sparse Core Ops, SparseCore 0:
  22.1 25.6 all-reduce.4
  69.1 187.9 reduce-scatter.2
  261.8 177.5 reduce-scatter.4
where the time goes:
time: 449 us; the launch traced here: 448 us
  waiting for transfers between devices  298 us (66%)
  blocking collectives  65.5 us (15%)
  matrix products  49.3 us (11%)
  between operations  13.9 us (3%)
  starting transfers between devices  13.7 us (3%)
  other arithmetic  5.2 us (1%)
    reduce_scatter x1, waiting for transfers between devices, body(): lax.psum_scatter(attrib_part, ('section', 'tp'), scatter_dimension=1, til...  182 us
    reduce_scatter x1, waiting for transfers between devices, body(): lax.psum_scatter(encoded_part, ('section', 'tp'), scatter_dimension=1, ti...  79.6 us
    psum x1, blocking collectives, body(): key_sum, value_sum = lax.psum((key_full, value_full), 'tp')  33 us
    psum x1, blocking collectives, body(): squares = lax.psum(jnp.sum(wide_out * wide_out, axis=1), ('section', 'tp'))  32.5 us
    psum x1, waiting for transfers between devices, spread(): return lax.psum(jnp.where(mine, value, jnp.zeros_like(value)), axis)  25.8 us
    dot_general x1, matrix products, body(): lax.dot_general(scored_grad, dec_weight, (((1,), (1,)), ((), ())), prefer...  24.8 us
    dot_general x1, matrix products, body(): jnp.dot(scored_out, enc_weight, preferred_element_type=jnp.float32)  21.1 us
    ppermute x12, starting transfers between devices, passed_along(): return lax.ppermute(value, axis, pairs)  13.6 us
  transfers between devices with their start and end apart: 15, of which 12 were waited for; matrix products, arithmetic and copies ran while one was open for 7% of the time, Pallas kernels for 0%

commit v1 on v0

v1 whole, which is shorter than its diff:
```python
import functools
import math

import jax
import jax.numpy as jnp
from jax import lax
from jax.experimental import pallas as pl
from jax.experimental.pallas import tpu as pltpu
from jax.sharding import PartitionSpec as P

QUERY_HEADS = 64
KEY_VALUE_HEADS = 8
HEAD_SIZE = 128
D_Z = 8192

SCHEDULE = (
    ("dec", 0, 384, (0, 1, 3, 5, 7)),
    ("dec", 384, 640, (0, 2, 4, 6, 8)),
    ("dec", 1024, 1024, (1, 3, 5, 7, 9)),
    ("enc", 1280, 768, (2, 4, 6, 8, 10)),
    ("enc", 640, 640, (3, 5, 7, 9, 10)),
    ("enc", 256, 384, (4, 6, 8, 10, 11)),
    ("enc", 0, 256, (5, 7, 9, 10, 11)),
)
SHORT_SCHEDULE = (("dec", 0, 1, (0, 2, 4, 6, 8)), ("enc", 0, 1, (1, 3, 5, 7, 9)))
COST = 100
ATTENTION_STEP = 0
FIRST_SQUARES = 4
FIRST_TERMS = 3


def shifted(value, axis, steps):
    count = lax.axis_size(axis)
    return lax.ppermute(value, axis, [(i, (i + steps) % count) for i in range(count)])


def swapped(value, axis, mask):
    count = lax.axis_size(axis)
    return lax.ppermute(value, axis, [(i, i ^ mask) for i in range(count)])


def from_last(value, axis):
    count = lax.axis_size(axis)
    rank = count - 1 - lax.axis_index(axis)
    reach = 1
    while reach < count:
        pairs = [
            (count - 1 - i, count - 1 - i - reach) for i in range(reach) if i + reach < count
        ]
        moved = lax.ppermute(value, axis, pairs)
        value = jnp.where((rank >= reach) & (rank < 2 * reach), moved, value)
        reach *= 2
    return value


def attention_kernel(cycle_size, queries, out_grad, *refs):
    pairs, (attn, query_grad, *terms) = refs[:cycle_size], refs[cycle_size:]
    rows, columns = queries.shape
    half = rows // 2
    scale = 1.0 / math.sqrt(HEAD_SIZE)
    me = lax.axis_index("ctx")

    def positions(device, axis):
        local = lax.broadcasted_iota(jnp.int32, (rows, rows), axis)
        late = (2 * cycle_size - 1 - device) * half + local - half
        return jnp.where(local >= half, late, device * half + local)

    mine = positions(me, 0)
    causal = jnp.concatenate(
        [
            (mine - positions(lax.rem(me + turn, cycle_size), 1)).astype(jnp.float32)
            for turn in range(cycle_size)
        ],
        axis=1,
    ) >= 0.0
    keys = jnp.concatenate([ref[0] for ref in pairs], axis=0)
    values = jnp.concatenate([ref[1] for ref in pairs], axis=0)
    key_term = value_term = 0.0

    def dot(left, right, left_dim, right_dim):
        return lax.dot_general(
            left, right, (((left_dim,), (right_dim,)), ((), ())),
            preferred_element_type=jnp.float32,
        )

    for first in range(0, columns, HEAD_SIZE):
        head = slice(first, first + HEAD_SIZE)
        query, grad = queries[:, head], out_grad[:, head]
        logits = jnp.where(causal, dot(query, keys, 1, 1) * scale, -1e30)
        raised = jnp.where(causal, jnp.exp(logits - jnp.max(logits, axis=1, keepdims=True)), 0.0)
        weights = raised / jnp.sum(raised, axis=1, keepdims=True)
        high = weights.astype(jnp.bfloat16)
        low = (weights - high.astype(jnp.float32)).astype(jnp.bfloat16)
        out = (dot(high, values, 1, 0) + dot(low, values, 1, 0)).astype(jnp.bfloat16)
        attn[:, head] = out
        row_dots = jnp.sum(
            grad.astype(jnp.float32) * out.astype(jnp.float32), axis=1, keepdims=True
        )
        value_term += dot(high, grad, 0, 0)
        logit_half = (weights * (dot(grad, values, 1, 1) - row_dots)).astype(jnp.bfloat16)
        query_grad[:, head] = (dot(logit_half, keys, 1, 0) * scale).astype(jnp.bfloat16)
        key_term += dot(logit_half, query, 0, 0)
    for turn, ref in enumerate(terms):
        block = slice(turn * rows, (turn + 1) * rows)
        ref[0] = key_term[block] * scale
        ref[1] = value_term[block]


def relative_blocks(order, stage, size):
    done = sum(order[:stage])
    bit = order[stage] if stage < len(order) else 0
    return [r for r in range(size) if not r & done and (r & bit or r == bit)]


class Chunk:
    def __init__(self, kind, offset, width, steps, order):
        self.kind, self.offset, self.width, self.order = kind, offset, width, order
        self.steps = steps
        self.received = []
        self.result = None


def step_kernel(plan, size, latents, tp, *refs):
    refs = list(refs)
    take = lambda count: [refs.pop(0) for _ in range(count)]
    sources = {kind: take(2) for kind in plan["kinds"]}
    jobs = plan["jobs"]
    incoming = [take(stage) for _, stage in jobs]
    extras = [take(2 + len(pieces)) if pieces else () for pieces in plan["pieces"]]
    outs = take(len(jobs))
    weight_bufs, sum_bufs, out_bufs = [], [], []
    for _, stage in jobs:
        weight_bufs.append(take(1)[0])
        sum_bufs.append(take(stage))
        out_bufs.append(take(1)[0])
    sems = take(1)[0]
    me = lax.axis_index("section") * tp + lax.axis_index("tp")
    used = 0

    def copy(source, target):
        nonlocal used
        used += 1
        return pltpu.make_async_copy(source, target, sems.at[used - 1])

    arrivals = []
    for number, (chunk, stage) in enumerate(jobs):
        blocks = relative_blocks(chunk.order, stage, size)
        weight = sources[chunk.kind][1]
        for index, r in enumerate(blocks):
            first = pl.multiple_of((me ^ r) * latents + chunk.offset, 128)
            if chunk.kind == "dec":
                piece = weight.at[pl.ds(first, chunk.width), :]
            else:
                piece = weight.at[:, pl.ds(first, chunk.width)]
            wanted = [copy(piece, weight_bufs[number].at[index])]
            for earlier in range(stage):
                sent = relative_blocks(chunk.order, earlier, size)
                place = sent.index(r ^ chunk.order[earlier])
                wanted.append(
                    copy(incoming[number][earlier].at[place], sum_bufs[number][earlier].at[index])
                )
            for item in wanted:
                item.start()
            arrivals.append(wanted)
    leaving = []
    for number, (chunk, stage) in enumerate(jobs):
        act = sources[chunk.kind][0]
        for index in range(len(relative_blocks(chunk.order, stage, size))):
            for item in arrivals.pop(0):
                item.wait()
            total = lax.dot_general(
                act[...],
                weight_bufs[number][index],
                (((1,), (1 if chunk.kind == "dec" else 0,)), ((), ())),
                preferred_element_type=jnp.float32,
            )
            for buf in sum_bufs[number]:
                total = total + buf[index].astype(jnp.float32)
            if plan["pieces"][number]:
                inverse, bias, *attribs = extras[number]
                active = jnp.maximum(total * inverse[:, :1] + bias[...], 0.0)
                attrib = [
                    ref[0, :, first:last]
                    for ref, (first, last) in zip(attribs, plan["pieces"][number])
                ]
                attrib = attrib[0] if len(attrib) == 1 else jnp.concatenate(attrib, axis=1)
                total = jnp.sum(active * attrib, axis=0, keepdims=True)
            out_bufs[number][index] = total.astype(out_bufs[number].dtype)
            item = copy(out_bufs[number].at[index], outs[number].at[index])
            item.start()
            leaving.append(item)
    for item in leaving:
        item.wait()


def run_step(jobs, acts, weights, size, latents, tp, finish):
    kinds = [kind for kind in ("dec", "enc") if any(c.kind == kind for c, _ in jobs)]
    rows, inner = acts[kinds[0]].shape
    operands, specs = [], []
    anywhere = pl.BlockSpec(memory_space=pltpu.HBM)
    vmem = pl.BlockSpec(memory_space=pltpu.VMEM)
    for kind in kinds:
        operands += [acts[kind], weights[kind]]
        specs += [vmem, anywhere]
    for chunk, stage in jobs:
        operands += chunk.received[:stage]
        specs += [anywhere] * stage
    outs, scratch, copies, flops, moved = [], [], 0, 0, 0
    pieces = []
    for chunk, stage in jobs:
        last = stage == len(chunk.order)
        pieces.append(())
        if last and chunk.kind == "enc":
            values, pieces[-1] = finish(chunk)
            operands += values
            specs += [vmem] * len(values)
        count = len(relative_blocks(chunk.order, stage, size))
        shape = (count, rows, chunk.width)
        if last:
            dtype = jnp.float32
            if chunk.kind == "enc":
                shape = (1, 1, chunk.width)
        else:
            dtype = jnp.bfloat16
        outs.append(jax.ShapeDtypeStruct(shape, dtype))
        side = (chunk.width, inner) if chunk.kind == "dec" else (inner, chunk.width)
        scratch.append(pltpu.VMEM((count, *side), jnp.bfloat16))
        scratch += [pltpu.VMEM((count, rows, chunk.width), jnp.bfloat16)] * stage
        scratch.append(pltpu.VMEM(shape, dtype))
        copies += count * (stage + 2)
        flops += 2 * count * rows * inner * chunk.width
        moved += 2 * count * chunk.width * (inner + (stage + 1) * rows)
    results = pl.pallas_call(
        functools.partial(step_kernel, {"kinds": kinds, "jobs": jobs, "pieces": pieces}, size, latents, tp),
        out_shape=outs,
        in_specs=specs,
        out_specs=[anywhere] * len(outs),
        scratch_shapes=[*scratch, pltpu.SemaphoreType.DMA((copies,))],
        compiler_params=pltpu.CompilerParams(vmem_limit_bytes=24 * 2**20),
        cost_estimate=pl.CostEstimate(
            flops=int(COST * flops), bytes_accessed=int(COST * moved), transcendentals=0
        ),
    )(*operands)
    for kind in acts:
        acts[kind], _ = lax.optimization_barrier((acts[kind], results[0]))
    for (chunk, stage), value in zip(jobs, results):
        chunk.latest = value
        if stage == len(chunk.order):
            chunk.result = value
        elif chunk.order[stage] >= tp:
            chunk.received.append(swapped(value, "section", chunk.order[stage] // tp))
        else:
            chunk.received.append(swapped(value, "tp", chunk.order[stage]))


def body(queries, keys, values, out_grad, enc_weight, enc_bias, dec_weight):
    row_count = queries.shape[0]
    heads_here = queries.shape[1] // HEAD_SIZE
    kv_here = keys.shape[1] // HEAD_SIZE
    group_width = QUERY_HEADS // KEY_VALUE_HEADS
    cycle_size = lax.axis_size("ctx")
    section_size, tp_size = lax.axis_size("section"), lax.axis_size("tp")
    tp_index = lax.axis_index("tp")
    local_kv = tp_index * heads_here // group_width
    group = (
        lax.axis_index("section") * tp_size + tp_index,
        section_size * tp_size,
        tp_size,
    )
    core, across, near, far = tp_size, 2 * tp_size, 1, 2
    order = (core, across, near, far)

    scored_grad = from_last(out_grad, "ctx")
    latents = enc_weight.shape[1] // group[1]
    weights = {"dec": dec_weight, "enc": enc_weight}
    full = max(first + width for _, first, width, _ in SCHEDULE)
    schedule, unit = (SHORT_SCHEDULE, latents) if latents % full else (SCHEDULE, latents // full)
    chunks = [
        Chunk(kind, first * unit, width * unit, times, order)
        for kind, first, width, times in schedule
    ]
    steps = [
        [(chunk, chunk.steps.index(step)) for chunk in chunks if step in chunk.steps]
        for step in range(1 + max(chunk.steps[-1] for chunk in chunks))
    ]
    acts = {"dec": scored_grad}
    early = next(step for step, jobs in enumerate(steps) if any(c.kind == "enc" for c, _ in jobs))
    for step in range(early):
        run_step(steps[step], acts, weights, group[1], latents, tp_size, None)
        if step == ATTENTION_STEP:
            queries, _ = lax.optimization_barrier((queries, acts["dec"]))

    pair = jnp.stack(
        [
            lax.dynamic_slice_in_dim(keys, local_kv * HEAD_SIZE, HEAD_SIZE, 1),
            lax.dynamic_slice_in_dim(values, local_kv * HEAD_SIZE, HEAD_SIZE, 1),
        ]
    )
    pairs = [pair] + [shifted(pair, "ctx", -turn) for turn in range(1, cycle_size)]
    attn_flat, query_grad, *terms = pl.pallas_call(
        functools.partial(attention_kernel, cycle_size),
        out_shape=[
            jax.ShapeDtypeStruct(queries.shape, jnp.bfloat16),
            jax.ShapeDtypeStruct(queries.shape, jnp.bfloat16),
            *[jax.ShapeDtypeStruct(pair.shape, jnp.float32)] * cycle_size,
        ],
        compiler_params=pltpu.CompilerParams(vmem_limit_bytes=32 * 2**20),
    )(queries, out_grad, *pairs)
    scored_out = from_last(attn_flat, "ctx")
    wide_out = scored_out.astype(jnp.float32)
    squares = jnp.sum(wide_out * wide_out, axis=1)
    acts["enc"], _ = lax.optimization_barrier((scored_out, acts["dec"]))

    def add_squares(axis, mask, token):
        nonlocal squares
        other = swapped(squares, axis, mask)
        squares, _ = lax.optimization_barrier((squares, token))
        squares = squares + other

    def gather_blocks(token):
        nonlocal summed
        others = [shifted(terms[turn], "ctx", turn) for turn in range(1, cycle_size)]
        summed, _ = lax.optimization_barrier((terms[0], token))
        for other in others:
            summed = summed + other

    def add_heads(mask, token):
        nonlocal summed
        other = swapped(summed, "tp", mask)
        summed, _ = lax.optimization_barrier((summed, token))
        summed = summed + other

    def gather_heads(token):
        nonlocal summed
        half = summed.astype(jnp.bfloat16)
        others = [swapped(half, "tp", share * step) for step in range(1, kv_here)]
        half, _ = lax.optimization_barrier((half, token))
        slots, columns = [half, *others], []
        for column in range(kv_here):
            value = slots[0]
            for step in range(1, kv_here):
                value = jnp.where((local_kv ^ step) == column, slots[step], value)
            columns.append(value)
        summed = jnp.concatenate(columns, axis=2)

    summed = terms[0]
    share = group_width // heads_here
    bits = lambda count: [1 << i for i in range((count - 1).bit_length())]
    tasks = {}
    square_tasks = [functools.partial(add_squares, "section", m) for m in bits(section_size)]
    square_tasks += [functools.partial(add_squares, "tp", m) for m in bits(tp_size)]
    term_tasks = [gather_blocks]
    term_tasks += [functools.partial(add_heads, mask) for mask in bits(share)]
    term_tasks += [gather_heads]
    for first, items in ((FIRST_SQUARES, square_tasks), (FIRST_TERMS, term_tasks)):
        for number, item in enumerate(items):
            tasks.setdefault(first + number, []).append(item)

    bias = enc_bias.reshape(1, latents)

    def finish(chunk):
        end = chunk.offset + chunk.width
        inverse = jnp.broadcast_to(
            lax.rsqrt(squares / D_Z + 1e-06)[:, None], (row_count, HEAD_SIZE)
        )
        values, pieces = [inverse, lax.slice_in_dim(bias, chunk.offset, end, axis=1)], []
        for other in chunks:
            first, last = max(other.offset, chunk.offset), min(other.offset + other.width, end)
            if other.kind == "dec" and first < last:
                values.append(other.result)
                pieces.append((first - other.offset, last - other.offset))
        return values, pieces

    for step, jobs in enumerate(steps[early:], early):
        run_step(jobs, acts, weights, group[1], latents, tp_size, finish)
        for task in tasks.get(step, ()):
            task(acts["enc"])
        if step in tasks:
            acts["enc"], _, _ = lax.optimization_barrier((acts["enc"], squares, summed))
    scores = sorted((c for c in chunks if c.kind == "enc"), key=lambda c: c.offset)
    feature_scores = jnp.concatenate([c.result[0] for c in scores], axis=1).reshape(latents)
    return (query_grad, summed[0], summed[1], feature_scores)


def solution(mesh):
    placed = (
        P("ctx", ("section", "tp")),
        P("ctx", "section"),
        P("ctx", "section"),
        P("ctx", ("section", "tp")),
        P(("section", "tp"), "ctx"),
        P(("ctx", "section", "tp")),
        P("ctx", ("section", "tp")),
    )
    return jax.shard_map(
        body,
        mesh=mesh,
        in_specs=placed,
        out_specs=(
            P("ctx", ("section", "tp")),
            P("ctx", "section"),
            P("ctx", "section"),
            P(("ctx", "section", "tp")),
        ),
        check_vma=False,
    )
```

time: 449 us -> 182 us (0.41)
  waiting for transfers between devices: 298 us -> 61.3 us
  Pallas kernels: 0 us -> 75.7 us
  blocking collectives: 65.5 us -> 0 us
  matrix products: 49.3 us -> 0 us
  starting transfers between devices: 13.7 us -> 38.7 us
  between operations: 13.9 us -> 1.02 us
    reduce_scatter x2 -> x0, waiting for transfers between devices: 262 us -> none  [the longest x1 182 us: body(): lax.psum_scatter(attrib_part, ('section', 'tp'), scatter_dimension=1, til...]
    pallas_call x0 -> x13, Pallas kernels: none -> 75.7 us  [the longest x12 72.9 us: run_step(): pl.pallas_call(functools.partial(step_kernel, {'kinds': kinds, 'jobs': jo...]
    psum x2 -> x0, blocking collectives: 65.5 us -> none  [the longest x1 33 us: body(): key_sum, value_sum = lax.psum((key_full, value_full), 'tp')]
    ppermute x12 -> x38, waiting for transfers between devices: 10.2 us -> 61.3 us  [the longest x34 46.6 us: swapped(): return lax.ppermute(value, axis, [(i, i ^ mask) for i in range(count)])]
    dot_general x18 -> x0, matrix products: 49.3 us -> none  [the longest x1 24.8 us: body(): lax.dot_general(scored_grad, dec_weight, (((1,), (1,)), ((), ())), prefer...]
    psum x1 -> x0, waiting for transfers between devices: 25.8 us -> none  [spread(): return lax.psum(jnp.where(mine, value, jnp.zeros_like(value)), axis)]
    ppermute x12 -> x38, starting transfers between devices: 13.6 us -> 38.7 us  [the longest x34 32.8 us: swapped(): return lax.ppermute(value, axis, [(i, i ^ mask) for i in range(count)])]
  transfers between devices with their start and end apart: 15 -> 38, of which waited for: 12 -> 12; matrix products, arithmetic and copies ran while one was open for 7% -> 2% of each run, Pallas kernels for 0% -> 33%
where the time goes in v1:
time: 182 us
  Pallas kernels  75.7 us (42%)
  waiting for transfers between devices  61.3 us (34%)
  starting transfers between devices  38.7 us (21%)
  other arithmetic  4.25 us (2%)
    pallas_call x12, Pallas kernels, run_step(): pl.pallas_call(functools.partial(step_kernel, {'kinds': kinds, 'jobs': jo...  72.9 us
    ppermute x34, waiting for transfers between devices, swapped(): return lax.ppermute(value, axis, [(i, i ^ mask) for i in range(count)])  46.6 us
    ppermute x34, starting transfers between devices, swapped(): return lax.ppermute(value, axis, [(i, i ^ mask) for i in range(count)])  32.8 us
    ppermute x2, waiting for transfers between devices, from_last(): moved = lax.ppermute(value, axis, pairs)  10.9 us
    ppermute x2, waiting for transfers between devices, shifted(): lax.ppermute(value, axis, [(i, (i + steps) % count) for i in range(count)])  3.9 us
  transfers between devices with their start and end apart: 38, of which 12 were waited for; matrix products, arithmetic and copies ran while one was open for 2% of the time, Pallas kernels for 33%

profile of v1, /device:TPU:0, one launch (start us, length us, event | category | flops | bytes accessed | tf_op | source)
XLA Modules:
  0.0 181.8 jit_solution(601075862280182777)
XLA Ops:
  0.6 1.3 collective-permute-start
  1.9 6.7 %collective-permute-done = bf16[128,512]{1,0:T(8,128)(2,1)S(1)} collective-permute-done((bf16[128,512]{1,0:T(8,128)(2,1)}, bf16[128,512]{1,0:T(8,128)(2,1)S(1)}, u32[]{:S(2)}, u32[]{:S(2)}) %collective-permute-start) | collective-permute-done | bytes 131104 | tf_op jit(solution)/shard_map/ppermute | solution.py:50
  8.7 9.3 %shard_map.102 = (bf16[8,128,384]{2,1,0:T(8,128)(2,1)S(1)}, bf16[8,128,640]{2,1,0:T(8,128)(2,1)S(1)}) custom-call(bf16[128,512]{1,0:T(8,128)(2,1)S(1)} %broadcast_select_fusion.1.refs_0_, bf16[32768,512]{1,0:T(8,128)(2,1)} %refs_1_.21), custom_call_target="tpu_custom_call" | custom-call | flops 107374182400 | bytes 1048576000 | tf_op jit(solution)/shard_map/pallas_call | solution.py:233
  18.2 0.6 collective-permute-start.1
  18.8 3.9 %collective-permute-done.1.refs_1_ = bf16[2,128,128]{2,1,0:T(8,128)(2,1)S(1)} collective-permute-done((bf16[2,128,128]{2,1,0:T(8,128)(2,1)S(1)}, bf16[2,128,128]{2,1,0:T(8,128)(2,1)S(1)}, u32[]{:S(2)}, u32[]{:S(2)}) %collective-permute-start.1) | collective-permute-done | bytes 65568 | tf_op jit(solution)/shard_map/ppermute | solution.py:34
  22.7 2.9 %shard_map.103 = (bf16[128,512]{1,0:T(8,128)(2,1)S(1)}, bf16[128,512]{1,0:T(8,128)(2,1)}, f32[2,128,128]{2,1,0:T(8,128)S(1)}, f32[2,128,128]{2,1,0:T(8,128)S(1)}) custom-call(bf16[128,512]{1,0:T(8,128)(2,1)S(1)} %copy-done.1, bf16[128,512]{1,0:T(8,128)(2,1)S(1)} %copy-done, bf16[2,128,128]{2,1,0:T(8,128)(2,1)S(1)} %pad_maximum_fusion.1.refs_0_, ...), custom_call_target="tpu_custom_call" | custom-call | tf_op jit(solution)/shard_map/pallas_call | solution.py:300
  25.5 0.7 copy-done.2
  26.2 1.3 collective-permute-start.2
  27.6 2.7 %collective-permute-start.7 = (f32[2,128,128]{2,1,0:T(8,128)}, f32[2,128,128]{2,1,0:T(8,128)}, u32[]{:S(2)}, u32[]{:S(2)}) collective-permute-start(f32[2,128,128]{2,1,0:T(8,128)} %copy-done.2), channel_id=1, source_target_pairs={{0,16},{16,0},{1,17},{17,1},{2,18},{18,2},{3,19},{19,3},{4,20},{20... | collective-permute-start | bytes 393224 | tf_op jit(solution)/shard_map/ppermute | solution.py:34
  30.3 4.2 %collective-permute-done.2 = bf16[128,512]{1,0:T(8,128)(2,1)S(1)} collective-permute-done((bf16[128,512]{1,0:T(8,128)(2,1)S(1)}, bf16[128,512]{1,0:T(8,128)(2,1)S(1)}, u32[]{:S(2)}, u32[]{:S(2)}) %collective-permute-start.2) | collective-permute-done | bytes 131104 | tf_op jit(solution)/shard_map/ppermute | solution.py:50
  34.5 0.6 multiply_reduce_fusion
  35.1 6.8 %shard_map.104 = (bf16[4,128,384]{2,1,0:T(8,128)(2,1)S(1)}, bf16[8,128,1024]{2,1,0:T(8,128)(2,1)S(1)}) custom-call(bf16[128,512]{1,0:T(8,128)(2,1)S(1)} %broadcast_select_fusion.1.refs_0_, bf16[32768,512]{1,0:T(8,128)(2,1)} %refs_1_.21, bf16[8,128,384]{2,1,0:T(8,128)(2,1)S(1)} %collective-permute-done.3.refs_2_.refs_4_), custom_call_target="tpu_custom_call" | custom-call | flops 127506841600 | bytes 1284505600 | tf_op jit(solution)/shard_map/pallas_call | solution.py:233
  42.0 2.4 %collective-permute-start.5 = (bf16[4,128,384]{2,1,0:T(8,128)(2,1)S(1)}, bf16[4,128,384]{2,1,0:T(8,128)(2,1)S(1)}, u32[]{:S(2)}, u32[]{:S(2)}) collective-permute-start(bf16[4,128,384]{2,1,0:T(8,128)(2,1)S(1)} %get-tuple-element.81), channel_id=1, source_target_pairs={{0,8},{4,12},{8,0},{12,4},{1,9},{5,13},{9,1},{13,5},{2,10},{6,14},... | collective-permute-start | bytes 1179656 | tf_op jit(solution)/shard_map/ppermute | solution.py:39
  44.6 8.1 %shard_map.105 = (bf16[4,128,640]{2,1,0:T(8,128)(2,1)S(1)}, bf16[8,128,768]{2,1,0:T(8,128)(2,1)S(1)}) custom-call(bf16[128,512]{1,0:T(8,128)(2,1)S(1)} %broadcast_select_fusion.1.refs_0_, bf16[32768,512]{1,0:T(8,128)(2,1)} %refs_1_.21, bf16[128,512]{1,0:T(8,128)(2,1)S(1)} %get-tuple-element.140.refs_2_.refs_0_, bf16[512,32768]{1,0:T(8,128)(2,1)} %refs_1_.23, ...), custom_call_target="tpu_custom_call" | custom-call | flops 114085068800 | bytes 1179648000 | tf_op jit(solution)/shard_map/pallas_call | solution.py:233
  53.2 1.0 collective-permute-done.5.refs_5_
  54.2 8.0 %shard_map.106 = (bf16[2,128,384]{2,1,0:T(8,128)(2,1)S(1)}, bf16[4,128,1024]{2,1,0:T(8,128)(2,1)S(1)}, bf16[8,128,640]{2,1,0:T(8,128)(2,1)S(1)}) custom-call(bf16[128,512]{1,0:T(8,128)(2,1)S(1)} %broadcast_select_fusion.1.refs_0_, bf16[32768,512]{1,0:T(8,128)(2,1)} %refs_1_.21, bf16[128,512]{1,0:T(8,128)(2,1)S(1)} %get-tuple-element.140.refs_2_.refs_0_, ...), custom_call_target="tpu_custom_call" | custom-call | flops 130862284800 | bytes 1422131200 | tf_op jit(solution)/shard_map/pallas_call | solution.py:233
  62.1 0.9 add.30
  63.1 1.9 %collective-permute-start.10 = (f32[2,128,128]{2,1,0:T(8,128)S(1)}, f32[2,128,128]{2,1,0:T(8,128)S(1)}, u32[]{:S(2)}, u32[]{:S(2)}) collective-permute-start(f32[2,128,128]{2,1,0:T(8,128)S(1)} %add.30), channel_id=1, source_target_pairs={{0,1},{1,0},{2,3},{3,2},{4,5},{5,4},{6,7},{7,6},{8,9},{9,8},{10,11... | collective-permute-start | bytes 393224 | tf_op jit(solution)/shard_map/ppermute | solution.py:39
  65.2 4.5 %collective-permute-done.8.refs_5_ = bf16[4,128,640]{2,1,0:T(8,128)(2,1)S(1)} collective-permute-done((bf16[4,128,640]{2,1,0:T(8,128)(2,1)S(1)}, bf16[4,128,640]{2,1,0:T(8,128)(2,1)S(1)}, u32[]{:S(2)}, u32[]{:S(2)}) %collective-permute-start.8) | collective-permute-done | bytes 655392 | tf_op jit(solution)/shard_map/ppermute | solution.py:39
  70.0 8.3 %shard_map.107 = (bf16[2,128,640]{2,1,0:T(8,128)(2,1)S(1)}, bf16[4,128,768]{2,1,0:T(8,128)(2,1)S(1)}, bf16[8,128,384]{2,1,0:T(8,128)(2,1)S(1)}) custom-call(bf16[128,512]{1,0:T(8,128)(2,1)S(1)} %broadcast_select_fusion.1.refs_0_, bf16[32768,512]{1,0:T(8,128)(2,1)} %refs_1_.21, bf16[128,512]{1,0:T(8,128)(2,1)S(1)} %get-tuple-element.140.refs_2_.refs_0_, ...), custom_call_target="tpu_custom_call" | custom-call | flops 97307852800 | bytes 1094451200 | tf_op jit(solution)/shard_map/pallas_call | solution.py:233
  78.4 1.9 %collective-permute-start.17 = (bf16[2,128,640]{2,1,0:T(8,128)(2,1)S(1)}, bf16[2,128,640]{2,1,0:T(8,128)(2,1)S(1)}, u32[]{:S(2)}, u32[]{:S(2)}) collective-permute-start(bf16[2,128,640]{2,1,0:T(8,128)(2,1)S(1)} %get-tuple-element.96), channel_id=1, source_target_pairs={{0,1},{1,0},{2,3},{3,2},{4,5},{5,4},{6,7},{7,6},{8,9},{9,8},{10,11... | collective-permute-start | bytes 983048 | tf_op jit(solution)/shard_map/ppermute | solution.py:39
  80.3 0.7 add.32
  81.0 1.5 collective-permute-start.16
  83.1 12.7 %collective-permute-done.14.refs_8_.refs_9_.refs_5_ = bf16[4,128,1024]{2,1,0:T(8,128)(2,1)S(1)} collective-permute-done((bf16[4,128,1024]{2,1,0:T(8,128)(2,1)S(1)}, bf16[4,128,1024]{2,1,0:T(8,128)(2,1)S(1)}, u32[]{:S(2)}, u32[]{:S(2)}) %collective-permute-start.14) | collective-permute-done | bytes 1048608 | tf_op jit(solution)/shard_map/ppermute | solution.py:39
  95.8 2.6 %collective-permute-start.11 = (bf16[2,128,128]{2,1,0:T(8,128)(2,1)S(1)}, bf16[2,128,128]{2,1,0:T(8,128)(2,1)S(1)}, u32[]{:S(2)}, u32[]{:S(2)}) collective-permute-start(bf16[2,128,128]{2,1,0:T(8,128)(2,1)S(1)} %add.31), channel_id=1, source_target_pairs={{0,2},{1,3},{2,0},{3,1},{4,6},{5,7},{6,4},{7,5},{8,10},{9,11},{10,... | collective-permute-start | bytes 196616 | tf_op jit(solution)/shard_map/ppermute | solution.py:39
  98.4 7.8 %shard_map.108 = (bf16[1,128,384]{2,1,0:T(8,128)(2,1)S(1)}, bf16[2,128,1024]{2,1,0:T(8,128)(2,1)S(1)}, bf16[4,128,640]{2,1,0:T(8,128)(2,1)S(1)}, bf16[8,128,256]{2,1,0:T(8,128)(2,1)S(1)}) custom-call(bf16[128,512]{1,0:T(8,128)(2,1)S(1)} %broadcast_select_fusion.1.refs_0_, bf16[32768,512]{1,0:T(8,128)(2,1)} %refs_1_.21, ...), custom_call_target="tpu_custom_call" | custom-call | flops 92274688000 | bytes 1101004800 | tf_op jit(solution)/shard_map/pallas_call | solution.py:233
  106.6 1.6 collective-permute-start.20
  108.2 0.7 broadcast_select_fusion.2
  109.3 1.8 collective-permute-done.18.refs_8_.refs_9_.refs_3_
  111.4 5.5 %shard_map.109 = (bf16[1,128,640]{2,1,0:T(8,128)(2,1)S(1)}, bf16[2,128,768]{2,1,0:T(8,128)(2,1)S(1)}, bf16[4,128,384]{2,1,0:T(8,128)(2,1)S(1)}) custom-call(bf16[128,512]{1,0:T(8,128)(2,1)S(1)} %broadcast_select_fusion.1.refs_0_, bf16[32768,512]{1,0:T(8,128)(2,1)} %refs_1_.21, bf16[128,512]{1,0:T(8,128)(2,1)S(1)} %get-tuple-element.140.refs_2_.refs_0_, ...), custom_call_target="tpu_custom_call" | custom-call | flops 48653926400 | bytes 642252800 | tf_op jit(solution)/shard_map/pallas_call | solution.py:233
  116.9 2.9 %collective-permute-start.26 = (bf16[1,128,640]{2,1,0:T(8,128)(2,1)S(1)}, bf16[1,128,640]{2,1,0:T(8,128)(2,1)S(1)}, u32[]{:S(2)}, u32[]{:S(2)}) collective-permute-start(bf16[1,128,640]{2,1,0:T(8,128)(2,1)S(1)} %get-tuple-element.112), channel_id=1, source_target_pairs={{0,2},{1,3},{2,0},{3,1},{4,6},{5,7},{6,4},{7,5},{8,10},{9,11},{10,... | collective-permute-start | bytes 491528 | tf_op jit(solution)/shard_map/ppermute | solution.py:39
  119.8 1.6 collective-permute-start.27
  121.4 6.8 %collective-permute-done.22.refs_10_.refs_6_ = bf16[2,128,1024]{2,1,0:T(8,128)(2,1)S(1)} collective-permute-done((bf16[2,128,1024]{2,1,0:T(8,128)(2,1)S(1)}, bf16[2,128,1024]{2,1,0:T(8,128)(2,1)S(1)}, u32[]{:S(2)}, u32[]{:S(2)}) %collective-permute-start.22) | collective-permute-done | bytes 524320 | tf_op jit(solution)/shard_map/ppermute | solution.py:39
  128.2 5.5 %shard_map.110 = (f32[1,128,384]{2,1,0:T(8,128)S(1)}, bf16[1,128,1024]{2,1,0:T(8,128)(2,1)S(1)}, bf16[2,128,640]{2,1,0:T(8,128)(2,1)S(1)}, bf16[4,128,256]{2,1,0:T(8,128)(2,1)S(1)}) custom-call(bf16[128,512]{1,0:T(8,128)(2,1)S(1)} %broadcast_select_fusion.1.refs_0_, bf16[32768,512]{1,0:T(8,128)(2,1)} %refs_1_.21, ...), custom_call_target="tpu_custom_call" | custom-call | flops 48653926400 | bytes 684851200 | tf_op jit(solution)/shard_map/pallas_call | solution.py:233
  133.7 2.9 %collective-permute-start.29 = (bf16[1,128,1024]{2,1,0:T(8,128)(2,1)S(1)}, bf16[1,128,1024]{2,1,0:T(8,128)(2,1)S(1)}, u32[]{:S(2)}, u32[]{:S(2)}) collective-permute-start(bf16[1,128,1024]{2,1,0:T(8,128)(2,1)S(1)} %get-tuple-element.130), channel_id=1, source_target_pairs={{0,2},{1,3},{2,0},{3,1},{4,6},{5,7},{6,4},{7,5},{8,10},{9,11},{10,... | collective-permute-start | bytes 786440 | tf_op jit(solution)/shard_map/ppermute | solution.py:39
  137.0 1.7 collective-permute-start.31
  138.7 4.0 %shard_map.111 = (f32[1,128,640]{2,1,0:T(8,128)S(1)}, bf16[1,128,768]{2,1,0:T(8,128)(2,1)S(1)}, bf16[2,128,384]{2,1,0:T(8,128)(2,1)S(1)}) custom-call(bf16[128,512]{1,0:T(8,128)(2,1)S(1)} %broadcast_select_fusion.1.refs_0_, bf16[32768,512]{1,0:T(8,128)(2,1)} %refs_1_.21, bf16[128,512]{1,0:T(8,128)(2,1)S(1)} %get-tuple-element.140.refs_2_.refs_0_, ...), custom_call_target="tpu_custom_call" | custom-call | flops 28521267200 | bytes 442368000 | tf_op jit(solution)/shard_map/pallas_call | solution.py:233
  142.8 1.8 collective-permute-start.32
  144.9 5.3 %collective-permute-done.29.refs_7_ = bf16[1,128,1024]{2,1,0:T(8,128)(2,1)S(1)} collective-permute-done((bf16[1,128,1024]{2,1,0:T(8,128)(2,1)S(1)}, bf16[1,128,1024]{2,1,0:T(8,128)(2,1)S(1)}, u32[]{:S(2)}, u32[]{:S(2)}) %collective-permute-start.29) | collective-permute-done | bytes 262176 | tf_op jit(solution)/shard_map/ppermute | solution.py:39
  150.2 5.6 %collective-permute-done.30.refs_10_.refs_8_ = bf16[2,128,640]{2,1,0:T(8,128)(2,1)S(1)} collective-permute-done((bf16[2,128,640]{2,1,0:T(8,128)(2,1)S(1)}, bf16[2,128,640]{2,1,0:T(8,128)(2,1)S(1)}, u32[]{:S(2)}, u32[]{:S(2)}) %collective-permute-start.30) | collective-permute-done | bytes 327712 | tf_op jit(solution)/shard_map/ppermute | solution.py:39
  155.8 3.0 %shard_map.112 = (f32[1,128,1024]{2,1,0:T(8,128)S(1)}, bf16[1,128,640]{2,1,0:T(8,128)(2,1)S(1)}, bf16[2,128,256]{2,1,0:T(8,128)(2,1)S(1)}) custom-call(bf16[128,512]{1,0:T(8,128)(2,1)S(1)} %broadcast_select_fusion.1.refs_0_, bf16[32768,512]{1,0:T(8,128)(2,1)} %refs_1_.21, bf16[128,512]{1,0:T(8,128)(2,1)S(1)} %get-tuple-element.140.refs_2_.refs_0_, ...), custom_call_target="tpu_custom_call" | custom-call | flops 28521267200 | bytes 458752000 | tf_op jit(solution)/shard_map/pallas_call | solution.py:233
  159.3 2.9 %collective-permute-start.35 = (bf16[2,128,256]{2,1,0:T(8,128)(2,1)S(1)}, bf16[2,128,256]{2,1,0:T(8,128)(2,1)S(1)}, u32[]{:S(2)}, u32[]{:S(2)}) collective-permute-start(bf16[2,128,256]{2,1,0:T(8,128)(2,1)S(1)} %get-tuple-element.138), channel_id=1, source_target_pairs={{0,1},{1,0},{2,3},{3,2},{4,5},{5,4},{6,7},{7,6},{8,9},{9,8},{10,11... | collective-permute-start | bytes 393224 | tf_op jit(solution)/shard_map/ppermute | solution.py:39
  162.2 4.6 %collective-permute-done.35.refs_15_.refs_8_ = bf16[2,128,256]{2,1,0:T(8,128)(2,1)S(1)} collective-permute-done((bf16[2,128,256]{2,1,0:T(8,128)(2,1)S(1)}, bf16[2,128,256]{2,1,0:T(8,128)(2,1)S(1)}, u32[]{:S(2)}, u32[]{:S(2)}) %collective-permute-start.35) | collective-permute-done | bytes 131104 | tf_op jit(solution)/shard_map/ppermute | solution.py:39
  166.9 4.6 %shard_map.113 = (f32[1,1,768]{2,1,0:T(1,128)S(1)}, f32[1,1,640]{2,1,0:T(1,128)S(1)}, bf16[1,128,384]{2,1,0:T(8,128)(2,1)S(1)}, bf16[1,128,256]{2,1,0:T(8,128)(2,1)S(1)}) custom-call(bf16[128,512]{1,0:T(8,128)(2,1)S(1)} %get-tuple-element.140.refs_2_.refs_0_, bf16[512,32768]{1,0:T(8,128)(2,1)} %refs_1_.23, ...), custom_call_target="tpu_custom_call" | custom-call | flops 26843545600 | bytes 455475200 | tf_op jit(solution)/shard_map/pallas_call | solution.py:233
  171.6 2.9 %collective-permute-start.37 = (bf16[1,128,256]{2,1,0:T(8,128)(2,1)S(1)}, bf16[1,128,256]{2,1,0:T(8,128)(2,1)S(1)}, u32[]{:S(2)}, u32[]{:S(2)}) collective-permute-start(bf16[1,128,256]{2,1,0:T(8,128)(2,1)S(1)} %get-tuple-element.142), channel_id=1, source_target_pairs={{0,2},{1,3},{2,0},{3,1},{4,6},{5,7},{6,4},{7,5},{8,10},{9,11},{10,... | collective-permute-start | bytes 196616 | tf_op jit(solution)/shard_map/ppermute | solution.py:39
  174.5 0.7 fusion.3
  175.2 4.1 %collective-permute-done.37.refs_9_ = bf16[1,128,256]{2,1,0:T(8,128)(2,1)S(1)} collective-permute-done((bf16[1,128,256]{2,1,0:T(8,128)(2,1)S(1)}, bf16[1,128,256]{2,1,0:T(8,128)(2,1)S(1)}, u32[]{:S(2)}, u32[]{:S(2)}) %collective-permute-start.37) | collective-permute-done | bytes 65568 | tf_op jit(solution)/shard_map/ppermute | solution.py:39
  179.3 1.9 %shard_map.114 = (f32[1,1,384]{2,1,0:T(1,128)S(1)}, f32[1,1,256]{2,1,0:T(1,128)S(1)}) custom-call(bf16[128,512]{1,0:T(8,128)(2,1)S(1)} %get-tuple-element.140.refs_2_.refs_0_, bf16[512,32768]{1,0:T(8,128)(2,1)} %refs_1_.23, bf16[8,128,384]{2,1,0:T(8,128)(2,1)S(1)} %collective-permute-done.19.refs_9_.refs_11_.refs_10_.refs_2_, ...), custom_call_target="tpu_custom_call" | custom-call | flops 8388608000 | bytes 147456000 | tf_op jit(solution)/shard_map/pallas_call | solution.py:233
  (75 shorter events, 5.2 us)
Async XLA Ops:
  0.6 8.0 %collective-permute-start = (bf16[128,512]{1,0:T(8,128)(2,1)}, bf16[128,512]{1,0:T(8,128)(2,1)S(1)}, u32[]{:S(2)}, u32[]{:S(2)}) collective-permute-start(bf16[128,512]{1,0:T(8,128)(2,1)} %out_grad.1), channel_id=1, source_target_pairs={{16,0},{17,1},{18,2},{19,3},{20,4},{21,5},{22,6},{23,7},{24,8},{25... | collective-permute-start | bytes 393224 | tf_op jit(solution)/shard_map/ppermute | solution.py:50
  8.6 9.5 %copy-start.5 = (bf16[128,256]{1,0:T(8,128)(2,1)S(1)}, bf16[128,256]{1,0:T(8,128)(2,1)}, u32[]{:S(2)}) copy-start(bf16[128,256]{1,0:T(8,128)(2,1)} %param.9) | copy-start | bytes 196612
  8.6 9.5 %copy-start.6 = (bf16[128,256]{1,0:T(8,128)(2,1)S(1)}, bf16[128,256]{1,0:T(8,128)(2,1)}, u32[]{:S(2)}) copy-start(bf16[128,256]{1,0:T(8,128)(2,1)} %param.8) | copy-start | bytes 196612
  8.6 14.0 %copy-start = (bf16[128,512]{1,0:T(8,128)(2,1)S(1)}, bf16[128,512]{1,0:T(8,128)(2,1)}, u32[]{:S(2)}) copy-start(bf16[128,512]{1,0:T(8,128)(2,1)} %out_grad.1) | copy-start | bytes 393220
  8.7 14.0 %copy-start.1 = (bf16[128,512]{1,0:T(8,128)(2,1)S(1)}, bf16[128,512]{1,0:T(8,128)(2,1)}, u32[]{:S(2)}) copy-start(bf16[128,512]{1,0:T(8,128)(2,1)} %queries) | copy-start | bytes 393220
  18.0 17.1 %collective-permute-start.3 = (bf16[8,128,384]{2,1,0:T(8,128)(2,1)S(1)}, bf16[8,128,384]{2,1,0:T(8,128)(2,1)S(1)}, u32[]{:S(2)}, u32[]{:S(2)}) collective-permute-start(bf16[8,128,384]{2,1,0:T(8,128)(2,1)S(1)} %get-tuple-element.75), channel_id=1, source_target_pairs={{0,4},{4,0},{8,12},{12,8},{1,5},{5,1},{9,13},{13,9},{2,6},{6,2},{1... | collective-permute-start | bytes 2359304 | tf_op jit(solution)/shard_map/ppermute | solution.py:39
  18.2 4.5 %collective-permute-start.1 = (bf16[2,128,128]{2,1,0:T(8,128)(2,1)S(1)}, bf16[2,128,128]{2,1,0:T(8,128)(2,1)S(1)}, u32[]{:S(2)}, u32[]{:S(2)}) collective-permute-start(bf16[2,128,128]{2,1,0:T(8,128)(2,1)S(1)} %pad_maximum_fusion.1.refs_0_), channel_id=1, source_target_pairs={{0,16},{16,0},{1,17},{17,1},{2,18},{18,2},{3,19},{19,3},{4,20},{20... | collective-permute-start | bytes 196616 | tf_op jit(solution)/shard_map/ppermute | solution.py:34
  25.5 0.7 copy-start.2
  26.2 8.3 %collective-permute-start.2 = (bf16[128,512]{1,0:T(8,128)(2,1)S(1)}, bf16[128,512]{1,0:T(8,128)(2,1)S(1)}, u32[]{:S(2)}, u32[]{:S(2)}) collective-permute-start(bf16[128,512]{1,0:T(8,128)(2,1)S(1)} %get-tuple-element.80), channel_id=1, source_target_pairs={{16,0},{17,1},{18,2},{19,3},{20,4},{21,5},{22,6},{23,7},{24,8},{25... | collective-permute-start | bytes 393224 | tf_op jit(solution)/shard_map/ppermute | solution.py:50
  27.5 17.1 %collective-permute-start.4 = (bf16[8,128,640]{2,1,0:T(8,128)(2,1)S(1)}, bf16[8,128,640]{2,1,0:T(8,128)(2,1)S(1)}, u32[]{:S(2)}, u32[]{:S(2)}) collective-permute-start(bf16[8,128,640]{2,1,0:T(8,128)(2,1)S(1)} %get-tuple-element.84), channel_id=1, source_target_pairs={{0,4},{4,0},{8,12},{12,8},{1,5},{5,1},{9,13},{13,9},{2,6},{6,2},{1... | collective-permute-start | bytes 3932168 | tf_op jit(solution)/shard_map/ppermute | solution.py:39
  27.6 34.6 %collective-permute-start.7 = (f32[2,128,128]{2,1,0:T(8,128)}, f32[2,128,128]{2,1,0:T(8,128)}, u32[]{:S(2)}, u32[]{:S(2)}) collective-permute-start(f32[2,128,128]{2,1,0:T(8,128)} %copy-done.2), channel_id=1, source_target_pairs={{0,16},{16,0},{1,17},{17,1},{2,18},{18,2},{3,19},{19,3},{4,20},{20... | collective-permute-start | bytes 393224 | tf_op jit(solution)/shard_map/ppermute | solution.py:34
  35.1 43.2 %collective-permute-start.12 = (f32[128]{0:T(128)}, f32[128]{0:T(128)}, u32[]{:S(2)}, u32[]{:S(2)}) collective-permute-start(f32[128]{0:T(128)} %get-tuple-element.148), channel_id=1, source_target_pairs={{0,4},{4,0},{8,12},{12,8},{1,5},{5,1},{9,13},{13,9},{2,6},{6,2},{1... | collective-permute-start | bytes 1544 | tf_op jit(solution)/shard_map/ppermute | solution.py:39
  42.0 12.2 %collective-permute-start.5 = (bf16[4,128,384]{2,1,0:T(8,128)(2,1)S(1)}, bf16[4,128,384]{2,1,0:T(8,128)(2,1)S(1)}, u32[]{:S(2)}, u32[]{:S(2)}) collective-permute-start(bf16[4,128,384]{2,1,0:T(8,128)(2,1)S(1)} %get-tuple-element.81), channel_id=1, source_target_pairs={{0,8},{4,12},{8,0},{12,4},{1,9},{5,13},{9,1},{13,5},{2,10},{6,14},... | collective-permute-start | bytes 1179656 | tf_op jit(solution)/shard_map/ppermute | solution.py:39
  44.4 9.8 %collective-permute-start.6 = (bf16[8,128,1024]{2,1,0:T(8,128)(2,1)S(1)}, bf16[8,128,1024]{2,1,0:T(8,128)(2,1)S(1)}, u32[]{:S(2)}, u32[]{:S(2)}) collective-permute-start(bf16[8,128,1024]{2,1,0:T(8,128)(2,1)S(1)} %get-tuple-element.88), channel_id=1, source_target_pairs={{0,4},{4,0},{8,12},{12,8},{1,5},{5,1},{9,13},{13,9},{2,6},{6,2},{1... | collective-permute-start | bytes 6291464 | tf_op jit(solution)/shard_map/ppermute | solution.py:39
  52.7 17.0 %collective-permute-start.8 = (bf16[4,128,640]{2,1,0:T(8,128)(2,1)S(1)}, bf16[4,128,640]{2,1,0:T(8,128)(2,1)S(1)}, u32[]{:S(2)}, u32[]{:S(2)}) collective-permute-start(bf16[4,128,640]{2,1,0:T(8,128)(2,1)S(1)} %get-tuple-element.85), channel_id=1, source_target_pairs={{0,8},{4,12},{8,0},{12,4},{1,9},{5,13},{9,1},{13,5},{2,10},{6,14},... | collective-permute-start | bytes 1966088 | tf_op jit(solution)/shard_map/ppermute | solution.py:39
  54.1 15.9 %collective-permute-start.9 = (bf16[8,128,768]{2,1,0:T(8,128)(2,1)S(1)}, bf16[8,128,768]{2,1,0:T(8,128)(2,1)S(1)}, u32[]{:S(2)}, u32[]{:S(2)}) collective-permute-start(bf16[8,128,768]{2,1,0:T(8,128)(2,1)S(1)} %get-tuple-element.95), channel_id=1, source_target_pairs={{0,4},{4,0},{8,12},{12,8},{1,5},{5,1},{9,13},{13,9},{2,6},{6,2},{1... | collective-permute-start | bytes 4718600 | tf_op jit(solution)/shard_map/ppermute | solution.py:39
  63.1 17.9 %collective-permute-start.10 = (f32[2,128,128]{2,1,0:T(8,128)S(1)}, f32[2,128,128]{2,1,0:T(8,128)S(1)}, u32[]{:S(2)}, u32[]{:S(2)}) collective-permute-start(f32[2,128,128]{2,1,0:T(8,128)S(1)} %add.30), channel_id=1, source_target_pairs={{0,1},{1,0},{2,3},{3,2},{4,5},{5,4},{6,7},{7,6},{8,9},{9,8},{10,11... | collective-permute-start | bytes 393224 | tf_op jit(solution)/shard_map/ppermute | solution.py:39
  64.9 17.5 %collective-permute-start.13 = (bf16[2,128,384]{2,1,0:T(8,128)(2,1)S(1)}, bf16[2,128,384]{2,1,0:T(8,128)(2,1)S(1)}, u32[]{:S(2)}, u32[]{:S(2)}) collective-permute-start(bf16[2,128,384]{2,1,0:T(8,128)(2,1)S(1)} %get-tuple-element.89), channel_id=1, source_target_pairs={{0,1},{1,0},{2,3},{3,2},{4,5},{5,4},{6,7},{7,6},{8,9},{9,8},{10,11... | collective-permute-start | bytes 589832 | tf_op jit(solution)/shard_map/ppermute | solution.py:39
  69.7 26.1 %collective-permute-start.14 = (bf16[4,128,1024]{2,1,0:T(8,128)(2,1)S(1)}, bf16[4,128,1024]{2,1,0:T(8,128)(2,1)S(1)}, u32[]{:S(2)}, u32[]{:S(2)}) collective-permute-start(bf16[4,128,1024]{2,1,0:T(8,128)(2,1)S(1)} %get-tuple-element.102), channel_id=1, source_target_pairs={{0,8},{4,12},{8,0},{12,4},{1,9},{5,13},{9,1},{13,5},{2,10},{6,14},... | collective-permute-start | bytes 3145736 | tf_op jit(solution)/shard_map/ppermute | solution.py:39
  70.0 25.8 %collective-permute-start.15 = (bf16[8,128,640]{2,1,0:T(8,128)(2,1)S(1)}, bf16[8,128,640]{2,1,0:T(8,128)(2,1)S(1)}, u32[]{:S(2)}, u32[]{:S(2)}) collective-permute-start(bf16[8,128,640]{2,1,0:T(8,128)(2,1)S(1)} %get-tuple-element.103), channel_id=1, source_target_pairs={{0,4},{4,0},{8,12},{12,8},{1,5},{5,1},{9,13},{13,9},{2,6},{6,2},{1... | collective-permute-start | bytes 3932168 | tf_op jit(solution)/shard_map/ppermute | solution.py:39
  78.4 30.5 %collective-permute-start.17 = (bf16[2,128,640]{2,1,0:T(8,128)(2,1)S(1)}, bf16[2,128,640]{2,1,0:T(8,128)(2,1)S(1)}, u32[]{:S(2)}, u32[]{:S(2)}) collective-permute-start(bf16[2,128,640]{2,1,0:T(8,128)(2,1)S(1)} %get-tuple-element.96), channel_id=1, source_target_pairs={{0,1},{1,0},{2,3},{3,2},{4,5},{5,4},{6,7},{7,6},{8,9},{9,8},{10,11... | collective-permute-start | bytes 983048 | tf_op jit(solution)/shard_map/ppermute | solution.py:39
  81.0 25.3 %collective-permute-start.16 = (f32[128]{0:T(128)S(1)}, f32[128]{0:T(128)S(1)}, u32[]{:S(2)}, u32[]{:S(2)}) collective-permute-start(f32[128]{0:T(128)S(1)} %add.32), channel_id=1, source_target_pairs={{0,8},{4,12},{8,0},{12,4},{1,9},{5,13},{9,1},{13,5},{2,10},{6,14},... | collective-permute-start | bytes 1544 | tf_op jit(solution)/shard_map/ppermute | solution.py:39
  82.5 28.6 %collective-permute-start.18 = (bf16[4,128,768]{2,1,0:T(8,128)(2,1)S(1)}, bf16[4,128,768]{2,1,0:T(8,128)(2,1)S(1)}, u32[]{:S(2)}, u32[]{:S(2)}) collective-permute-start(bf16[4,128,768]{2,1,0:T(8,128)(2,1)S(1)} %get-tuple-element.110), channel_id=1, source_target_pairs={{0,8},{4,12},{8,0},{12,4},{1,9},{5,13},{9,1},{13,5},{2,10},{6,14},... | collective-permute-start | bytes 2359304 | tf_op jit(solution)/shard_map/ppermute | solution.py:39
  95.8 15.6 %collective-permute-start.19 = (bf16[8,128,384]{2,1,0:T(8,128)(2,1)S(1)}, bf16[8,128,384]{2,1,0:T(8,128)(2,1)S(1)}, u32[]{:S(2)}, u32[]{:S(2)}) collective-permute-start(bf16[8,128,384]{2,1,0:T(8,128)(2,1)S(1)} %get-tuple-element.111), channel_id=1, source_target_pairs={{0,4},{4,0},{8,12},{12,8},{1,5},{5,1},{9,13},{13,9},{2,6},{6,2},{1... | collective-permute-start | bytes 2359304 | tf_op jit(solution)/shard_map/ppermute | solution.py:39
  95.8 10.8 %collective-permute-start.11 = (bf16[2,128,128]{2,1,0:T(8,128)(2,1)S(1)}, bf16[2,128,128]{2,1,0:T(8,128)(2,1)S(1)}, u32[]{:S(2)}, u32[]{:S(2)}) collective-permute-start(bf16[2,128,128]{2,1,0:T(8,128)(2,1)S(1)} %add.31), channel_id=1, source_target_pairs={{0,2},{1,3},{2,0},{3,1},{4,6},{5,7},{6,4},{7,5},{8,10},{9,11},{10,... | collective-permute-start | bytes 196616 | tf_op jit(solution)/shard_map/ppermute | solution.py:39
  106.2 13.6 %collective-permute-start.21 = (bf16[1,128,384]{2,1,0:T(8,128)(2,1)S(1)}, bf16[1,128,384]{2,1,0:T(8,128)(2,1)S(1)}, u32[]{:S(2)}, u32[]{:S(2)}) collective-permute-start(bf16[1,128,384]{2,1,0:T(8,128)(2,1)S(1)} %get-tuple-element.104), channel_id=1, source_target_pairs={{0,2},{1,3},{2,0},{3,1},{4,6},{5,7},{6,4},{7,5},{8,10},{9,11},{10,... | collective-permute-start | bytes 294920 | tf_op jit(solution)/shard_map/ppermute | solution.py:39
  106.6 10.3 %collective-permute-start.20 = (f32[128]{0:T(128)S(1)}, f32[128]{0:T(128)S(1)}, u32[]{:S(2)}, u32[]{:S(2)}) collective-permute-start(f32[128]{0:T(128)S(1)} %add.33), channel_id=1, source_target_pairs={{0,1},{1,0},{2,3},{3,2},{4,5},{5,4},{6,7},{7,6},{8,9},{9,8},{10,11... | collective-permute-start | bytes 1544 | tf_op jit(solution)/shard_map/ppermute | solution.py:39
  108.9 19.3 %collective-permute-start.22 = (bf16[2,128,1024]{2,1,0:T(8,128)(2,1)S(1)}, bf16[2,128,1024]{2,1,0:T(8,128)(2,1)S(1)}, u32[]{:S(2)}, u32[]{:S(2)}) collective-permute-start(bf16[2,128,1024]{2,1,0:T(8,128)(2,1)S(1)} %get-tuple-element.117), channel_id=1, source_target_pairs={{0,1},{1,0},{2,3},{3,2},{4,5},{5,4},{6,7},{7,6},{8,9},{9,8},{10,11... | collective-permute-start | bytes 1572872 | tf_op jit(solution)/shard_map/ppermute | solution.py:39
  111.1 17.1 %collective-permute-start.23 = (bf16[4,128,640]{2,1,0:T(8,128)(2,1)S(1)}, bf16[4,128,640]{2,1,0:T(8,128)(2,1)S(1)}, u32[]{:S(2)}, u32[]{:S(2)}) collective-permute-start(bf16[4,128,640]{2,1,0:T(8,128)(2,1)S(1)} %get-tuple-element.118), channel_id=1, source_target_pairs={{0,8},{4,12},{8,0},{12,4},{1,9},{5,13},{9,1},{13,5},{2,10},{6,14},... | collective-permute-start | bytes 1966088 | tf_op jit(solution)/shard_map/ppermute | solution.py:39
  111.4 16.8 %collective-permute-start.24 = (bf16[8,128,256]{2,1,0:T(8,128)(2,1)S(1)}, bf16[8,128,256]{2,1,0:T(8,128)(2,1)S(1)}, u32[]{:S(2)}, u32[]{:S(2)}) collective-permute-start(bf16[8,128,256]{2,1,0:T(8,128)(2,1)S(1)} %get-tuple-element.119), channel_id=1, source_target_pairs={{0,4},{4,0},{8,12},{12,8},{1,5},{5,1},{9,13},{13,9},{2,6},{6,2},{1... | collective-permute-start | bytes 1572872 | tf_op jit(solution)/shard_map/ppermute | solution.py:39
  116.9 20.0 %collective-permute-start.26 = (bf16[1,128,640]{2,1,0:T(8,128)(2,1)S(1)}, bf16[1,128,640]{2,1,0:T(8,128)(2,1)S(1)}, u32[]{:S(2)}, u32[]{:S(2)}) collective-permute-start(bf16[1,128,640]{2,1,0:T(8,128)(2,1)S(1)} %get-tuple-element.112), channel_id=1, source_target_pairs={{0,2},{1,3},{2,0},{3,1},{4,6},{5,7},{6,4},{7,5},{8,10},{9,11},{10,... | collective-permute-start | bytes 491528 | tf_op jit(solution)/shard_map/ppermute | solution.py:39
  119.8 18.9 %collective-permute-start.27 = (bf16[2,128,768]{2,1,0:T(8,128)(2,1)S(1)}, bf16[2,128,768]{2,1,0:T(8,128)(2,1)S(1)}, u32[]{:S(2)}, u32[]{:S(2)}) collective-permute-start(bf16[2,128,768]{2,1,0:T(8,128)(2,1)S(1)} %get-tuple-element.125), channel_id=1, source_target_pairs={{0,1},{1,0},{2,3},{3,2},{4,5},{5,4},{6,7},{7,6},{8,9},{9,8},{10,11... | collective-permute-start | bytes 1179656 | tf_op jit(solution)/shard_map/ppermute | solution.py:39
  128.2 10.5 %collective-permute-start.28 = (bf16[4,128,384]{2,1,0:T(8,128)(2,1)S(1)}, bf16[4,128,384]{2,1,0:T(8,128)(2,1)S(1)}, u32[]{:S(2)}, u32[]{:S(2)}) collective-permute-start(bf16[4,128,384]{2,1,0:T(8,128)(2,1)S(1)} %get-tuple-element.126), channel_id=1, source_target_pairs={{0,8},{4,12},{8,0},{12,4},{1,9},{5,13},{9,1},{13,5},{2,10},{6,14},... | collective-permute-start | bytes 1179656 | tf_op jit(solution)/shard_map/ppermute | solution.py:39
  128.2 5.5 %collective-permute-start.25 = (f32[128]{0:T(128)S(1)}, f32[128]{0:T(128)S(1)}, u32[]{:S(2)}, u32[]{:S(2)}) collective-permute-start(f32[128]{0:T(128)S(1)} %add.34), channel_id=1, source_target_pairs={{0,2},{1,3},{2,0},{3,1},{4,6},{5,7},{6,4},{7,5},{8,10},{9,11},{10,... | collective-permute-start | bytes 1544 | tf_op jit(solution)/shard_map/ppermute | solution.py:39
  133.7 16.5 %collective-permute-start.29 = (bf16[1,128,1024]{2,1,0:T(8,128)(2,1)S(1)}, bf16[1,128,1024]{2,1,0:T(8,128)(2,1)S(1)}, u32[]{:S(2)}, u32[]{:S(2)}) collective-permute-start(bf16[1,128,1024]{2,1,0:T(8,128)(2,1)S(1)} %get-tuple-element.130), channel_id=1, source_target_pairs={{0,2},{1,3},{2,0},{3,1},{4,6},{5,7},{6,4},{7,5},{8,10},{9,11},{10,... | collective-permute-start | bytes 786440 | tf_op jit(solution)/shard_map/ppermute | solution.py:39
  136.7 19.1 %collective-permute-start.30 = (bf16[2,128,640]{2,1,0:T(8,128)(2,1)S(1)}, bf16[2,128,640]{2,1,0:T(8,128)(2,1)S(1)}, u32[]{:S(2)}, u32[]{:S(2)}) collective-permute-start(bf16[2,128,640]{2,1,0:T(8,128)(2,1)S(1)} %get-tuple-element.131), channel_id=1, source_target_pairs={{0,1},{1,0},{2,3},{3,2},{4,5},{5,4},{6,7},{7,6},{8,9},{9,8},{10,11... | collective-permute-start | bytes 983048 | tf_op jit(solution)/shard_map/ppermute | solution.py:39
  137.0 13.3 %collective-permute-start.31 = (bf16[4,128,256]{2,1,0:T(8,128)(2,1)S(1)}, bf16[4,128,256]{2,1,0:T(8,128)(2,1)S(1)}, u32[]{:S(2)}, u32[]{:S(2)}) collective-permute-start(bf16[4,128,256]{2,1,0:T(8,128)(2,1)S(1)} %get-tuple-element.132), channel_id=1, source_target_pairs={{0,8},{4,12},{8,0},{12,4},{1,9},{5,13},{9,1},{13,5},{2,10},{6,14},... | collective-permute-start | bytes 786440 | tf_op jit(solution)/shard_map/ppermute | solution.py:39
  142.8 19.4 %collective-permute-start.32 = (bf16[1,128,768]{2,1,0:T(8,128)(2,1)S(1)}, bf16[1,128,768]{2,1,0:T(8,128)(2,1)S(1)}, u32[]{:S(2)}, u32[]{:S(2)}) collective-permute-start(bf16[1,128,768]{2,1,0:T(8,128)(2,1)S(1)} %get-tuple-element.135), channel_id=1, source_target_pairs={{0,2},{1,3},{2,0},{3,1},{4,6},{5,7},{6,4},{7,5},{8,10},{9,11},{10,... | collective-permute-start | bytes 589832 | tf_op jit(solution)/shard_map/ppermute | solution.py:39
  144.5 17.6 %copy-start.7 = (f32[2048]{0:T(1024)S(1)}, f32[2048]{0:T(1024)}, u32[]{:S(2)}) copy-start(f32[2048]{0:T(1024)} %param.12) | copy-start | bytes 24580
  144.5 17.7 %collective-permute-start.34 = (bf16[2,128,384]{2,1,0:T(8,128)(2,1)S(1)}, bf16[2,128,384]{2,1,0:T(8,128)(2,1)S(1)}, u32[]{:S(2)}, u32[]{:S(2)}) collective-permute-start(bf16[2,128,384]{2,1,0:T(8,128)(2,1)S(1)} %get-tuple-element.137), channel_id=1, source_target_pairs={{0,1},{1,0},{2,3},{3,2},{4,5},{5,4},{6,7},{7,6},{8,9},{9,8},{10,11... | collective-permute-start | bytes 589832 | tf_op jit(solution)/shard_map/ppermute | solution.py:39
  158.8 8.0 %collective-permute-start.33 = (bf16[1,128,640]{2,1,0:T(8,128)(2,1)S(1)}, bf16[1,128,640]{2,1,0:T(8,128)(2,1)S(1)}, u32[]{:S(2)}, u32[]{:S(2)}) collective-permute-start(bf16[1,128,640]{2,1,0:T(8,128)(2,1)S(1)} %get-tuple-element.136), channel_id=1, source_target_pairs={{0,2},{1,3},{2,0},{3,1},{4,6},{5,7},{6,4},{7,5},{8,10},{9,11},{10,... | collective-permute-start | bytes 491528 | tf_op jit(solution)/shard_map/ppermute | solution.py:39
  159.3 7.5 %collective-permute-start.35 = (bf16[2,128,256]{2,1,0:T(8,128)(2,1)S(1)}, bf16[2,128,256]{2,1,0:T(8,128)(2,1)S(1)}, u32[]{:S(2)}, u32[]{:S(2)}) collective-permute-start(bf16[2,128,256]{2,1,0:T(8,128)(2,1)S(1)} %get-tuple-element.138), channel_id=1, source_target_pairs={{0,1},{1,0},{2,3},{3,2},{4,5},{5,4},{6,7},{7,6},{8,9},{9,8},{10,11... | collective-permute-start | bytes 393224 | tf_op jit(solution)/shard_map/ppermute | solution.py:39
  166.9 7.6 %copy-start.3 = (bf16[2,128,128]{2,1,0:T(8,128)(2,1)S(1)}, bf16[2,128,128]{2,1,0:T(8,128)(2,1)}, u32[]{:S(2)}) copy-start(bf16[2,128,128]{2,1,0:T(8,128)(2,1)} %get-tuple-element.152) | copy-start | bytes 196612
  166.9 7.6 %copy-start.4 = (bf16[2,128,128]{2,1,0:T(8,128)(2,1)S(1)}, bf16[2,128,128]{2,1,0:T(8,128)(2,1)}, u32[]{:S(2)}) copy-start(bf16[2,128,128]{2,1,0:T(8,128)(2,1)} %get-tuple-element.153) | copy-start | bytes 196612
  171.5 7.8 %collective-permute-start.36 = (bf16[1,128,384]{2,1,0:T(8,128)(2,1)S(1)}, bf16[1,128,384]{2,1,0:T(8,128)(2,1)S(1)}, u32[]{:S(2)}, u32[]{:S(2)}) collective-permute-start(bf16[1,128,384]{2,1,0:T(8,128)(2,1)S(1)} %get-tuple-element.141), channel_id=1, source_target_pairs={{0,2},{1,3},{2,0},{3,1},{4,6},{5,7},{6,4},{7,5},{8,10},{9,11},{10,... | collective-permute-start | bytes 294920 | tf_op jit(solution)/shard_map/ppermute | solution.py:39
  171.6 7.7 %collective-permute-start.37 = (bf16[1,128,256]{2,1,0:T(8,128)(2,1)S(1)}, bf16[1,128,256]{2,1,0:T(8,128)(2,1)S(1)}, u32[]{:S(2)}, u32[]{:S(2)}) collective-permute-start(bf16[1,128,256]{2,1,0:T(8,128)(2,1)S(1)} %get-tuple-element.142), channel_id=1, source_target_pairs={{0,2},{1,3},{2,0},{3,1},{4,6},{5,7},{6,4},{7,5},{8,10},{9,11},{10,... | collective-permute-start | bytes 196616 | tf_op jit(solution)/shard_map/ppermute | solution.py:39

commit v2 on v1

--- a/solution.py
+++ b/solution.py
@@ -14,17 +14,21 @@
 D_Z = 8192
 
 SCHEDULE = (
-    ("dec", 0, 384, (0, 1, 3, 5, 7)),
-    ("dec", 384, 640, (0, 2, 4, 6, 8)),
-    ("dec", 1024, 1024, (1, 3, 5, 7, 9)),
-    ("enc", 1280, 768, (2, 4, 6, 8, 10)),
-    ("enc", 640, 640, (3, 5, 7, 9, 10)),
-    ("enc", 256, 384, (4, 6, 8, 10, 11)),
-    ("enc", 0, 256, (5, 7, 9, 10, 11)),
+    ("dec", 0, 512, (0, 1, 3, 5, 7), False),
+    ("dec", 512, 512, (0, 2, 4, 6, 8), True),
+    ("dec", 1024, 1024, (1, 3, 5, 7, 9), False),
+    ("enc", 1280, 768, (2, 4, 6, 8, 10), False),
+    ("enc", 768, 512, (3, 5, 7, 9, 10), False),
+    ("enc", 256, 512, (4, 6, 8, 10, 11), False),
+    ("enc", 0, 256, (5, 7, 9, 10, 11), False),
 )
-SHORT_SCHEDULE = (("dec", 0, 1, (0, 2, 4, 6, 8)), ("enc", 0, 1, (1, 3, 5, 7, 9)))
+SHORT_SCHEDULE = (
+    ("dec", 0, 1, (0, 2, 4, 6, 8), False),
+    ("enc", 0, 1, (1, 3, 5, 7, 9), False),
+)
 COST = 100
-ATTENTION_STEP = 0
+AHEAD = 8
+TOGETHER = 2048
 FIRST_SQUARES = 4
 FIRST_TERMS = 3
 
@@ -39,7 +43,7 @@
     return lax.ppermute(value, axis, [(i, i ^ mask) for i in range(count)])
 
 
-def from_last(value, axis):
+def from_last(value, axis, tokens=()):
     count = lax.axis_size(axis)
     rank = count - 1 - lax.axis_index(axis)
     reach = 1
@@ -48,6 +52,8 @@
             (count - 1 - i, count - 1 - i - reach) for i in range(reach) if i + reach < count
         ]
         moved = lax.ppermute(value, axis, pairs)
+        value, *_ = lax.optimization_barrier((value, *tokens))
+        tokens = ()
         value = jnp.where((rank >= reach) & (rank < 2 * reach), moved, value)
         reach *= 2
     return value
@@ -123,16 +129,18 @@
 def step_kernel(plan, size, latents, tp, *refs):
     refs = list(refs)
     take = lambda count: [refs.pop(0) for _ in range(count)]
-    sources = {kind: take(2) for kind in plan["kinds"]}
-    jobs = plan["jobs"]
+    kinds, jobs, pieces = plan["kinds"], plan["jobs"], plan["pieces"]
+    sources = {kind: take(2) for kind in kinds}
     incoming = [take(stage) for _, stage in jobs]
-    extras = [take(2 + len(pieces)) if pieces else () for pieces in plan["pieces"]]
+    extras = [take(2 + len(piece)) if piece else () for piece in pieces]
     outs = take(len(jobs))
-    weight_bufs, sum_bufs, out_bufs = [], [], []
-    for _, stage in jobs:
+    acts = {kind: take(1)[0] for kind in kinds}
+    weight_bufs, sum_bufs, out_bufs, extra_bufs = [], [], [], []
+    for (_, stage), piece in zip(jobs, pieces):
         weight_bufs.append(take(1)[0])
         sum_bufs.append(take(stage))
         out_bufs.append(take(1)[0])
+        extra_bufs.append(take(3) if piece else ())
     sems = take(1)[0]
     me = lax.axis_index("section") * tp + lax.axis_index("tp")
     used = 0
@@ -142,7 +150,7 @@
         used += 1
         return pltpu.make_async_copy(source, target, sems.at[used - 1])
 
-    arrivals = []
+    arrivals, seen = [], set()
     for number, (chunk, stage) in enumerate(jobs):
         blocks = relative_blocks(chunk.order, stage, size)
         weight = sources[chunk.kind][1]
@@ -153,21 +161,38 @@
             else:
                 piece = weight.at[:, pl.ds(first, chunk.width)]
             wanted = [copy(piece, weight_bufs[number].at[index])]
+            if chunk.kind not in seen:
+                seen.add(chunk.kind)
+                wanted.insert(0, copy(sources[chunk.kind][0], acts[chunk.kind]))
             for earlier in range(stage):
-                sent = relative_blocks(chunk.order, earlier, size)
-                place = sent.index(r ^ chunk.order[earlier])
-                wanted.append(
-                    copy(incoming[number][earlier].at[place], sum_bufs[number][earlier].at[index])
-                )
-            for item in wanted:
+                for place, to, count in runs(chunk.order, earlier, stage, size):
+                    if to == index:
+                        source = incoming[number][earlier].at[pl.ds(place, count)]
+                        target = sum_bufs[number][earlier].at[pl.ds(to, count)]
+                        wanted.append(copy(source, target))
+            if pieces[number]:
+                inverse, bias, *attribs = extras[number]
+                inverse_buf, bias_buf, attrib_buf = extra_bufs[number]
+                wanted.append(copy(inverse, inverse_buf))
+                wanted.append(copy(bias.at[:, pl.ds(chunk.offset, chunk.width)], bias_buf))
+                place = 0
+                for ref, (first, last) in zip(attribs, pieces[number]):
+                    source = ref.at[0, :, pl.ds(first, last - first)]
+                    wanted.append(copy(source, attrib_buf.at[:, pl.ds(place, last - first)]))
+                    place += last - first
+            arrivals.append(wanted)
+    for item in sum(arrivals[:AHEAD], []):
+        item.start()
+    leaving, current = [], 0
+    for number, (chunk, stage) in enumerate(jobs):
+        act = acts[chunk.kind]
+        count, sent = len(relative_blocks(chunk.order, stage, size)), 0
+        for index in range(count):
+            for item in arrivals[current]:
+                item.wait()
+            for item in sum(arrivals[current + AHEAD : current + AHEAD + 1], []):
                 item.start()
-            arrivals.append(wanted)
-    leaving = []
-    for number, (chunk, stage) in enumerate(jobs):
-        act = sources[chunk.kind][0]
-        for index in range(len(relative_blocks(chunk.order, stage, size))):
-            for item in arrivals.pop(0):
-                item.wait()
+            current += 1
             total = lax.dot_general(
                 act[...],
                 weight_bufs[number][index],
@@ -176,67 +201,78 @@
             )
             for buf in sum_bufs[number]:
                 total = total + buf[index].astype(jnp.float32)
-            if plan["pieces"][number]:
-                inverse, bias, *attribs = extras[number]
-                active = jnp.maximum(total * inverse[:, :1] + bias[...], 0.0)
-                attrib = [
-                    ref[0, :, first:last]
-                    for ref, (first, last) in zip(attribs, plan["pieces"][number])
-                ]
-                attrib = attrib[0] if len(attrib) == 1 else jnp.concatenate(attrib, axis=1)
-                total = jnp.sum(active * attrib, axis=0, keepdims=True)
+            if pieces[number]:
+                inverse_buf, bias_buf, attrib_buf = extra_bufs[number]
+                active = jnp.maximum(total * inverse_buf[:, :1] + bias_buf[...], 0.0)
+                total = jnp.sum(active * attrib_buf[...], axis=0, keepdims=True)
             out_bufs[number][index] = total.astype(out_bufs[number].dtype)
-            item = copy(out_bufs[number].at[index], outs[number].at[index])
-            item.start()
-            leaving.append(item)
+            if index + 1 == count or (index + 1 - sent) * chunk.width >= TOGETHER:
+                part = pl.ds(sent, index + 1 - sent)
+                item = copy(out_bufs[number].at[part], outs[number].at[part])
+                item.start()
+                leaving.append(item)
+                sent = index + 1
     for item in leaving:
         item.wait()
+
+
+def runs(order, earlier, stage, size):
+    sent = relative_blocks(order, earlier, size)
+    found = []
+    for index, r in enumerate(relative_blocks(order, stage, size)):
+        place = sent.index(r ^ order[earlier])
+        if found and found[-1][0] + found[-1][2] == place:
+            found[-1][2] += 1
+        else:
+            found.append([place, index, 1])
+    return found
 
 
 def run_step(jobs, acts, weights, size, latents, tp, finish):
     kinds = [kind for kind in ("dec", "enc") if any(c.kind == kind for c, _ in jobs)]
     rows, inner = acts[kinds[0]].shape
-    operands, specs = [], []
+    operands = []
     anywhere = pl.BlockSpec(memory_space=pltpu.HBM)
-    vmem = pl.BlockSpec(memory_space=pltpu.VMEM)
     for kind in kinds:
         operands += [acts[kind], weights[kind]]
-        specs += [vmem, anywhere]
     for chunk, stage in jobs:
         operands += chunk.received[:stage]
-        specs += [anywhere] * stage
-    outs, scratch, copies, flops, moved = [], [], 0, 0, 0
-    pieces = []
+    scratch = [pltpu.VMEM((rows, inner), jnp.bfloat16)] * len(kinds)
+    outs, pieces, copies, flops, moved = [], [], len(kinds), 0, 0
     for chunk, stage in jobs:
         last = stage == len(chunk.order)
+        count = len(relative_blocks(chunk.order, stage, size))
+        shape = (count, rows, chunk.width)
+        dtype = jnp.float32 if last else jnp.bfloat16
         pieces.append(())
+        side = (chunk.width, inner) if chunk.kind == "dec" else (inner, chunk.width)
+        scratch.append(pltpu.VMEM((count, *side), jnp.bfloat16))
+        scratch += [pltpu.VMEM(shape, jnp.bfloat16)] * stage
         if last and chunk.kind == "enc":
             values, pieces[-1] = finish(chunk)
             operands += values
-            specs += [vmem] * len(values)
-        count = len(relative_blocks(chunk.order, stage, size))
-        shape = (count, rows, chunk.width)
-        if last:
-            dtype = jnp.float32
-            if chunk.kind == "enc":
-                shape = (1, 1, chunk.width)
-        else:
-            dtype = jnp.bfloat16
+            copies += len(values)
+            shape = (1, 1, chunk.width)
+        scratch.append(pltpu.VMEM(shape, dtype))
+        if pieces[-1]:
+            scratch += [
+                pltpu.VMEM((rows, HEAD_SIZE), jnp.float32),
+                pltpu.VMEM((1, chunk.width), jnp.float32),
+                pltpu.VMEM((rows, chunk.width), jnp.float32),
+            ]
         outs.append(jax.ShapeDtypeStruct(shape, dtype))
-        side = (chunk.width, inner) if chunk.kind == "dec" else (inner, chunk.width)
-        scratch.append(pltpu.VMEM((count, *side), jnp.bfloat16))
-        scratch += [pltpu.VMEM((count, rows, chunk.width), jnp.bfloat16)] * stage
-        scratch.append(pltpu.VMEM(shape, dtype))
         copies += count * (stage + 2)
         flops += 2 * count * rows * inner * chunk.width
         moved += 2 * count * chunk.width * (inner + (stage + 1) * rows)
     results = pl.pallas_call(
-        functools.partial(step_kernel, {"kinds": kinds, "jobs": jobs, "pieces": pieces}, size, latents, tp),
+        functools.partial(
+            step_kernel, {"kinds": kinds, "jobs": jobs, "pieces": pieces}, size, latents, tp
+        ),
         out_shape=outs,
-        in_specs=specs,
+        in_specs=[anywhere] * len(operands),
         out_specs=[anywhere] * len(outs),
         scratch_shapes=[*scratch, pltpu.SemaphoreType.DMA((copies,))],
-        compiler_params=pltpu.CompilerParams(vmem_limit_bytes=24 * 2**20),
+        compiler_params=pltpu.CompilerParams(vmem_limit_bytes=32 * 2**20),
         cost_estimate=pl.CostEstimate(
             flops=int(COST * flops), bytes_accessed=int(COST * moved), transcendentals=0
         ),
@@ -268,16 +304,23 @@
         tp_size,
     )
     core, across, near, far = tp_size, 2 * tp_size, 1, 2
-    order = (core, across, near, far)
-
-    scored_grad = from_last(out_grad, "ctx")
+    orders = {False: (core, across, near, far), True: (core, near, far, across)}
+
+    pair = jnp.stack(
+        [
+            lax.dynamic_slice_in_dim(keys, local_kv * HEAD_SIZE, HEAD_SIZE, 1),
+            lax.dynamic_slice_in_dim(values, local_kv * HEAD_SIZE, HEAD_SIZE, 1),
+        ]
+    )
+    pairs = [pair] + [shifted(pair, "ctx", -turn) for turn in range(1, cycle_size)]
+    scored_grad = from_last(out_grad, "ctx", pairs[1:])
     latents = enc_weight.shape[1] // group[1]
     weights = {"dec": dec_weight, "enc": enc_weight}
-    full = max(first + width for _, first, width, _ in SCHEDULE)
+    full = max(first + width for _, first, width, *_ in SCHEDULE)
     schedule, unit = (SHORT_SCHEDULE, latents) if latents % full else (SCHEDULE, latents // full)
     chunks = [
-        Chunk(kind, first * unit, width * unit, times, order)
-        for kind, first, width, times in schedule
+        Chunk(kind, first * unit, width * unit, times, orders[late])
+        for kind, first, width, times, late in schedule
     ]
     steps = [
         [(chunk, chunk.steps.index(step)) for chunk in chunks if step in chunk.steps]
@@ -285,18 +328,8 @@
     ]
     acts = {"dec": scored_grad}
     early = next(step for step, jobs in enumerate(steps) if any(c.kind == "enc" for c, _ in jobs))
-    for step in range(early):
-        run_step(steps[step], acts, weights, group[1], latents, tp_size, None)
-        if step == ATTENTION_STEP:
-            queries, _ = lax.optimization_barrier((queries, acts["dec"]))
-
-    pair = jnp.stack(
-        [
-            lax.dynamic_slice_in_dim(keys, local_kv * HEAD_SIZE, HEAD_SIZE, 1),
-            lax.dynamic_slice_in_dim(values, local_kv * HEAD_SIZE, HEAD_SIZE, 1),
-        ]
-    )
-    pairs = [pair] + [shifted(pair, "ctx", -turn) for turn in range(1, cycle_size)]
+    run_step(steps[0], acts, weights, group[1], latents, tp_size, None)
+    queries, _ = lax.optimization_barrier((queries, acts["dec"]))
     attn_flat, query_grad, *terms = pl.pallas_call(
         functools.partial(attention_kernel, cycle_size),
         out_shape=[
@@ -306,7 +339,10 @@
         ],
         compiler_params=pltpu.CompilerParams(vmem_limit_bytes=32 * 2**20),
     )(queries, out_grad, *pairs)
-    scored_out = from_last(attn_flat, "ctx")
+    acts["dec"], _ = lax.optimization_barrier((acts["dec"], attn_flat))
+    for step in range(1, early):
+        run_step(steps[step], acts, weights, group[1], latents, tp_size, None)
+    scored_out = from_last(attn_flat, "ctx", (acts["dec"],))
     wide_out = scored_out.astype(jnp.float32)
     squares = jnp.sum(wide_out * wide_out, axis=1)
     acts["enc"], _ = lax.optimization_barrier((scored_out, acts["dec"]))
@@ -363,7 +399,7 @@
         inverse = jnp.broadcast_to(
             lax.rsqrt(squares / D_Z + 1e-06)[:, None], (row_count, HEAD_SIZE)
         )
-        values, pieces = [inverse, lax.slice_in_dim(bias, chunk.offset, end, axis=1)], []
+        values, pieces = [inverse, bias], []
         for other in chunks:
             first, last = max(other.offset, chunk.offset), min(other.offset + other.width, end)
             if other.kind == "dec" and first < last:

time: 182 us -> 163 us (0.90)
  waiting for transfers between devices: 61.3 us -> 46.2 us
  Pallas kernels: 75.7 us -> 64.6 us
  starting transfers between devices: 38.7 us -> 45.9 us
    pallas_call x12, Pallas kernels: 72.9 us -> 61.7 us  [run_step(): pl.pallas_call(functools.partial(step_kernel, {'kinds': kinds, 'jobs': jo...]
    ppermute x2, waiting for transfers between devices: 10.9 us -> 0.01 us  [from_last(): moved = lax.ppermute(value, axis, pairs)]
    ppermute x34, starting transfers between devices: 32.8 us -> 37.4 us  [swapped(): return lax.ppermute(value, axis, [(i, i ^ mask) for i in range(count)])]
    ppermute x34, waiting for transfers between devices: 46.6 us -> 42 us  [swapped(): return lax.ppermute(value, axis, [(i, i ^ mask) for i in range(count)])]
    ppermute x2, starting transfers between devices: 3.33 us -> 5.75 us  [shifted(): lax.ppermute(value, axis, [(i, (i + steps) % count) for i in range(count)])]
  transfers between devices with their start and end apart: 38 -> 38, of which waited for: 12 -> 11; matrix products, arithmetic and copies ran while one was open for 2% -> 3% of each run, Pallas kernels for 33% -> 31%
where the time goes in v2:
time: 163 us
  Pallas kernels  64.6 us (40%)
  waiting for transfers between devices  46.2 us (28%)
  starting transfers between devices  45.9 us (28%)
  other arithmetic  4.24 us (3%)
    pallas_call x12, Pallas kernels, run_step(): pl.pallas_call(functools.partial(step_kernel, {'kinds': kinds, 'jobs': jo...  61.7 us
    ppermute x34, waiting for transfers between devices, swapped(): return lax.ppermute(value, axis, [(i, i ^ mask) for i in range(count)])  42 us
    ppermute x34, starting transfers between devices, swapped(): return lax.ppermute(value, axis, [(i, i ^ mask) for i in range(count)])  37.4 us
    ppermute x2, starting transfers between devices, shifted(): lax.ppermute(value, axis, [(i, (i + steps) % count) for i in range(count)])  5.75 us
    ppermute x2, waiting for transfers between devices, shifted(): lax.ppermute(value, axis, [(i, (i + steps) % count) for i in range(count)])  4.21 us
  transfers between devices with their start and end apart: 38, of which 11 were waited for; matrix products, arithmetic and copies ran while one was open for 3% of the time, Pallas kernels for 31%

profile of v2, /device:TPU:0, one launch (start us, length us, event | category | flops | bytes accessed | tf_op | source)
XLA Modules:
  0.0 162.8 jit_solution(17160759188828376816)
XLA Ops:
  0.6 1.3 collective-permute-start
  2.0 0.8 dynamic-slice_bitcast_fusion
  2.7 3.0 %collective-permute-start.1 = (bf16[2,128,128]{2,1,0:T(8,128)(2,1)S(1)}, bf16[2,128,128]{2,1,0:T(8,128)(2,1)S(1)}, u32[]{:S(2)}, u32[]{:S(2)}) collective-permute-start(bf16[2,128,128]{2,1,0:T(8,128)(2,1)S(1)} %pad_maximum_fusion.1.refs_0_), channel_id=1, source_target_pairs={{0,16},{16,0},{1,17},{17,1},{2,18},{18,2},{3,19},{19,3},{4,20},{20... | collective-permute-start | bytes 196616 | tf_op jit(solution)/shard_map/ppermute | solution.py:38
  5.8 4.2 %collective-permute-done.1.refs_1_ = bf16[2,128,128]{2,1,0:T(8,128)(2,1)S(1)} collective-permute-done((bf16[2,128,128]{2,1,0:T(8,128)(2,1)S(1)}, bf16[2,128,128]{2,1,0:T(8,128)(2,1)S(1)}, u32[]{:S(2)}, u32[]{:S(2)}) %collective-permute-start.1) | collective-permute-done | bytes 65568 | tf_op jit(solution)/shard_map/ppermute | solution.py:38
  10.0 6.6 %shard_map.102 = (bf16[8,128,512]{2,1,0:T(8,128)(2,1)}, bf16[8,128,512]{2,1,0:T(8,128)(2,1)S(1)}) custom-call(bf16[128,512]{1,0:T(8,128)(2,1)S(1)} %broadcast_select_fusion.1.refs_0_, bf16[32768,512]{1,0:T(8,128)(2,1)} %refs_1_.21), custom_call_target="tpu_custom_call" | custom-call | flops 107374182400 | bytes 1048576000 | tf_op jit(solution)/shard_map/pallas_call | solution.py:267
  16.7 2.9 %shard_map.103 = (bf16[128,512]{1,0:T(8,128)(2,1)S(1)}, bf16[128,512]{1,0:T(8,128)(2,1)}, f32[2,128,128]{2,1,0:T(8,128)S(1)}, f32[2,128,128]{2,1,0:T(8,128)}) custom-call(bf16[128,512]{1,0:T(8,128)(2,1)S(1)} %copy-done.1, bf16[128,512]{1,0:T(8,128)(2,1)S(1)} %copy-done, bf16[2,128,128]{2,1,0:T(8,128)(2,1)S(1)} %pad_maximum_fusion.1.refs_0_, ...), custom_call_target="tpu_custom_call" | custom-call | tf_op jit(solution)/shard_map/pallas_call | solution.py:333
  19.6 1.5 collective-permute-start.2
  21.1 2.7 %collective-permute-start.7 = (f32[2,128,128]{2,1,0:T(8,128)}, f32[2,128,128]{2,1,0:T(8,128)}, u32[]{:S(2)}, u32[]{:S(2)}) collective-permute-start(f32[2,128,128]{2,1,0:T(8,128)} %get-tuple-element.98), channel_id=1, source_target_pairs={{0,16},{16,0},{1,17},{17,1},{2,18},{18,2},{3,19},{19,3},{4,20},{20... | collective-permute-start | bytes 393224 | tf_op jit(solution)/shard_map/ppermute | solution.py:38
  23.8 6.7 %shard_map.104 = (bf16[4,128,512]{2,1,0:T(8,128)(2,1)S(1)}, bf16[8,128,1024]{2,1,0:T(8,128)(2,1)S(1)}) custom-call(bf16[128,512]{1,0:T(8,128)(2,1)S(1)} %broadcast_select_fusion.1.refs_0_, bf16[32768,512]{1,0:T(8,128)(2,1)} %refs_1_.21, bf16[8,128,512]{2,1,0:T(8,128)(2,1)S(1)} %collective-permute-done.3.refs_2_.refs_4_), custom_call_target="tpu_custom_call" | custom-call | flops 134217728000 | bytes 1363148800 | tf_op jit(solution)/shard_map/pallas_call | solution.py:267
  30.6 2.4 %collective-permute-start.5 = (bf16[4,128,512]{2,1,0:T(8,128)(2,1)S(1)}, bf16[4,128,512]{2,1,0:T(8,128)(2,1)S(1)}, u32[]{:S(2)}, u32[]{:S(2)}) collective-permute-start(bf16[4,128,512]{2,1,0:T(8,128)(2,1)S(1)} %get-tuple-element.86), channel_id=1, source_target_pairs={{0,8},{4,12},{8,0},{12,4},{1,9},{5,13},{9,1},{13,5},{2,10},{6,14},... | collective-permute-start | bytes 1572872 | tf_op jit(solution)/shard_map/ppermute | solution.py:43
  33.8 5.7 %shard_map.105 = (bf16[4,128,512]{2,1,0:T(8,128)(2,1)S(1)}, bf16[8,128,768]{2,1,0:T(8,128)(2,1)S(1)}) custom-call(bf16[128,512]{1,0:T(8,128)(2,1)S(1)} %broadcast_select_fusion.1.refs_0_, bf16[32768,512]{1,0:T(8,128)(2,1)} %refs_1_.21, bf16[128,512]{1,0:T(8,128)(2,1)S(1)} %get-tuple-element.146.refs_2_.refs_0_, bf16[512,32768]{1,0:T(8,128)(2,1)} %refs_1_.23, ...), custom_call_target="tpu_custom_call" | custom-call | flops 107374182400 | bytes 1101004800 | tf_op jit(solution)/shard_map/pallas_call | solution.py:267
  39.5 1.6 %collective-permute-start.8 = (bf16[4,128,512]{2,1,0:T(8,128)(2,1)S(1)}, bf16[4,128,512]{2,1,0:T(8,128)(2,1)S(1)}, u32[]{:S(2)}, u32[]{:S(2)}) collective-permute-start(bf16[4,128,512]{2,1,0:T(8,128)(2,1)S(1)} %get-tuple-element.91), channel_id=1, source_target_pairs={{0,1},{1,0},{2,3},{3,2},{4,5},{5,4},{6,7},{7,6},{8,9},{9,8},{10,11... | collective-permute-start | bytes 1572872 | tf_op jit(solution)/shard_map/ppermute | solution.py:43
  41.1 4.4 %collective-permute-done.5.refs_5_ = bf16[4,128,512]{2,1,0:T(8,128)(2,1)S(1)} collective-permute-done((bf16[4,128,512]{2,1,0:T(8,128)(2,1)S(1)}, bf16[4,128,512]{2,1,0:T(8,128)(2,1)S(1)}, u32[]{:S(2)}, u32[]{:S(2)}) %collective-permute-start.5) | collective-permute-done | bytes 524320 | tf_op jit(solution)/shard_map/ppermute | solution.py:43
  45.5 6.4 %shard_map.106 = (bf16[2,128,512]{2,1,0:T(8,128)(2,1)S(1)}, bf16[4,128,1024]{2,1,0:T(8,128)(2,1)S(1)}, bf16[8,128,512]{2,1,0:T(8,128)(2,1)S(1)}) custom-call(bf16[128,512]{1,0:T(8,128)(2,1)S(1)} %broadcast_select_fusion.1.refs_0_, bf16[32768,512]{1,0:T(8,128)(2,1)} %refs_1_.21, bf16[128,512]{1,0:T(8,128)(2,1)S(1)} %get-tuple-element.146.refs_2_.refs_0_, ...), custom_call_target="tpu_custom_call" | custom-call | flops 120795955200 | bytes 1336934400 | tf_op jit(solution)/shard_map/pallas_call | solution.py:267
  52.0 0.9 add.30
  52.9 1.9 %collective-permute-start.10 = (f32[2,128,128]{2,1,0:T(8,128)S(1)}, f32[2,128,128]{2,1,0:T(8,128)S(1)}, u32[]{:S(2)}, u32[]{:S(2)}) collective-permute-start(f32[2,128,128]{2,1,0:T(8,128)S(1)} %add.30), channel_id=1, source_target_pairs={{0,1},{1,0},{2,3},{3,2},{4,5},{5,4},{6,7},{7,6},{8,9},{9,8},{10,11... | collective-permute-start | bytes 393224 | tf_op jit(solution)/shard_map/ppermute | solution.py:43
  55.0 1.7 %collective-permute-start.14 = (bf16[4,128,1024]{2,1,0:T(8,128)(2,1)S(1)}, bf16[4,128,1024]{2,1,0:T(8,128)(2,1)S(1)}, u32[]{:S(2)}, u32[]{:S(2)}) collective-permute-start(bf16[4,128,1024]{2,1,0:T(8,128)(2,1)S(1)} %get-tuple-element.108), channel_id=1, source_target_pairs={{0,8},{4,12},{8,0},{12,4},{1,9},{5,13},{9,1},{13,5},{2,10},{6,14},... | collective-permute-start | bytes 3145736 | tf_op jit(solution)/shard_map/ppermute | solution.py:43
  56.7 6.2 %shard_map.107 = (bf16[2,128,512]{2,1,0:T(8,128)(2,1)S(1)}, bf16[4,128,768]{2,1,0:T(8,128)(2,1)S(1)}, bf16[8,128,512]{2,1,0:T(8,128)(2,1)S(1)}) custom-call(bf16[128,512]{1,0:T(8,128)(2,1)S(1)} %broadcast_select_fusion.1.refs_0_, bf16[32768,512]{1,0:T(8,128)(2,1)} %refs_1_.21, bf16[128,512]{1,0:T(8,128)(2,1)S(1)} %get-tuple-element.146.refs_2_.refs_0_, ...), custom_call_target="tpu_custom_call" | custom-call | flops 107374182400 | bytes 1179648000 | tf_op jit(solution)/shard_map/pallas_call | solution.py:267
  62.9 2.7 %collective-permute-start.17 = (bf16[2,128,512]{2,1,0:T(8,128)(2,1)S(1)}, bf16[2,128,512]{2,1,0:T(8,128)(2,1)S(1)}, u32[]{:S(2)}, u32[]{:S(2)}) collective-permute-start(bf16[2,128,512]{2,1,0:T(8,128)(2,1)S(1)} %get-tuple-element.102), channel_id=1, source_target_pairs={{0,2},{1,3},{2,0},{3,1},{4,6},{5,7},{6,4},{7,5},{8,10},{9,11},{10,... | collective-permute-start | bytes 786440 | tf_op jit(solution)/shard_map/ppermute | solution.py:43
  66.8 1.6 collective-permute-start.18
  68.4 12.6 %collective-permute-done.14.refs_8_.refs_9_.refs_5_ = bf16[4,128,1024]{2,1,0:T(8,128)(2,1)S(1)} collective-permute-done((bf16[4,128,1024]{2,1,0:T(8,128)(2,1)S(1)}, bf16[4,128,1024]{2,1,0:T(8,128)(2,1)S(1)}, u32[]{:S(2)}, u32[]{:S(2)}) %collective-permute-start.14) | collective-permute-done | bytes 1048608 | tf_op jit(solution)/shard_map/ppermute | solution.py:43
  81.0 2.8 %collective-permute-start.11 = (bf16[2,128,128]{2,1,0:T(8,128)(2,1)S(1)}, bf16[2,128,128]{2,1,0:T(8,128)(2,1)S(1)}, u32[]{:S(2)}, u32[]{:S(2)}) collective-permute-start(bf16[2,128,128]{2,1,0:T(8,128)(2,1)S(1)} %add.31), channel_id=1, source_target_pairs={{0,2},{1,3},{2,0},{3,1},{4,6},{5,7},{6,4},{7,5},{8,10},{9,11},{10,... | collective-permute-start | bytes 196616 | tf_op jit(solution)/shard_map/ppermute | solution.py:43
  83.9 6.3 %shard_map.108 = (bf16[1,128,512]{2,1,0:T(8,128)(2,1)S(1)}, bf16[2,128,1024]{2,1,0:T(8,128)(2,1)S(1)}, bf16[4,128,512]{2,1,0:T(8,128)(2,1)S(1)}, bf16[8,128,256]{2,1,0:T(8,128)(2,1)S(1)}) custom-call(bf16[128,512]{1,0:T(8,128)(2,1)S(1)} %broadcast_select_fusion.1.refs_0_, bf16[32768,512]{1,0:T(8,128)(2,1)} %refs_1_.21, ...), custom_call_target="tpu_custom_call" | custom-call | flops 87241523200 | bytes 1048576000 | tf_op jit(solution)/shard_map/pallas_call | solution.py:267
  90.3 1.8 %collective-permute-start.20 = (f32[128]{0:T(128)S(1)}, f32[128]{0:T(128)S(1)}, u32[]{:S(2)}, u32[]{:S(2)}) collective-permute-start(f32[128]{0:T(128)S(1)} %add.33), channel_id=1, source_target_pairs={{0,1},{1,0},{2,3},{3,2},{4,5},{5,4},{6,7},{7,6},{8,9},{9,8},{10,11... | collective-permute-start | bytes 1544 | tf_op jit(solution)/shard_map/ppermute | solution.py:43
  93.0 4.0 %collective-permute-done.18.refs_8_.refs_9_.refs_3_ = bf16[4,128,768]{2,1,0:T(8,128)(2,1)S(1)} collective-permute-done((bf16[4,128,768]{2,1,0:T(8,128)(2,1)S(1)}, bf16[4,128,768]{2,1,0:T(8,128)(2,1)S(1)}, u32[]{:S(2)}, u32[]{:S(2)}) %collective-permute-start.18) | collective-permute-done | bytes 786464 | tf_op jit(solution)/shard_map/ppermute | solution.py:43
  97.0 1.6 collective-permute-start.23
  98.6 4.5 %shard_map.109 = (bf16[1,128,512]{2,1,0:T(8,128)(2,1)S(1)}, bf16[2,128,768]{2,1,0:T(8,128)(2,1)S(1)}, bf16[4,128,512]{2,1,0:T(8,128)(2,1)S(1)}) custom-call(bf16[128,512]{1,0:T(8,128)(2,1)S(1)} %broadcast_select_fusion.1.refs_0_, bf16[32768,512]{1,0:T(8,128)(2,1)} %refs_1_.21, bf16[128,512]{1,0:T(8,128)(2,1)S(1)} %get-tuple-element.146.refs_2_.refs_0_, ...), custom_call_target="tpu_custom_call" | custom-call | flops 53687091200 | bytes 694681600 | tf_op jit(solution)/shard_map/pallas_call | solution.py:267
  103.6 1.7 %collective-permute-start.27 = (bf16[2,128,768]{2,1,0:T(8,128)(2,1)S(1)}, bf16[2,128,768]{2,1,0:T(8,128)(2,1)S(1)}, u32[]{:S(2)}, u32[]{:S(2)}) collective-permute-start(bf16[2,128,768]{2,1,0:T(8,128)(2,1)S(1)} %get-tuple-element.131), channel_id=1, source_target_pairs={{0,1},{1,0},{2,3},{3,2},{4,5},{5,4},{6,7},{7,6},{8,9},{9,8},{10,11... | collective-permute-start | bytes 1179656 | tf_op jit(solution)/shard_map/ppermute | solution.py:43
  105.3 4.1 %collective-permute-done.22.refs_10_.refs_6_ = bf16[2,128,1024]{2,1,0:T(8,128)(2,1)S(1)} collective-permute-done((bf16[2,128,1024]{2,1,0:T(8,128)(2,1)S(1)}, bf16[2,128,1024]{2,1,0:T(8,128)(2,1)S(1)}, u32[]{:S(2)}, u32[]{:S(2)}) %collective-permute-start.22) | collective-permute-done | bytes 524320 | tf_op jit(solution)/shard_map/ppermute | solution.py:43
  109.3 1.5 collective-permute-start.28
  110.8 1.0 collective-permute-done.23.refs_12_.refs_9_.refs_7_
  111.9 2.7 %collective-permute-start.25 = (f32[128]{0:T(128)S(1)}, f32[128]{0:T(128)S(1)}, u32[]{:S(2)}, u32[]{:S(2)}) collective-permute-start(f32[128]{0:T(128)S(1)} %add.34), channel_id=1, source_target_pairs={{0,2},{1,3},{2,0},{3,1},{4,6},{5,7},{6,4},{7,5},{8,10},{9,11},{10,... | collective-permute-start | bytes 1544 | tf_op jit(solution)/shard_map/ppermute | solution.py:43
  114.6 4.4 %shard_map.110 = (f32[1,128,512]{2,1,0:T(8,128)S(1)}, bf16[1,128,1024]{2,1,0:T(8,128)(2,1)S(1)}, bf16[2,128,512]{2,1,0:T(8,128)(2,1)S(1)}, bf16[4,128,256]{2,1,0:T(8,128)(2,1)S(1)}) custom-call(bf16[128,512]{1,0:T(8,128)(2,1)S(1)} %broadcast_select_fusion.1.refs_0_, bf16[32768,512]{1,0:T(8,128)(2,1)} %refs_1_.21, ...), custom_call_target="tpu_custom_call" | custom-call | flops 46976204800 | bytes 668467200 | tf_op jit(solution)/shard_map/pallas_call | solution.py:267
  119.3 1.7 %collective-permute-start.30 = (bf16[2,128,512]{2,1,0:T(8,128)(2,1)S(1)}, bf16[2,128,512]{2,1,0:T(8,128)(2,1)S(1)}, u32[]{:S(2)}, u32[]{:S(2)}) collective-permute-start(bf16[2,128,512]{2,1,0:T(8,128)(2,1)S(1)} %get-tuple-element.137), channel_id=1, source_target_pairs={{0,1},{1,0},{2,3},{3,2},{4,5},{5,4},{6,7},{7,6},{8,9},{9,8},{10,11... | collective-permute-start | bytes 786440 | tf_op jit(solution)/shard_map/ppermute | solution.py:43
  121.0 1.5 collective-permute-start.31
  122.5 3.4 %collective-permute-done.28.refs_12_.refs_11_.refs_3_ = bf16[4,128,512]{2,1,0:T(8,128)(2,1)S(1)} collective-permute-done((bf16[4,128,512]{2,1,0:T(8,128)(2,1)S(1)}, bf16[4,128,512]{2,1,0:T(8,128)(2,1)S(1)}, u32[]{:S(2)}, u32[]{:S(2)}) %collective-permute-start.28) | collective-permute-done | bytes 524320 | tf_op jit(solution)/shard_map/ppermute | solution.py:43
  125.9 4.1 %shard_map.111 = (f32[1,128,512]{2,1,0:T(8,128)S(1)}, bf16[1,128,768]{2,1,0:T(8,128)(2,1)S(1)}, bf16[2,128,512]{2,1,0:T(8,128)(2,1)S(1)}) custom-call(bf16[128,512]{1,0:T(8,128)(2,1)S(1)} %broadcast_select_fusion.1.refs_0_, bf16[32768,512]{1,0:T(8,128)(2,1)} %refs_1_.21, bf16[128,512]{1,0:T(8,128)(2,1)S(1)} %get-tuple-element.146.refs_2_.refs_0_, ...), custom_call_target="tpu_custom_call" | custom-call | flops 30198988800 | bytes 458752000 | tf_op jit(solution)/shard_map/pallas_call | solution.py:267
  130.0 2.7 %collective-permute-start.32 = (bf16[1,128,768]{2,1,0:T(8,128)(2,1)S(1)}, bf16[1,128,768]{2,1,0:T(8,128)(2,1)S(1)}, u32[]{:S(2)}, u32[]{:S(2)}) collective-permute-start(bf16[1,128,768]{2,1,0:T(8,128)(2,1)S(1)} %get-tuple-element.141), channel_id=1, source_target_pairs={{0,2},{1,3},{2,0},{3,1},{4,6},{5,7},{6,4},{7,5},{8,10},{9,11},{10,... | collective-permute-start | bytes 589832 | tf_op jit(solution)/shard_map/ppermute | solution.py:43
  132.8 1.6 collective-permute-start.34
  134.4 3.2 %shard_map.112 = (f32[1,128,1024]{2,1,0:T(8,128)S(1)}, bf16[1,128,512]{2,1,0:T(8,128)(2,1)S(1)}, bf16[2,128,256]{2,1,0:T(8,128)(2,1)S(1)}) custom-call(bf16[128,512]{1,0:T(8,128)(2,1)S(1)} %broadcast_select_fusion.1.refs_0_, bf16[32768,512]{1,0:T(8,128)(2,1)} %refs_1_.21, bf16[128,512]{1,0:T(8,128)(2,1)S(1)} %get-tuple-element.146.refs_2_.refs_0_, ...), custom_call_target="tpu_custom_call" | custom-call | flops 26843545600 | bytes 432537600 | tf_op jit(solution)/shard_map/pallas_call | solution.py:267
  138.4 2.2 %collective-permute-done.32.refs_5_ = bf16[1,128,768]{2,1,0:T(8,128)(2,1)S(1)} collective-permute-done((bf16[1,128,768]{2,1,0:T(8,128)(2,1)S(1)}, bf16[1,128,768]{2,1,0:T(8,128)(2,1)S(1)}, u32[]{:S(2)}, u32[]{:S(2)}) %collective-permute-start.32) | collective-permute-done | bytes 196640 | tf_op jit(solution)/shard_map/ppermute | solution.py:43
  140.6 3.7 %collective-permute-done.34.refs_12_.refs_4_ = bf16[2,128,512]{2,1,0:T(8,128)(2,1)S(1)} collective-permute-done((bf16[2,128,512]{2,1,0:T(8,128)(2,1)S(1)}, bf16[2,128,512]{2,1,0:T(8,128)(2,1)S(1)}, u32[]{:S(2)}, u32[]{:S(2)}) %collective-permute-start.34) | collective-permute-done | bytes 262176 | tf_op jit(solution)/shard_map/ppermute | solution.py:43
  144.3 1.4 collective-permute-done.35.refs_15_.refs_8_
  145.9 5.1 %shard_map.113 = (f32[1,1,768]{2,1,0:T(1,128)S(1)}, f32[1,1,512]{2,1,0:T(1,128)S(1)}, bf16[1,128,512]{2,1,0:T(8,128)(2,1)S(1)}, bf16[1,128,256]{2,1,0:T(8,128)(2,1)S(1)}) custom-call(bf16[128,512]{1,0:T(8,128)(2,1)S(1)} %get-tuple-element.146.refs_2_.refs_0_, bf16[512,32768]{1,0:T(8,128)(2,1)} %refs_1_.23, ...), custom_call_target="tpu_custom_call" | custom-call | flops 26843545600 | bytes 452198400 | tf_op jit(solution)/shard_map/pallas_call | solution.py:267
  151.0 2.0 %collective-permute-start.36 = (bf16[1,128,512]{2,1,0:T(8,128)(2,1)S(1)}, bf16[1,128,512]{2,1,0:T(8,128)(2,1)S(1)}, u32[]{:S(2)}, u32[]{:S(2)}) collective-permute-start(bf16[1,128,512]{2,1,0:T(8,128)(2,1)S(1)} %get-tuple-element.147), channel_id=1, source_target_pairs={{0,2},{1,3},{2,0},{3,1},{4,6},{5,7},{6,4},{7,5},{8,10},{9,11},{10,... | collective-permute-start | bytes 393224 | tf_op jit(solution)/shard_map/ppermute | solution.py:43
  153.0 0.9 collective-permute-start.37
  154.6 5.1 %collective-permute-done.37.refs_9_ = bf16[1,128,256]{2,1,0:T(8,128)(2,1)S(1)} collective-permute-done((bf16[1,128,256]{2,1,0:T(8,128)(2,1)S(1)}, bf16[1,128,256]{2,1,0:T(8,128)(2,1)S(1)}, u32[]{:S(2)}, u32[]{:S(2)}) %collective-permute-start.37) | collective-permute-done | bytes 65568 | tf_op jit(solution)/shard_map/ppermute | solution.py:43
  159.7 2.4 %shard_map.114 = (f32[1,1,512]{2,1,0:T(1,128)S(1)}, f32[1,1,256]{2,1,0:T(1,128)S(1)}) custom-call(bf16[128,512]{1,0:T(8,128)(2,1)S(1)} %get-tuple-element.146.refs_2_.refs_0_, bf16[512,32768]{1,0:T(8,128)(2,1)} %refs_1_.23, bf16[8,128,512]{2,1,0:T(8,128)(2,1)S(1)} %collective-permute-done.19.refs_9_.refs_11_.refs_10_.refs_2_, ...), custom_call_target="tpu_custom_call" | custom-call | flops 10066329600 | bytes 176947200 | tf_op jit(solution)/shard_map/pallas_call | solution.py:267
  (65 shorter events, 6.5 us)
Async XLA Ops:
  0.6 9.4 %collective-permute-start = (bf16[128,512]{1,0:T(8,128)(2,1)}, bf16[128,512]{1,0:T(8,128)(2,1)S(1)}, u32[]{:S(2)}, u32[]{:S(2)}) collective-permute-start(bf16[128,512]{1,0:T(8,128)(2,1)} %out_grad.1), channel_id=1, source_target_pairs={{16,0},{17,1},{18,2},{19,3},{20,4},{21,5},{22,6},{23,7},{24,8},{25... | collective-permute-start | bytes 393224 | tf_op jit(solution)/shard_map/ppermute | solution.py:54
  2.7 7.2 %collective-permute-start.1 = (bf16[2,128,128]{2,1,0:T(8,128)(2,1)S(1)}, bf16[2,128,128]{2,1,0:T(8,128)(2,1)S(1)}, u32[]{:S(2)}, u32[]{:S(2)}) collective-permute-start(bf16[2,128,128]{2,1,0:T(8,128)(2,1)S(1)} %pad_maximum_fusion.1.refs_0_), channel_id=1, source_target_pairs={{0,16},{16,0},{1,17},{17,1},{2,18},{18,2},{3,19},{19,3},{4,20},{20... | collective-permute-start | bytes 196616 | tf_op jit(solution)/shard_map/ppermute | solution.py:38
  10.0 6.7 %copy-start = (bf16[128,512]{1,0:T(8,128)(2,1)S(1)}, bf16[128,512]{1,0:T(8,128)(2,1)}, u32[]{:S(2)}) copy-start(bf16[128,512]{1,0:T(8,128)(2,1)} %out_grad.1) | copy-start | bytes 393220
  10.0 6.7 %copy-start.1 = (bf16[128,512]{1,0:T(8,128)(2,1)S(1)}, bf16[128,512]{1,0:T(8,128)(2,1)}, u32[]{:S(2)}) copy-start(bf16[128,512]{1,0:T(8,128)(2,1)} %queries) | copy-start | bytes 393220
  16.6 7.2 %collective-permute-start.3 = (bf16[8,128,512]{2,1,0:T(8,128)(2,1)}, bf16[8,128,512]{2,1,0:T(8,128)(2,1)S(1)}, u32[]{:S(2)}, u32[]{:S(2)}) collective-permute-start(bf16[8,128,512]{2,1,0:T(8,128)(2,1)} %get-tuple-element.79), channel_id=1, source_target_pairs={{0,4},{4,0},{8,12},{12,8},{1,5},{5,1},{9,13},{13,9},{2,6},{6,2},{1... | collective-permute-start | bytes 3145736 | tf_op jit(solution)/shard_map/ppermute | solution.py:43
  19.6 13.3 %collective-permute-start.2 = (bf16[128,512]{1,0:T(8,128)(2,1)S(1)}, bf16[128,512]{1,0:T(8,128)(2,1)S(1)}, u32[]{:S(2)}, u32[]{:S(2)}) collective-permute-start(bf16[128,512]{1,0:T(8,128)(2,1)S(1)} %get-tuple-element.88), channel_id=1, source_target_pairs={{16,0},{17,1},{18,2},{19,3},{20,4},{21,5},{22,6},{23,7},{24,8},{25... | collective-permute-start | bytes 393224 | tf_op jit(solution)/shard_map/ppermute | solution.py:54
  21.1 30.8 %collective-permute-start.7 = (f32[2,128,128]{2,1,0:T(8,128)}, f32[2,128,128]{2,1,0:T(8,128)}, u32[]{:S(2)}, u32[]{:S(2)}) collective-permute-start(f32[2,128,128]{2,1,0:T(8,128)} %get-tuple-element.98), channel_id=1, source_target_pairs={{0,16},{16,0},{1,17},{17,1},{2,18},{18,2},{3,19},{19,3},{4,20},{20... | collective-permute-start | bytes 393224 | tf_op jit(solution)/shard_map/ppermute | solution.py:38
  23.8 10.0 %collective-permute-start.4 = (bf16[8,128,512]{2,1,0:T(8,128)(2,1)S(1)}, bf16[8,128,512]{2,1,0:T(8,128)(2,1)S(1)}, u32[]{:S(2)}, u32[]{:S(2)}) collective-permute-start(bf16[8,128,512]{2,1,0:T(8,128)(2,1)S(1)} %get-tuple-element.90), channel_id=1, source_target_pairs={{0,4},{4,0},{8,12},{12,8},{1,5},{5,1},{9,13},{13,9},{2,6},{6,2},{1... | collective-permute-start | bytes 3145736 | tf_op jit(solution)/shard_map/ppermute | solution.py:43
  30.6 15.0 %collective-permute-start.5 = (bf16[4,128,512]{2,1,0:T(8,128)(2,1)S(1)}, bf16[4,128,512]{2,1,0:T(8,128)(2,1)S(1)}, u32[]{:S(2)}, u32[]{:S(2)}) collective-permute-start(bf16[4,128,512]{2,1,0:T(8,128)(2,1)S(1)} %get-tuple-element.86), channel_id=1, source_target_pairs={{0,8},{4,12},{8,0},{12,4},{1,9},{5,13},{9,1},{13,5},{2,10},{6,14},... | collective-permute-start | bytes 1572872 | tf_op jit(solution)/shard_map/ppermute | solution.py:43
  33.6 11.9 %collective-permute-start.6 = (bf16[8,128,1024]{2,1,0:T(8,128)(2,1)S(1)}, bf16[8,128,1024]{2,1,0:T(8,128)(2,1)S(1)}, u32[]{:S(2)}, u32[]{:S(2)}) collective-permute-start(bf16[8,128,1024]{2,1,0:T(8,128)(2,1)S(1)} %get-tuple-element.94), channel_id=1, source_target_pairs={{0,4},{4,0},{8,12},{12,8},{1,5},{5,1},{9,13},{13,9},{2,6},{6,2},{1... | collective-permute-start | bytes 6291464 | tf_op jit(solution)/shard_map/ppermute | solution.py:43
  39.5 15.5 %collective-permute-start.8 = (bf16[4,128,512]{2,1,0:T(8,128)(2,1)S(1)}, bf16[4,128,512]{2,1,0:T(8,128)(2,1)S(1)}, u32[]{:S(2)}, u32[]{:S(2)}) collective-permute-start(bf16[4,128,512]{2,1,0:T(8,128)(2,1)S(1)} %get-tuple-element.91), channel_id=1, source_target_pairs={{0,1},{1,0},{2,3},{3,2},{4,5},{5,4},{6,7},{7,6},{8,9},{9,8},{10,11... | collective-permute-start | bytes 1572872 | tf_op jit(solution)/shard_map/ppermute | solution.py:43
  41.1 21.8 %collective-permute-start.12 = (f32[128]{0:T(128)}, f32[128]{0:T(128)}, u32[]{:S(2)}, u32[]{:S(2)}) collective-permute-start(f32[128]{0:T(128)} %get-tuple-element.154), channel_id=1, source_target_pairs={{0,4},{4,0},{8,12},{12,8},{1,5},{5,1},{9,13},{13,9},{2,6},{6,2},{1... | collective-permute-start | bytes 1544 | tf_op jit(solution)/shard_map/ppermute | solution.py:43
  45.5 11.2 %collective-permute-start.9 = (bf16[8,128,768]{2,1,0:T(8,128)(2,1)S(1)}, bf16[8,128,768]{2,1,0:T(8,128)(2,1)S(1)}, u32[]{:S(2)}, u32[]{:S(2)}) collective-permute-start(bf16[8,128,768]{2,1,0:T(8,128)(2,1)S(1)} %get-tuple-element.101), channel_id=1, source_target_pairs={{0,4},{4,0},{8,12},{12,8},{1,5},{5,1},{9,13},{13,9},{2,6},{6,2},{1... | collective-permute-start | bytes 4718600 | tf_op jit(solution)/shard_map/ppermute | solution.py:43
  52.9 13.4 %collective-permute-start.10 = (f32[2,128,128]{2,1,0:T(8,128)S(1)}, f32[2,128,128]{2,1,0:T(8,128)S(1)}, u32[]{:S(2)}, u32[]{:S(2)}) collective-permute-start(f32[2,128,128]{2,1,0:T(8,128)S(1)} %add.30), channel_id=1, source_target_pairs={{0,1},{1,0},{2,3},{3,2},{4,5},{5,4},{6,7},{7,6},{8,9},{9,8},{10,11... | collective-permute-start | bytes 393224 | tf_op jit(solution)/shard_map/ppermute | solution.py:43
  54.8 12.1 %collective-permute-start.13 = (bf16[2,128,512]{2,1,0:T(8,128)(2,1)S(1)}, bf16[2,128,512]{2,1,0:T(8,128)(2,1)S(1)}, u32[]{:S(2)}, u32[]{:S(2)}) collective-permute-start(bf16[2,128,512]{2,1,0:T(8,128)(2,1)S(1)} %get-tuple-element.95), channel_id=1, source_target_pairs={{0,1},{1,0},{2,3},{3,2},{4,5},{5,4},{6,7},{7,6},{8,9},{9,8},{10,11... | collective-permute-start | bytes 786440 | tf_op jit(solution)/shard_map/ppermute | solution.py:43
  55.0 26.0 %collective-permute-start.14 = (bf16[4,128,1024]{2,1,0:T(8,128)(2,1)S(1)}, bf16[4,128,1024]{2,1,0:T(8,128)(2,1)S(1)}, u32[]{:S(2)}, u32[]{:S(2)}) collective-permute-start(bf16[4,128,1024]{2,1,0:T(8,128)(2,1)S(1)} %get-tuple-element.108), channel_id=1, source_target_pairs={{0,8},{4,12},{8,0},{12,4},{1,9},{5,13},{9,1},{13,5},{2,10},{6,14},... | collective-permute-start | bytes 3145736 | tf_op jit(solution)/shard_map/ppermute | solution.py:43
  56.7 24.3 %collective-permute-start.15 = (bf16[8,128,512]{2,1,0:T(8,128)(2,1)S(1)}, bf16[8,128,512]{2,1,0:T(8,128)(2,1)S(1)}, u32[]{:S(2)}, u32[]{:S(2)}) collective-permute-start(bf16[8,128,512]{2,1,0:T(8,128)(2,1)S(1)} %get-tuple-element.109), channel_id=1, source_target_pairs={{0,4},{4,0},{8,12},{12,8},{1,5},{5,1},{9,13},{13,9},{2,6},{6,2},{1... | collective-permute-start | bytes 3145736 | tf_op jit(solution)/shard_map/ppermute | solution.py:43
  62.9 29.9 %collective-permute-start.17 = (bf16[2,128,512]{2,1,0:T(8,128)(2,1)S(1)}, bf16[2,128,512]{2,1,0:T(8,128)(2,1)S(1)}, u32[]{:S(2)}, u32[]{:S(2)}) collective-permute-start(bf16[2,128,512]{2,1,0:T(8,128)(2,1)S(1)} %get-tuple-element.102), channel_id=1, source_target_pairs={{0,2},{1,3},{2,0},{3,1},{4,6},{5,7},{6,4},{7,5},{8,10},{9,11},{10,... | collective-permute-start | bytes 786440 | tf_op jit(solution)/shard_map/ppermute | solution.py:43
  66.3 23.9 %collective-permute-start.16 = (f32[128]{0:T(128)S(1)}, f32[128]{0:T(128)S(1)}, u32[]{:S(2)}, u32[]{:S(2)}) collective-permute-start(f32[128]{0:T(128)S(1)} %add.32), channel_id=1, source_target_pairs={{0,8},{4,12},{8,0},{12,4},{1,9},{5,13},{9,1},{13,5},{2,10},{6,14},... | collective-permute-start | bytes 1544 | tf_op jit(solution)/shard_map/ppermute | solution.py:43
  66.8 30.2 %collective-permute-start.18 = (bf16[4,128,768]{2,1,0:T(8,128)(2,1)S(1)}, bf16[4,128,768]{2,1,0:T(8,128)(2,1)S(1)}, u32[]{:S(2)}, u32[]{:S(2)}) collective-permute-start(bf16[4,128,768]{2,1,0:T(8,128)(2,1)S(1)} %get-tuple-element.116), channel_id=1, source_target_pairs={{0,8},{4,12},{8,0},{12,4},{1,9},{5,13},{9,1},{13,5},{2,10},{6,14},... | collective-permute-start | bytes 2359304 | tf_op jit(solution)/shard_map/ppermute | solution.py:43
  81.0 17.6 %collective-permute-start.19 = (bf16[8,128,512]{2,1,0:T(8,128)(2,1)S(1)}, bf16[8,128,512]{2,1,0:T(8,128)(2,1)S(1)}, u32[]{:S(2)}, u32[]{:S(2)}) collective-permute-start(bf16[8,128,512]{2,1,0:T(8,128)(2,1)S(1)} %get-tuple-element.117), channel_id=1, source_target_pairs={{0,4},{4,0},{8,12},{12,8},{1,5},{5,1},{9,13},{13,9},{2,6},{6,2},{1... | collective-permute-start | bytes 3145736 | tf_op jit(solution)/shard_map/ppermute | solution.py:43
  81.0 9.3 %collective-permute-start.11 = (bf16[2,128,128]{2,1,0:T(8,128)(2,1)S(1)}, bf16[2,128,128]{2,1,0:T(8,128)(2,1)S(1)}, u32[]{:S(2)}, u32[]{:S(2)}) collective-permute-start(bf16[2,128,128]{2,1,0:T(8,128)(2,1)S(1)} %add.31), channel_id=1, source_target_pairs={{0,2},{1,3},{2,0},{3,1},{4,6},{5,7},{6,4},{7,5},{8,10},{9,11},{10,... | collective-permute-start | bytes 196616 | tf_op jit(solution)/shard_map/ppermute | solution.py:43
  90.2 13.4 %collective-permute-start.21 = (bf16[1,128,512]{2,1,0:T(8,128)(2,1)S(1)}, bf16[1,128,512]{2,1,0:T(8,128)(2,1)S(1)}, u32[]{:S(2)}, u32[]{:S(2)}) collective-permute-start(bf16[1,128,512]{2,1,0:T(8,128)(2,1)S(1)} %get-tuple-element.110), channel_id=1, source_target_pairs={{0,2},{1,3},{2,0},{3,1},{4,6},{5,7},{6,4},{7,5},{8,10},{9,11},{10,... | collective-permute-start | bytes 393224 | tf_op jit(solution)/shard_map/ppermute | solution.py:43
  90.3 12.7 %collective-permute-start.20 = (f32[128]{0:T(128)S(1)}, f32[128]{0:T(128)S(1)}, u32[]{:S(2)}, u32[]{:S(2)}) collective-permute-start(f32[128]{0:T(128)S(1)} %add.33), channel_id=1, source_target_pairs={{0,1},{1,0},{2,3},{3,2},{4,5},{5,4},{6,7},{7,6},{8,9},{9,8},{10,11... | collective-permute-start | bytes 1544 | tf_op jit(solution)/shard_map/ppermute | solution.py:43
  92.8 16.5 %collective-permute-start.22 = (bf16[2,128,1024]{2,1,0:T(8,128)(2,1)S(1)}, bf16[2,128,1024]{2,1,0:T(8,128)(2,1)S(1)}, u32[]{:S(2)}, u32[]{:S(2)}) collective-permute-start(bf16[2,128,1024]{2,1,0:T(8,128)(2,1)S(1)} %get-tuple-element.123), channel_id=1, source_target_pairs={{0,1},{1,0},{2,3},{3,2},{4,5},{5,4},{6,7},{7,6},{8,9},{9,8},{10,11... | collective-permute-start | bytes 1572872 | tf_op jit(solution)/shard_map/ppermute | solution.py:43
  97.0 14.9 %collective-permute-start.23 = (bf16[4,128,512]{2,1,0:T(8,128)(2,1)S(1)}, bf16[4,128,512]{2,1,0:T(8,128)(2,1)S(1)}, u32[]{:S(2)}, u32[]{:S(2)}) collective-permute-start(bf16[4,128,512]{2,1,0:T(8,128)(2,1)S(1)} %get-tuple-element.124), channel_id=1, source_target_pairs={{0,8},{4,12},{8,0},{12,4},{1,9},{5,13},{9,1},{13,5},{2,10},{6,14},... | collective-permute-start | bytes 1572872 | tf_op jit(solution)/shard_map/ppermute | solution.py:43
  98.6 16.0 %collective-permute-start.24 = (bf16[8,128,256]{2,1,0:T(8,128)(2,1)S(1)}, bf16[8,128,256]{2,1,0:T(8,128)(2,1)S(1)}, u32[]{:S(2)}, u32[]{:S(2)}) collective-permute-start(bf16[8,128,256]{2,1,0:T(8,128)(2,1)S(1)} %get-tuple-element.125), channel_id=1, source_target_pairs={{0,4},{4,0},{8,12},{12,8},{1,5},{5,1},{9,13},{13,9},{2,6},{6,2},{1... | collective-permute-start | bytes 1572872 | tf_op jit(solution)/shard_map/ppermute | solution.py:43
  103.1 17.9 %collective-permute-start.26 = (bf16[1,128,512]{2,1,0:T(8,128)(2,1)S(1)}, bf16[1,128,512]{2,1,0:T(8,128)(2,1)S(1)}, u32[]{:S(2)}, u32[]{:S(2)}) collective-permute-start(bf16[1,128,512]{2,1,0:T(8,128)(2,1)S(1)} %get-tuple-element.118), channel_id=1, source_target_pairs={{0,8},{4,12},{8,0},{12,4},{1,9},{5,13},{9,1},{13,5},{2,10},{6,14},... | collective-permute-start | bytes 393224 | tf_op jit(solution)/shard_map/ppermute | solution.py:43
  103.6 18.9 %collective-permute-start.27 = (bf16[2,128,768]{2,1,0:T(8,128)(2,1)S(1)}, bf16[2,128,768]{2,1,0:T(8,128)(2,1)S(1)}, u32[]{:S(2)}, u32[]{:S(2)}) collective-permute-start(bf16[2,128,768]{2,1,0:T(8,128)(2,1)S(1)} %get-tuple-element.131), channel_id=1, source_target_pairs={{0,1},{1,0},{2,3},{3,2},{4,5},{5,4},{6,7},{7,6},{8,9},{9,8},{10,11... | collective-permute-start | bytes 1179656 | tf_op jit(solution)/shard_map/ppermute | solution.py:43
  109.3 16.6 %collective-permute-start.28 = (bf16[4,128,512]{2,1,0:T(8,128)(2,1)S(1)}, bf16[4,128,512]{2,1,0:T(8,128)(2,1)S(1)}, u32[]{:S(2)}, u32[]{:S(2)}) collective-permute-start(bf16[4,128,512]{2,1,0:T(8,128)(2,1)S(1)} %get-tuple-element.132), channel_id=1, source_target_pairs={{0,8},{4,12},{8,0},{12,4},{1,9},{5,13},{9,1},{13,5},{2,10},{6,14},... | collective-permute-start | bytes 1572872 | tf_op jit(solution)/shard_map/ppermute | solution.py:43
  111.9 7.1 %collective-permute-start.25 = (f32[128]{0:T(128)S(1)}, f32[128]{0:T(128)S(1)}, u32[]{:S(2)}, u32[]{:S(2)}) collective-permute-start(f32[128]{0:T(128)S(1)} %add.34), channel_id=1, source_target_pairs={{0,2},{1,3},{2,0},{3,1},{4,6},{5,7},{6,4},{7,5},{8,10},{9,11},{10,... | collective-permute-start | bytes 1544 | tf_op jit(solution)/shard_map/ppermute | solution.py:43
  119.0 15.4 %collective-permute-start.29 = (bf16[1,128,1024]{2,1,0:T(8,128)(2,1)S(1)}, bf16[1,128,1024]{2,1,0:T(8,128)(2,1)S(1)}, u32[]{:S(2)}, u32[]{:S(2)}) collective-permute-start(bf16[1,128,1024]{2,1,0:T(8,128)(2,1)S(1)} %get-tuple-element.136), channel_id=1, source_target_pairs={{0,2},{1,3},{2,0},{3,1},{4,6},{5,7},{6,4},{7,5},{8,10},{9,11},{10,... | collective-permute-start | bytes 786440 | tf_op jit(solution)/shard_map/ppermute | solution.py:43
  119.3 15.1 %collective-permute-start.30 = (bf16[2,128,512]{2,1,0:T(8,128)(2,1)S(1)}, bf16[2,128,512]{2,1,0:T(8,128)(2,1)S(1)}, u32[]{:S(2)}, u32[]{:S(2)}) collective-permute-start(bf16[2,128,512]{2,1,0:T(8,128)(2,1)S(1)} %get-tuple-element.137), channel_id=1, source_target_pairs={{0,1},{1,0},{2,3},{3,2},{4,5},{5,4},{6,7},{7,6},{8,9},{9,8},{10,11... | collective-permute-start | bytes 786440 | tf_op jit(solution)/shard_map/ppermute | solution.py:43
  121.0 13.4 %collective-permute-start.31 = (bf16[4,128,256]{2,1,0:T(8,128)(2,1)S(1)}, bf16[4,128,256]{2,1,0:T(8,128)(2,1)S(1)}, u32[]{:S(2)}, u32[]{:S(2)}) collective-permute-start(bf16[4,128,256]{2,1,0:T(8,128)(2,1)S(1)} %get-tuple-element.138), channel_id=1, source_target_pairs={{0,8},{4,12},{8,0},{12,4},{1,9},{5,13},{9,1},{13,5},{2,10},{6,14},... | collective-permute-start | bytes 786440 | tf_op jit(solution)/shard_map/ppermute | solution.py:43
  130.0 10.6 %collective-permute-start.32 = (bf16[1,128,768]{2,1,0:T(8,128)(2,1)S(1)}, bf16[1,128,768]{2,1,0:T(8,128)(2,1)S(1)}, u32[]{:S(2)}, u32[]{:S(2)}) collective-permute-start(bf16[1,128,768]{2,1,0:T(8,128)(2,1)S(1)} %get-tuple-element.141), channel_id=1, source_target_pairs={{0,2},{1,3},{2,0},{3,1},{4,6},{5,7},{6,4},{7,5},{8,10},{9,11},{10,... | collective-permute-start | bytes 589832 | tf_op jit(solution)/shard_map/ppermute | solution.py:43
  132.8 13.0 %copy-start.2 = (f32[2048]{0:T(1024)S(1)}, f32[2048]{0:T(1024)}, u32[]{:S(2)}) copy-start(f32[2048]{0:T(1024)} %param.12) | copy-start | bytes 24580
  132.8 11.6 %collective-permute-start.34 = (bf16[2,128,512]{2,1,0:T(8,128)(2,1)S(1)}, bf16[2,128,512]{2,1,0:T(8,128)(2,1)S(1)}, u32[]{:S(2)}, u32[]{:S(2)}) collective-permute-start(bf16[2,128,512]{2,1,0:T(8,128)(2,1)S(1)} %get-tuple-element.143), channel_id=1, source_target_pairs={{0,1},{1,0},{2,3},{3,2},{4,5},{5,4},{6,7},{7,6},{8,9},{9,8},{10,11... | collective-permute-start | bytes 786440 | tf_op jit(solution)/shard_map/ppermute | solution.py:43
  137.6 6.7 %collective-permute-start.33 = (bf16[1,128,512]{2,1,0:T(8,128)(2,1)S(1)}, bf16[1,128,512]{2,1,0:T(8,128)(2,1)S(1)}, u32[]{:S(2)}, u32[]{:S(2)}) collective-permute-start(bf16[1,128,512]{2,1,0:T(8,128)(2,1)S(1)} %get-tuple-element.142), channel_id=1, source_target_pairs={{0,2},{1,3},{2,0},{3,1},{4,6},{5,7},{6,4},{7,5},{8,10},{9,11},{10,... | collective-permute-start | bytes 393224 | tf_op jit(solution)/shard_map/ppermute | solution.py:43
  138.0 7.7 %collective-permute-start.35 = (bf16[2,128,256]{2,1,0:T(8,128)(2,1)S(1)}, bf16[2,128,256]{2,1,0:T(8,128)(2,1)S(1)}, u32[]{:S(2)}, u32[]{:S(2)}) collective-permute-start(bf16[2,128,256]{2,1,0:T(8,128)(2,1)S(1)} %get-tuple-element.144), channel_id=1, source_target_pairs={{0,1},{1,0},{2,3},{3,2},{4,5},{5,4},{6,7},{7,6},{8,9},{9,8},{10,11... | collective-permute-start | bytes 393224 | tf_op jit(solution)/shard_map/ppermute | solution.py:43
  145.8 8.1 %copy-start.3 = (bf16[2,128,128]{2,1,0:T(8,128)(2,1)S(1)}, bf16[2,128,128]{2,1,0:T(8,128)(2,1)}, u32[]{:S(2)}) copy-start(bf16[2,128,128]{2,1,0:T(8,128)(2,1)} %get-tuple-element.158) | copy-start | bytes 196612
  145.8 8.1 %copy-start.4 = (bf16[2,128,128]{2,1,0:T(8,128)(2,1)S(1)}, bf16[2,128,128]{2,1,0:T(8,128)(2,1)}, u32[]{:S(2)}) copy-start(bf16[2,128,128]{2,1,0:T(8,128)(2,1)} %get-tuple-element.159) | copy-start | bytes 196612
  151.0 8.7 %collective-permute-start.36 = (bf16[1,128,512]{2,1,0:T(8,128)(2,1)S(1)}, bf16[1,128,512]{2,1,0:T(8,128)(2,1)S(1)}, u32[]{:S(2)}, u32[]{:S(2)}) collective-permute-start(bf16[1,128,512]{2,1,0:T(8,128)(2,1)S(1)} %get-tuple-element.147), channel_id=1, source_target_pairs={{0,2},{1,3},{2,0},{3,1},{4,6},{5,7},{6,4},{7,5},{8,10},{9,11},{10,... | collective-permute-start | bytes 393224 | tf_op jit(solution)/shard_map/ppermute | solution.py:43
  153.0 6.7 %collective-permute-start.37 = (bf16[1,128,256]{2,1,0:T(8,128)(2,1)S(1)}, bf16[1,128,256]{2,1,0:T(8,128)(2,1)S(1)}, u32[]{:S(2)}, u32[]{:S(2)}) collective-permute-start(bf16[1,128,256]{2,1,0:T(8,128)(2,1)S(1)} %get-tuple-element.148), channel_id=1, source_target_pairs={{0,2},{1,3},{2,0},{3,1},{4,6},{5,7},{6,4},{7,5},{8,10},{9,11},{10,... | collective-permute-start | bytes 196616 | tf_op jit(solution)/shard_map/ppermute | solution.py:43

commit v3 on v2

--- a/solution.py
+++ b/solution.py
@@ -18,17 +18,17 @@
     ("dec", 512, 512, (0, 2, 4, 6, 8), True),
     ("dec", 1024, 1024, (1, 3, 5, 7, 9), False),
     ("enc", 1280, 768, (2, 4, 6, 8, 10), False),
-    ("enc", 768, 512, (3, 5, 7, 9, 10), False),
-    ("enc", 256, 512, (4, 6, 8, 10, 11), False),
-    ("enc", 0, 256, (5, 7, 9, 10, 11), False),
+    ("enc", 768, 512, (3, 5, 7, 9, 11), False),
+    ("enc", 256, 512, (4, 6, 8, 10, 12), False),
+    ("enc", 0, 256, (5, 7, 9, 10, 12), False),
 )
 SHORT_SCHEDULE = (
     ("dec", 0, 1, (0, 2, 4, 6, 8), False),
     ("enc", 0, 1, (1, 3, 5, 7, 9), False),
 )
 COST = 100
-AHEAD = 8
-TOGETHER = 2048
+AHEAD = 16
+TOGETHER = 4096
 FIRST_SQUARES = 4
 FIRST_TERMS = 3
 

time: 163 us -> 160 us (0.982)
  waiting for transfers between devices: 46.2 us -> 43.3 us
    ppermute x34, waiting for transfers between devices: 42 us -> 39.1 us  [swapped(): return lax.ppermute(value, axis, [(i, i ^ mask) for i in range(count)])]
    pallas_call x12 -> x13, Pallas kernels: 61.7 us -> 61.3 us  [run_step(): pl.pallas_call(functools.partial(step_kernel, {'kinds': kinds, 'jobs': jo...]
  transfers between devices with their start and end apart: 38 -> 38, of which waited for: 11 -> 11; matrix products, arithmetic and copies ran while one was open for 3% -> 3% of each run, Pallas kernels for 31% -> 35%
where the time goes in v3:
time: 160 us; the launch traced here: 159 us
  Pallas kernels  64.2 us (40%)
  starting transfers between devices  45.7 us (29%)
  waiting for transfers between devices  43.3 us (27%)
  other arithmetic  4.24 us (3%)
    pallas_call x13, Pallas kernels, run_step(): pl.pallas_call(functools.partial(step_kernel, {'kinds': kinds, 'jobs': jo...  61.3 us
    ppermute x34, waiting for transfers between devices, swapped(): return lax.ppermute(value, axis, [(i, i ^ mask) for i in range(count)])  39.1 us
    ppermute x34, starting transfers between devices, swapped(): return lax.ppermute(value, axis, [(i, i ^ mask) for i in range(count)])  37.4 us
    ppermute x2, starting transfers between devices, shifted(): lax.ppermute(value, axis, [(i, (i + steps) % count) for i in range(count)])  5.75 us
    ppermute x2, waiting for transfers between devices, shifted(): lax.ppermute(value, axis, [(i, (i + steps) % count) for i in range(count)])  4.21 us
  transfers between devices with their start and end apart: 38, of which 11 were waited for; matrix products, arithmetic and copies ran while one was open for 3% of the time, Pallas kernels for 35%

profile of v3, /device:TPU:0, one launch (start us, length us, event | category | flops | bytes accessed | tf_op | source)
XLA Modules:
  0.0 159.2 jit_solution(11407042580894686164)
XLA Ops:
  0.6 1.3 collective-permute-start
  2.7 3.0 %collective-permute-start.1 = (bf16[2,128,128]{2,1,0:T(8,128)(2,1)S(1)}, bf16[2,128,128]{2,1,0:T(8,128)(2,1)S(1)}, u32[]{:S(2)}, u32[]{:S(2)}) collective-permute-start(bf16[2,128,128]{2,1,0:T(8,128)(2,1)S(1)} %pad_maximum_fusion.1.refs_0_), channel_id=1, source_target_pairs={{0,16},{16,0},{1,17},{17,1},{2,18},{18,2},{3,19},{19,3},{4,20},{20... | collective-permute-start | bytes 196616 | tf_op jit(solution)/shard_map/ppermute | solution.py:38
  5.8 4.2 %collective-permute-done.1.refs_1_ = bf16[2,128,128]{2,1,0:T(8,128)(2,1)S(1)} collective-permute-done((bf16[2,128,128]{2,1,0:T(8,128)(2,1)S(1)}, bf16[2,128,128]{2,1,0:T(8,128)(2,1)S(1)}, u32[]{:S(2)}, u32[]{:S(2)}) %collective-permute-start.1) | collective-permute-done | bytes 65568 | tf_op jit(solution)/shard_map/ppermute | solution.py:38
  10.0 6.6 %shard_map.102 = (bf16[8,128,512]{2,1,0:T(8,128)(2,1)}, bf16[8,128,512]{2,1,0:T(8,128)(2,1)S(1)}) custom-call(bf16[128,512]{1,0:T(8,128)(2,1)S(1)} %broadcast_select_fusion.1.refs_0_, bf16[32768,512]{1,0:T(8,128)(2,1)} %refs_1_.22), custom_call_target="tpu_custom_call" | custom-call | flops 107374182400 | bytes 1048576000 | tf_op jit(solution)/shard_map/pallas_call | solution.py:267
  16.7 2.9 %shard_map.103 = (bf16[128,512]{1,0:T(8,128)(2,1)S(1)}, bf16[128,512]{1,0:T(8,128)(2,1)}, f32[2,128,128]{2,1,0:T(8,128)S(1)}, f32[2,128,128]{2,1,0:T(8,128)}) custom-call(bf16[128,512]{1,0:T(8,128)(2,1)S(1)} %copy-done.1, bf16[128,512]{1,0:T(8,128)(2,1)S(1)} %copy-done, bf16[2,128,128]{2,1,0:T(8,128)(2,1)S(1)} %pad_maximum_fusion.1.refs_0_, ...), custom_call_target="tpu_custom_call" | custom-call | tf_op jit(solution)/shard_map/pallas_call | solution.py:333
  19.6 1.3 collective-permute-start.2
  20.9 2.7 %collective-permute-start.7 = (f32[2,128,128]{2,1,0:T(8,128)}, f32[2,128,128]{2,1,0:T(8,128)}, u32[]{:S(2)}, u32[]{:S(2)}) collective-permute-start(f32[2,128,128]{2,1,0:T(8,128)} %get-tuple-element.98), channel_id=1, source_target_pairs={{0,16},{16,0},{1,17},{17,1},{2,18},{18,2},{3,19},{19,3},{4,20},{20... | collective-permute-start | bytes 393224 | tf_op jit(solution)/shard_map/ppermute | solution.py:38
  23.6 6.7 %shard_map.104 = (bf16[4,128,512]{2,1,0:T(8,128)(2,1)S(1)}, bf16[8,128,1024]{2,1,0:T(8,128)(2,1)S(1)}) custom-call(bf16[128,512]{1,0:T(8,128)(2,1)S(1)} %broadcast_select_fusion.1.refs_0_, bf16[32768,512]{1,0:T(8,128)(2,1)} %refs_1_.22, bf16[8,128,512]{2,1,0:T(8,128)(2,1)S(1)} %collective-permute-done.3.refs_2_.refs_4_), custom_call_target="tpu_custom_call" | custom-call | flops 134217728000 | bytes 1363148800 | tf_op jit(solution)/shard_map/pallas_call | solution.py:267
  30.4 2.4 %collective-permute-start.5 = (bf16[4,128,512]{2,1,0:T(8,128)(2,1)S(1)}, bf16[4,128,512]{2,1,0:T(8,128)(2,1)S(1)}, u32[]{:S(2)}, u32[]{:S(2)}) collective-permute-start(bf16[4,128,512]{2,1,0:T(8,128)(2,1)S(1)} %get-tuple-element.86), channel_id=1, source_target_pairs={{0,8},{4,12},{8,0},{12,4},{1,9},{5,13},{9,1},{13,5},{2,10},{6,14},... | collective-permute-start | bytes 1572872 | tf_op jit(solution)/shard_map/ppermute | solution.py:43
  33.6 5.7 %shard_map.105 = (bf16[4,128,512]{2,1,0:T(8,128)(2,1)S(1)}, bf16[8,128,768]{2,1,0:T(8,128)(2,1)S(1)}) custom-call(bf16[128,512]{1,0:T(8,128)(2,1)S(1)} %broadcast_select_fusion.1.refs_0_, bf16[32768,512]{1,0:T(8,128)(2,1)} %refs_1_.22, bf16[128,512]{1,0:T(8,128)(2,1)S(1)} %get-tuple-element.147.refs_2_.refs_0_, bf16[512,32768]{1,0:T(8,128)(2,1)} %refs_1_.25, ...), custom_call_target="tpu_custom_call" | custom-call | flops 107374182400 | bytes 1101004800 | tf_op jit(solution)/shard_map/pallas_call | solution.py:267
  39.3 1.6 %collective-permute-start.8 = (bf16[4,128,512]{2,1,0:T(8,128)(2,1)S(1)}, bf16[4,128,512]{2,1,0:T(8,128)(2,1)S(1)}, u32[]{:S(2)}, u32[]{:S(2)}) collective-permute-start(bf16[4,128,512]{2,1,0:T(8,128)(2,1)S(1)} %get-tuple-element.91), channel_id=1, source_target_pairs={{0,1},{1,0},{2,3},{3,2},{4,5},{5,4},{6,7},{7,6},{8,9},{9,8},{10,11... | collective-permute-start | bytes 1572872 | tf_op jit(solution)/shard_map/ppermute | solution.py:43
  41.0 4.4 %collective-permute-done.5.refs_5_ = bf16[4,128,512]{2,1,0:T(8,128)(2,1)S(1)} collective-permute-done((bf16[4,128,512]{2,1,0:T(8,128)(2,1)S(1)}, bf16[4,128,512]{2,1,0:T(8,128)(2,1)S(1)}, u32[]{:S(2)}, u32[]{:S(2)}) %collective-permute-start.5) | collective-permute-done | bytes 524320 | tf_op jit(solution)/shard_map/ppermute | solution.py:43
  45.4 6.4 %shard_map.106 = (bf16[2,128,512]{2,1,0:T(8,128)(2,1)S(1)}, bf16[4,128,1024]{2,1,0:T(8,128)(2,1)S(1)}, bf16[8,128,512]{2,1,0:T(8,128)(2,1)S(1)}) custom-call(bf16[128,512]{1,0:T(8,128)(2,1)S(1)} %broadcast_select_fusion.1.refs_0_, bf16[32768,512]{1,0:T(8,128)(2,1)} %refs_1_.22, bf16[128,512]{1,0:T(8,128)(2,1)S(1)} %get-tuple-element.147.refs_2_.refs_0_, ...), custom_call_target="tpu_custom_call" | custom-call | flops 120795955200 | bytes 1336934400 | tf_op jit(solution)/shard_map/pallas_call | solution.py:267
  51.8 0.9 add.30
  52.7 1.9 %collective-permute-start.10 = (f32[2,128,128]{2,1,0:T(8,128)S(1)}, f32[2,128,128]{2,1,0:T(8,128)S(1)}, u32[]{:S(2)}, u32[]{:S(2)}) collective-permute-start(f32[2,128,128]{2,1,0:T(8,128)S(1)} %add.30), channel_id=1, source_target_pairs={{0,1},{1,0},{2,3},{3,2},{4,5},{5,4},{6,7},{7,6},{8,9},{9,8},{10,11... | collective-permute-start | bytes 393224 | tf_op jit(solution)/shard_map/ppermute | solution.py:43
  54.8 1.7 %collective-permute-start.14 = (bf16[4,128,1024]{2,1,0:T(8,128)(2,1)S(1)}, bf16[4,128,1024]{2,1,0:T(8,128)(2,1)S(1)}, u32[]{:S(2)}, u32[]{:S(2)}) collective-permute-start(bf16[4,128,1024]{2,1,0:T(8,128)(2,1)S(1)} %get-tuple-element.108), channel_id=1, source_target_pairs={{0,8},{4,12},{8,0},{12,4},{1,9},{5,13},{9,1},{13,5},{2,10},{6,14},... | collective-permute-start | bytes 3145736 | tf_op jit(solution)/shard_map/ppermute | solution.py:43
  56.6 5.8 %shard_map.107 = (bf16[2,128,512]{2,1,0:T(8,128)(2,1)S(1)}, bf16[4,128,768]{2,1,0:T(8,128)(2,1)S(1)}, bf16[8,128,512]{2,1,0:T(8,128)(2,1)S(1)}) custom-call(bf16[128,512]{1,0:T(8,128)(2,1)S(1)} %broadcast_select_fusion.1.refs_0_, bf16[32768,512]{1,0:T(8,128)(2,1)} %refs_1_.22, bf16[128,512]{1,0:T(8,128)(2,1)S(1)} %get-tuple-element.147.refs_2_.refs_0_, ...), custom_call_target="tpu_custom_call" | custom-call | flops 107374182400 | bytes 1179648000 | tf_op jit(solution)/shard_map/pallas_call | solution.py:267
  62.4 2.6 %collective-permute-start.17 = (bf16[2,128,512]{2,1,0:T(8,128)(2,1)S(1)}, bf16[2,128,512]{2,1,0:T(8,128)(2,1)S(1)}, u32[]{:S(2)}, u32[]{:S(2)}) collective-permute-start(bf16[2,128,512]{2,1,0:T(8,128)(2,1)S(1)} %get-tuple-element.102), channel_id=1, source_target_pairs={{0,2},{1,3},{2,0},{3,1},{4,6},{5,7},{6,4},{7,5},{8,10},{9,11},{10,... | collective-permute-start | bytes 786440 | tf_op jit(solution)/shard_map/ppermute | solution.py:43
  66.3 1.6 collective-permute-start.18
  67.8 13.0 %collective-permute-done.14.refs_8_.refs_9_.refs_5_ = bf16[4,128,1024]{2,1,0:T(8,128)(2,1)S(1)} collective-permute-done((bf16[4,128,1024]{2,1,0:T(8,128)(2,1)S(1)}, bf16[4,128,1024]{2,1,0:T(8,128)(2,1)S(1)}, u32[]{:S(2)}, u32[]{:S(2)}) %collective-permute-start.14) | collective-permute-done | bytes 1048608 | tf_op jit(solution)/shard_map/ppermute | solution.py:43
  80.9 2.8 %collective-permute-start.11 = (bf16[2,128,128]{2,1,0:T(8,128)(2,1)S(1)}, bf16[2,128,128]{2,1,0:T(8,128)(2,1)S(1)}, u32[]{:S(2)}, u32[]{:S(2)}) collective-permute-start(bf16[2,128,128]{2,1,0:T(8,128)(2,1)S(1)} %add.31), channel_id=1, source_target_pairs={{0,2},{1,3},{2,0},{3,1},{4,6},{5,7},{6,4},{7,5},{8,10},{9,11},{10,... | collective-permute-start | bytes 196616 | tf_op jit(solution)/shard_map/ppermute | solution.py:43
  83.7 6.3 %shard_map.108 = (bf16[1,128,512]{2,1,0:T(8,128)(2,1)S(1)}, bf16[2,128,1024]{2,1,0:T(8,128)(2,1)S(1)}, bf16[4,128,512]{2,1,0:T(8,128)(2,1)S(1)}, bf16[8,128,256]{2,1,0:T(8,128)(2,1)S(1)}) custom-call(bf16[128,512]{1,0:T(8,128)(2,1)S(1)} %broadcast_select_fusion.1.refs_0_, bf16[32768,512]{1,0:T(8,128)(2,1)} %refs_1_.22, ...), custom_call_target="tpu_custom_call" | custom-call | flops 87241523200 | bytes 1048576000 | tf_op jit(solution)/shard_map/pallas_call | solution.py:267
  90.2 1.8 %collective-permute-start.20 = (f32[128]{0:T(128)S(1)}, f32[128]{0:T(128)S(1)}, u32[]{:S(2)}, u32[]{:S(2)}) collective-permute-start(f32[128]{0:T(128)S(1)} %add.33), channel_id=1, source_target_pairs={{0,1},{1,0},{2,3},{3,2},{4,5},{5,4},{6,7},{7,6},{8,9},{9,8},{10,11... | collective-permute-start | bytes 1544 | tf_op jit(solution)/shard_map/ppermute | solution.py:43
  92.9 4.0 %collective-permute-done.18.refs_8_.refs_9_.refs_3_ = bf16[4,128,768]{2,1,0:T(8,128)(2,1)S(1)} collective-permute-done((bf16[4,128,768]{2,1,0:T(8,128)(2,1)S(1)}, bf16[4,128,768]{2,1,0:T(8,128)(2,1)S(1)}, u32[]{:S(2)}, u32[]{:S(2)}) %collective-permute-start.18) | collective-permute-done | bytes 786464 | tf_op jit(solution)/shard_map/ppermute | solution.py:43
  96.8 1.6 collective-permute-start.23
  98.4 4.5 %shard_map.109 = (bf16[1,128,512]{2,1,0:T(8,128)(2,1)S(1)}, bf16[2,128,768]{2,1,0:T(8,128)(2,1)S(1)}, bf16[4,128,512]{2,1,0:T(8,128)(2,1)S(1)}) custom-call(bf16[128,512]{1,0:T(8,128)(2,1)S(1)} %broadcast_select_fusion.1.refs_0_, bf16[32768,512]{1,0:T(8,128)(2,1)} %refs_1_.22, bf16[128,512]{1,0:T(8,128)(2,1)S(1)} %get-tuple-element.147.refs_2_.refs_0_, ...), custom_call_target="tpu_custom_call" | custom-call | flops 53687091200 | bytes 694681600 | tf_op jit(solution)/shard_map/pallas_call | solution.py:267
  103.4 1.7 %collective-permute-start.27 = (bf16[2,128,768]{2,1,0:T(8,128)(2,1)S(1)}, bf16[2,128,768]{2,1,0:T(8,128)(2,1)S(1)}, u32[]{:S(2)}, u32[]{:S(2)}) collective-permute-start(bf16[2,128,768]{2,1,0:T(8,128)(2,1)S(1)} %get-tuple-element.131), channel_id=1, source_target_pairs={{0,1},{1,0},{2,3},{3,2},{4,5},{5,4},{6,7},{7,6},{8,9},{9,8},{10,11... | collective-permute-start | bytes 1179656 | tf_op jit(solution)/shard_map/ppermute | solution.py:43
  105.1 4.1 %collective-permute-done.22.refs_10_.refs_6_ = bf16[2,128,1024]{2,1,0:T(8,128)(2,1)S(1)} collective-permute-done((bf16[2,128,1024]{2,1,0:T(8,128)(2,1)S(1)}, bf16[2,128,1024]{2,1,0:T(8,128)(2,1)S(1)}, u32[]{:S(2)}, u32[]{:S(2)}) %collective-permute-start.22) | collective-permute-done | bytes 524320 | tf_op jit(solution)/shard_map/ppermute | solution.py:43
  109.2 1.5 collective-permute-start.28
  110.7 1.0 collective-permute-done.23.refs_12_.refs_9_.refs_3_
  111.7 2.7 %collective-permute-start.25 = (f32[128]{0:T(128)S(1)}, f32[128]{0:T(128)S(1)}, u32[]{:S(2)}, u32[]{:S(2)}) collective-permute-start(f32[128]{0:T(128)S(1)} %add.34), channel_id=1, source_target_pairs={{0,2},{1,3},{2,0},{3,1},{4,6},{5,7},{6,4},{7,5},{8,10},{9,11},{10,... | collective-permute-start | bytes 1544 | tf_op jit(solution)/shard_map/ppermute | solution.py:43
  114.4 4.4 %shard_map.110 = (f32[1,128,512]{2,1,0:T(8,128)S(1)}, bf16[1,128,1024]{2,1,0:T(8,128)(2,1)S(1)}, bf16[2,128,512]{2,1,0:T(8,128)(2,1)S(1)}, bf16[4,128,256]{2,1,0:T(8,128)(2,1)S(1)}) custom-call(bf16[128,512]{1,0:T(8,128)(2,1)S(1)} %broadcast_select_fusion.1.refs_0_, bf16[32768,512]{1,0:T(8,128)(2,1)} %refs_1_.22, ...), custom_call_target="tpu_custom_call" | custom-call | flops 46976204800 | bytes 668467200 | tf_op jit(solution)/shard_map/pallas_call | solution.py:267
  119.2 1.7 %collective-permute-start.30 = (bf16[2,128,512]{2,1,0:T(8,128)(2,1)S(1)}, bf16[2,128,512]{2,1,0:T(8,128)(2,1)S(1)}, u32[]{:S(2)}, u32[]{:S(2)}) collective-permute-start(bf16[2,128,512]{2,1,0:T(8,128)(2,1)S(1)} %get-tuple-element.137), channel_id=1, source_target_pairs={{0,1},{1,0},{2,3},{3,2},{4,5},{5,4},{6,7},{7,6},{8,9},{9,8},{10,11... | collective-permute-start | bytes 786440 | tf_op jit(solution)/shard_map/ppermute | solution.py:43
  120.8 1.5 collective-permute-start.31
  122.3 3.4 %collective-permute-done.28.refs_12_.refs_7_.refs_3_ = bf16[4,128,512]{2,1,0:T(8,128)(2,1)S(1)} collective-permute-done((bf16[4,128,512]{2,1,0:T(8,128)(2,1)S(1)}, bf16[4,128,512]{2,1,0:T(8,128)(2,1)S(1)}, u32[]{:S(2)}, u32[]{:S(2)}) %collective-permute-start.28) | collective-permute-done | bytes 524320 | tf_op jit(solution)/shard_map/ppermute | solution.py:43
  125.7 4.1 %shard_map.111 = (f32[1,128,512]{2,1,0:T(8,128)S(1)}, bf16[1,128,768]{2,1,0:T(8,128)(2,1)S(1)}, bf16[2,128,512]{2,1,0:T(8,128)(2,1)S(1)}) custom-call(bf16[128,512]{1,0:T(8,128)(2,1)S(1)} %broadcast_select_fusion.1.refs_0_, bf16[32768,512]{1,0:T(8,128)(2,1)} %refs_1_.22, bf16[128,512]{1,0:T(8,128)(2,1)S(1)} %get-tuple-element.147.refs_2_.refs_0_, ...), custom_call_target="tpu_custom_call" | custom-call | flops 30198988800 | bytes 458752000 | tf_op jit(solution)/shard_map/pallas_call | solution.py:267
  129.9 2.7 %collective-permute-start.32 = (bf16[1,128,768]{2,1,0:T(8,128)(2,1)S(1)}, bf16[1,128,768]{2,1,0:T(8,128)(2,1)S(1)}, u32[]{:S(2)}, u32[]{:S(2)}) collective-permute-start(bf16[1,128,768]{2,1,0:T(8,128)(2,1)S(1)} %get-tuple-element.141), channel_id=1, source_target_pairs={{0,2},{1,3},{2,0},{3,1},{4,6},{5,7},{6,4},{7,5},{8,10},{9,11},{10,... | collective-permute-start | bytes 589832 | tf_op jit(solution)/shard_map/ppermute | solution.py:43
  132.6 1.6 collective-permute-start.33
  134.2 3.2 %shard_map.112 = (f32[1,128,1024]{2,1,0:T(8,128)S(1)}, bf16[1,128,512]{2,1,0:T(8,128)(2,1)S(1)}, bf16[2,128,256]{2,1,0:T(8,128)(2,1)S(1)}) custom-call(bf16[128,512]{1,0:T(8,128)(2,1)S(1)} %broadcast_select_fusion.1.refs_0_, bf16[32768,512]{1,0:T(8,128)(2,1)} %refs_1_.22, bf16[128,512]{1,0:T(8,128)(2,1)S(1)} %get-tuple-element.147.refs_2_.refs_0_, ...), custom_call_target="tpu_custom_call" | custom-call | flops 26843545600 | bytes 432537600 | tf_op jit(solution)/shard_map/pallas_call | solution.py:267
  138.9 3.8 %collective-permute-done.33.refs_8_.refs_4_ = bf16[2,128,512]{2,1,0:T(8,128)(2,1)S(1)} collective-permute-done((bf16[2,128,512]{2,1,0:T(8,128)(2,1)S(1)}, bf16[2,128,512]{2,1,0:T(8,128)(2,1)S(1)}, u32[]{:S(2)}, u32[]{:S(2)}) %collective-permute-start.33) | collective-permute-done | bytes 262176 | tf_op jit(solution)/shard_map/ppermute | solution.py:43
  142.7 2.8 %collective-permute-done.34.refs_11_.refs_8_ = bf16[2,128,256]{2,1,0:T(8,128)(2,1)S(1)} collective-permute-done((bf16[2,128,256]{2,1,0:T(8,128)(2,1)S(1)}, bf16[2,128,256]{2,1,0:T(8,128)(2,1)S(1)}, u32[]{:S(2)}, u32[]{:S(2)}) %collective-permute-start.34) | collective-permute-done | bytes 131104 | tf_op jit(solution)/shard_map/ppermute | solution.py:43
  145.6 3.5 %shard_map.113 = (f32[1,1,768]{2,1,0:T(1,128)S(1)}, bf16[1,128,512]{2,1,0:T(8,128)(2,1)S(1)}, bf16[1,128,256]{2,1,0:T(8,128)(2,1)S(1)}) custom-call(bf16[128,512]{1,0:T(8,128)(2,1)S(1)} %get-tuple-element.147.refs_2_.refs_0_, bf16[512,32768]{1,0:T(8,128)(2,1)} %refs_1_.25, bf16[8,128,768]{2,1,0:T(8,128)(2,1)S(1)} %collective-permute-done.9.refs_6_.refs_7_.refs_8_.refs_2_, ...), custom_call_target="tpu_custom_call" | custom-call | flops 20132659200 | bytes 334233600 | tf_op jit(solution)/shard_map/pallas_call | solution.py:267
  149.1 0.8 collective-permute-start.37
  149.9 2.2 %collective-permute-start.36 = (bf16[1,128,512]{2,1,0:T(8,128)(2,1)S(1)}, bf16[1,128,512]{2,1,0:T(8,128)(2,1)S(1)}, u32[]{:S(2)}, u32[]{:S(2)}) collective-permute-start(bf16[1,128,512]{2,1,0:T(8,128)(2,1)S(1)} %get-tuple-element.148), channel_id=1, source_target_pairs={{0,2},{1,3},{2,0},{3,1},{4,6},{5,7},{6,4},{7,5},{8,10},{9,11},{10,... | collective-permute-start | bytes 393224 | tf_op jit(solution)/shard_map/ppermute | solution.py:43
  152.1 1.6 %shard_map.114 = f32[1,1,512]{2,1,0:T(1,128)S(1)} custom-call(bf16[128,512]{1,0:T(8,128)(2,1)S(1)} %get-tuple-element.147.refs_2_.refs_0_, bf16[512,32768]{1,0:T(8,128)(2,1)} %refs_1_.25, bf16[8,128,512]{2,1,0:T(8,128)(2,1)S(1)} %collective-permute-done.15.refs_9_.refs_11_.refs_8_.refs_2_, ...), custom_call_target="tpu_custom_call" | custom-call | flops 6710886400 | bytes 117964800 | tf_op jit(solution)/shard_map/pallas_call | solution.py:267
  153.7 1.1 collective-permute-done.37.refs_9_
  154.8 1.4 collective-permute-done.36.refs_5_
  156.2 2.4 %shard_map.115 = (f32[1,1,512]{2,1,0:T(1,128)S(1)}, f32[1,1,256]{2,1,0:T(1,128)S(1)}) custom-call(bf16[128,512]{1,0:T(8,128)(2,1)S(1)} %get-tuple-element.147.refs_2_.refs_0_, bf16[512,32768]{1,0:T(8,128)(2,1)} %refs_1_.25, bf16[8,128,512]{2,1,0:T(8,128)(2,1)S(1)} %collective-permute-done.19.refs_9_.refs_11_.refs_6_.refs_2_, ...), custom_call_target="tpu_custom_call" | custom-call | flops 10066329600 | bytes 176947200 | tf_op jit(solution)/shard_map/pallas_call | solution.py:267
  (66 shorter events, 7.3 us)
Async XLA Ops:
  0.6 9.4 %collective-permute-start = (bf16[128,512]{1,0:T(8,128)(2,1)}, bf16[128,512]{1,0:T(8,128)(2,1)S(1)}, u32[]{:S(2)}, u32[]{:S(2)}) collective-permute-start(bf16[128,512]{1,0:T(8,128)(2,1)} %out_grad.1), channel_id=1, source_target_pairs={{16,0},{17,1},{18,2},{19,3},{20,4},{21,5},{22,6},{23,7},{24,8},{25... | collective-permute-start | bytes 393224 | tf_op jit(solution)/shard_map/ppermute | solution.py:54
  2.7 7.2 %collective-permute-start.1 = (bf16[2,128,128]{2,1,0:T(8,128)(2,1)S(1)}, bf16[2,128,128]{2,1,0:T(8,128)(2,1)S(1)}, u32[]{:S(2)}, u32[]{:S(2)}) collective-permute-start(bf16[2,128,128]{2,1,0:T(8,128)(2,1)S(1)} %pad_maximum_fusion.1.refs_0_), channel_id=1, source_target_pairs={{0,16},{16,0},{1,17},{17,1},{2,18},{18,2},{3,19},{19,3},{4,20},{20... | collective-permute-start | bytes 196616 | tf_op jit(solution)/shard_map/ppermute | solution.py:38
  10.0 6.7 %copy-start = (bf16[128,512]{1,0:T(8,128)(2,1)S(1)}, bf16[128,512]{1,0:T(8,128)(2,1)}, u32[]{:S(2)}) copy-start(bf16[128,512]{1,0:T(8,128)(2,1)} %out_grad.1) | copy-start | bytes 393220
  10.0 6.7 %copy-start.1 = (bf16[128,512]{1,0:T(8,128)(2,1)S(1)}, bf16[128,512]{1,0:T(8,128)(2,1)}, u32[]{:S(2)}) copy-start(bf16[128,512]{1,0:T(8,128)(2,1)} %queries) | copy-start | bytes 393220
  16.6 7.0 %collective-permute-start.3 = (bf16[8,128,512]{2,1,0:T(8,128)(2,1)}, bf16[8,128,512]{2,1,0:T(8,128)(2,1)S(1)}, u32[]{:S(2)}, u32[]{:S(2)}) collective-permute-start(bf16[8,128,512]{2,1,0:T(8,128)(2,1)} %get-tuple-element.79), channel_id=1, source_target_pairs={{0,4},{4,0},{8,12},{12,8},{1,5},{5,1},{9,13},{13,9},{2,6},{6,2},{1... | collective-permute-start | bytes 3145736 | tf_op jit(solution)/shard_map/ppermute | solution.py:43
  19.6 13.1 %collective-permute-start.2 = (bf16[128,512]{1,0:T(8,128)(2,1)S(1)}, bf16[128,512]{1,0:T(8,128)(2,1)S(1)}, u32[]{:S(2)}, u32[]{:S(2)}) collective-permute-start(bf16[128,512]{1,0:T(8,128)(2,1)S(1)} %get-tuple-element.88), channel_id=1, source_target_pairs={{16,0},{17,1},{18,2},{19,3},{20,4},{21,5},{22,6},{23,7},{24,8},{25... | collective-permute-start | bytes 393224 | tf_op jit(solution)/shard_map/ppermute | solution.py:54
  20.9 30.9 %collective-permute-start.7 = (f32[2,128,128]{2,1,0:T(8,128)}, f32[2,128,128]{2,1,0:T(8,128)}, u32[]{:S(2)}, u32[]{:S(2)}) collective-permute-start(f32[2,128,128]{2,1,0:T(8,128)} %get-tuple-element.98), channel_id=1, source_target_pairs={{0,16},{16,0},{1,17},{17,1},{2,18},{18,2},{3,19},{19,3},{4,20},{20... | collective-permute-start | bytes 393224 | tf_op jit(solution)/shard_map/ppermute | solution.py:38
  23.6 10.0 %collective-permute-start.4 = (bf16[8,128,512]{2,1,0:T(8,128)(2,1)S(1)}, bf16[8,128,512]{2,1,0:T(8,128)(2,1)S(1)}, u32[]{:S(2)}, u32[]{:S(2)}) collective-permute-start(bf16[8,128,512]{2,1,0:T(8,128)(2,1)S(1)} %get-tuple-element.90), channel_id=1, source_target_pairs={{0,4},{4,0},{8,12},{12,8},{1,5},{5,1},{9,13},{13,9},{2,6},{6,2},{1... | collective-permute-start | bytes 3145736 | tf_op jit(solution)/shard_map/ppermute | solution.py:43
  30.4 15.0 %collective-permute-start.5 = (bf16[4,128,512]{2,1,0:T(8,128)(2,1)S(1)}, bf16[4,128,512]{2,1,0:T(8,128)(2,1)S(1)}, u32[]{:S(2)}, u32[]{:S(2)}) collective-permute-start(bf16[4,128,512]{2,1,0:T(8,128)(2,1)S(1)} %get-tuple-element.86), channel_id=1, source_target_pairs={{0,8},{4,12},{8,0},{12,4},{1,9},{5,13},{9,1},{13,5},{2,10},{6,14},... | collective-permute-start | bytes 1572872 | tf_op jit(solution)/shard_map/ppermute | solution.py:43
  33.4 11.9 %collective-permute-start.6 = (bf16[8,128,1024]{2,1,0:T(8,128)(2,1)S(1)}, bf16[8,128,1024]{2,1,0:T(8,128)(2,1)S(1)}, u32[]{:S(2)}, u32[]{:S(2)}) collective-permute-start(bf16[8,128,1024]{2,1,0:T(8,128)(2,1)S(1)} %get-tuple-element.94), channel_id=1, source_target_pairs={{0,4},{4,0},{8,12},{12,8},{1,5},{5,1},{9,13},{13,9},{2,6},{6,2},{1... | collective-permute-start | bytes 6291464 | tf_op jit(solution)/shard_map/ppermute | solution.py:43
  39.3 15.5 %collective-permute-start.8 = (bf16[4,128,512]{2,1,0:T(8,128)(2,1)S(1)}, bf16[4,128,512]{2,1,0:T(8,128)(2,1)S(1)}, u32[]{:S(2)}, u32[]{:S(2)}) collective-permute-start(bf16[4,128,512]{2,1,0:T(8,128)(2,1)S(1)} %get-tuple-element.91), channel_id=1, source_target_pairs={{0,1},{1,0},{2,3},{3,2},{4,5},{5,4},{6,7},{7,6},{8,9},{9,8},{10,11... | collective-permute-start | bytes 1572872 | tf_op jit(solution)/shard_map/ppermute | solution.py:43
  41.0 21.4 %collective-permute-start.12 = (f32[128]{0:T(128)}, f32[128]{0:T(128)}, u32[]{:S(2)}, u32[]{:S(2)}) collective-permute-start(f32[128]{0:T(128)} %get-tuple-element.154), channel_id=1, source_target_pairs={{0,4},{4,0},{8,12},{12,8},{1,5},{5,1},{9,13},{13,9},{2,6},{6,2},{1... | collective-permute-start | bytes 1544 | tf_op jit(solution)/shard_map/ppermute | solution.py:43
  45.3 11.2 %collective-permute-start.9 = (bf16[8,128,768]{2,1,0:T(8,128)(2,1)S(1)}, bf16[8,128,768]{2,1,0:T(8,128)(2,1)S(1)}, u32[]{:S(2)}, u32[]{:S(2)}) collective-permute-start(bf16[8,128,768]{2,1,0:T(8,128)(2,1)S(1)} %get-tuple-element.101), channel_id=1, source_target_pairs={{0,4},{4,0},{8,12},{12,8},{1,5},{5,1},{9,13},{13,9},{2,6},{6,2},{1... | collective-permute-start | bytes 4718600 | tf_op jit(solution)/shard_map/ppermute | solution.py:43
  52.7 13.0 %collective-permute-start.10 = (f32[2,128,128]{2,1,0:T(8,128)S(1)}, f32[2,128,128]{2,1,0:T(8,128)S(1)}, u32[]{:S(2)}, u32[]{:S(2)}) collective-permute-start(f32[2,128,128]{2,1,0:T(8,128)S(1)} %add.30), channel_id=1, source_target_pairs={{0,1},{1,0},{2,3},{3,2},{4,5},{5,4},{6,7},{7,6},{8,9},{9,8},{10,11... | collective-permute-start | bytes 393224 | tf_op jit(solution)/shard_map/ppermute | solution.py:43
  54.6 11.7 %collective-permute-start.13 = (bf16[2,128,512]{2,1,0:T(8,128)(2,1)S(1)}, bf16[2,128,512]{2,1,0:T(8,128)(2,1)S(1)}, u32[]{:S(2)}, u32[]{:S(2)}) collective-permute-start(bf16[2,128,512]{2,1,0:T(8,128)(2,1)S(1)} %get-tuple-element.95), channel_id=1, source_target_pairs={{0,1},{1,0},{2,3},{3,2},{4,5},{5,4},{6,7},{7,6},{8,9},{9,8},{10,11... | collective-permute-start | bytes 786440 | tf_op jit(solution)/shard_map/ppermute | solution.py:43
  54.8 26.0 %collective-permute-start.14 = (bf16[4,128,1024]{2,1,0:T(8,128)(2,1)S(1)}, bf16[4,128,1024]{2,1,0:T(8,128)(2,1)S(1)}, u32[]{:S(2)}, u32[]{:S(2)}) collective-permute-start(bf16[4,128,1024]{2,1,0:T(8,128)(2,1)S(1)} %get-tuple-element.108), channel_id=1, source_target_pairs={{0,8},{4,12},{8,0},{12,4},{1,9},{5,13},{9,1},{13,5},{2,10},{6,14},... | collective-permute-start | bytes 3145736 | tf_op jit(solution)/shard_map/ppermute | solution.py:43
  56.6 24.3 %collective-permute-start.15 = (bf16[8,128,512]{2,1,0:T(8,128)(2,1)S(1)}, bf16[8,128,512]{2,1,0:T(8,128)(2,1)S(1)}, u32[]{:S(2)}, u32[]{:S(2)}) collective-permute-start(bf16[8,128,512]{2,1,0:T(8,128)(2,1)S(1)} %get-tuple-element.109), channel_id=1, source_target_pairs={{0,4},{4,0},{8,12},{12,8},{1,5},{5,1},{9,13},{13,9},{2,6},{6,2},{1... | collective-permute-start | bytes 3145736 | tf_op jit(solution)/shard_map/ppermute | solution.py:43
  62.4 30.2 %collective-permute-start.17 = (bf16[2,128,512]{2,1,0:T(8,128)(2,1)S(1)}, bf16[2,128,512]{2,1,0:T(8,128)(2,1)S(1)}, u32[]{:S(2)}, u32[]{:S(2)}) collective-permute-start(bf16[2,128,512]{2,1,0:T(8,128)(2,1)S(1)} %get-tuple-element.102), channel_id=1, source_target_pairs={{0,2},{1,3},{2,0},{3,1},{4,6},{5,7},{6,4},{7,5},{8,10},{9,11},{10,... | collective-permute-start | bytes 786440 | tf_op jit(solution)/shard_map/ppermute | solution.py:43
  65.7 24.3 %collective-permute-start.16 = (f32[128]{0:T(128)S(1)}, f32[128]{0:T(128)S(1)}, u32[]{:S(2)}, u32[]{:S(2)}) collective-permute-start(f32[128]{0:T(128)S(1)} %add.32), channel_id=1, source_target_pairs={{0,8},{4,12},{8,0},{12,4},{1,9},{5,13},{9,1},{13,5},{2,10},{6,14},... | collective-permute-start | bytes 1544 | tf_op jit(solution)/shard_map/ppermute | solution.py:43
  66.3 30.5 %collective-permute-start.18 = (bf16[4,128,768]{2,1,0:T(8,128)(2,1)S(1)}, bf16[4,128,768]{2,1,0:T(8,128)(2,1)S(1)}, u32[]{:S(2)}, u32[]{:S(2)}) collective-permute-start(bf16[4,128,768]{2,1,0:T(8,128)(2,1)S(1)} %get-tuple-element.116), channel_id=1, source_target_pairs={{0,8},{4,12},{8,0},{12,4},{1,9},{5,13},{9,1},{13,5},{2,10},{6,14},... | collective-permute-start | bytes 2359304 | tf_op jit(solution)/shard_map/ppermute | solution.py:43
  80.9 17.6 %collective-permute-start.19 = (bf16[8,128,512]{2,1,0:T(8,128)(2,1)S(1)}, bf16[8,128,512]{2,1,0:T(8,128)(2,1)S(1)}, u32[]{:S(2)}, u32[]{:S(2)}) collective-permute-start(bf16[8,128,512]{2,1,0:T(8,128)(2,1)S(1)} %get-tuple-element.117), channel_id=1, source_target_pairs={{0,4},{4,0},{8,12},{12,8},{1,5},{5,1},{9,13},{13,9},{2,6},{6,2},{1... | collective-permute-start | bytes 3145736 | tf_op jit(solution)/shard_map/ppermute | solution.py:43
  80.9 9.3 %collective-permute-start.11 = (bf16[2,128,128]{2,1,0:T(8,128)(2,1)S(1)}, bf16[2,128,128]{2,1,0:T(8,128)(2,1)S(1)}, u32[]{:S(2)}, u32[]{:S(2)}) collective-permute-start(bf16[2,128,128]{2,1,0:T(8,128)(2,1)S(1)} %add.31), channel_id=1, source_target_pairs={{0,2},{1,3},{2,0},{3,1},{4,6},{5,7},{6,4},{7,5},{8,10},{9,11},{10,... | collective-permute-start | bytes 196616 | tf_op jit(solution)/shard_map/ppermute | solution.py:43
  90.0 13.4 %collective-permute-start.21 = (bf16[1,128,512]{2,1,0:T(8,128)(2,1)S(1)}, bf16[1,128,512]{2,1,0:T(8,128)(2,1)S(1)}, u32[]{:S(2)}, u32[]{:S(2)}) collective-permute-start(bf16[1,128,512]{2,1,0:T(8,128)(2,1)S(1)} %get-tuple-element.110), channel_id=1, source_target_pairs={{0,2},{1,3},{2,0},{3,1},{4,6},{5,7},{6,4},{7,5},{8,10},{9,11},{10,... | collective-permute-start | bytes 393224 | tf_op jit(solution)/shard_map/ppermute | solution.py:43
  90.2 12.7 %collective-permute-start.20 = (f32[128]{0:T(128)S(1)}, f32[128]{0:T(128)S(1)}, u32[]{:S(2)}, u32[]{:S(2)}) collective-permute-start(f32[128]{0:T(128)S(1)} %add.33), channel_id=1, source_target_pairs={{0,1},{1,0},{2,3},{3,2},{4,5},{5,4},{6,7},{7,6},{8,9},{9,8},{10,11... | collective-permute-start | bytes 1544 | tf_op jit(solution)/shard_map/ppermute | solution.py:43
  92.6 16.5 %collective-permute-start.22 = (bf16[2,128,1024]{2,1,0:T(8,128)(2,1)S(1)}, bf16[2,128,1024]{2,1,0:T(8,128)(2,1)S(1)}, u32[]{:S(2)}, u32[]{:S(2)}) collective-permute-start(bf16[2,128,1024]{2,1,0:T(8,128)(2,1)S(1)} %get-tuple-element.123), channel_id=1, source_target_pairs={{0,1},{1,0},{2,3},{3,2},{4,5},{5,4},{6,7},{7,6},{8,9},{9,8},{10,11... | collective-permute-start | bytes 1572872 | tf_op jit(solution)/shard_map/ppermute | solution.py:43
  96.8 14.9 %collective-permute-start.23 = (bf16[4,128,512]{2,1,0:T(8,128)(2,1)S(1)}, bf16[4,128,512]{2,1,0:T(8,128)(2,1)S(1)}, u32[]{:S(2)}, u32[]{:S(2)}) collective-permute-start(bf16[4,128,512]{2,1,0:T(8,128)(2,1)S(1)} %get-tuple-element.124), channel_id=1, source_target_pairs={{0,8},{4,12},{8,0},{12,4},{1,9},{5,13},{9,1},{13,5},{2,10},{6,14},... | collective-permute-start | bytes 1572872 | tf_op jit(solution)/shard_map/ppermute | solution.py:43
  98.4 16.0 %collective-permute-start.24 = (bf16[8,128,256]{2,1,0:T(8,128)(2,1)S(1)}, bf16[8,128,256]{2,1,0:T(8,128)(2,1)S(1)}, u32[]{:S(2)}, u32[]{:S(2)}) collective-permute-start(bf16[8,128,256]{2,1,0:T(8,128)(2,1)S(1)} %get-tuple-element.125), channel_id=1, source_target_pairs={{0,4},{4,0},{8,12},{12,8},{1,5},{5,1},{9,13},{13,9},{2,6},{6,2},{1... | collective-permute-start | bytes 1572872 | tf_op jit(solution)/shard_map/ppermute | solution.py:43
  102.9 17.9 %collective-permute-start.26 = (bf16[1,128,512]{2,1,0:T(8,128)(2,1)S(1)}, bf16[1,128,512]{2,1,0:T(8,128)(2,1)S(1)}, u32[]{:S(2)}, u32[]{:S(2)}) collective-permute-start(bf16[1,128,512]{2,1,0:T(8,128)(2,1)S(1)} %get-tuple-element.118), channel_id=1, source_target_pairs={{0,8},{4,12},{8,0},{12,4},{1,9},{5,13},{9,1},{13,5},{2,10},{6,14},... | collective-permute-start | bytes 393224 | tf_op jit(solution)/shard_map/ppermute | solution.py:43
  103.4 18.9 %collective-permute-start.27 = (bf16[2,128,768]{2,1,0:T(8,128)(2,1)S(1)}, bf16[2,128,768]{2,1,0:T(8,128)(2,1)S(1)}, u32[]{:S(2)}, u32[]{:S(2)}) collective-permute-start(bf16[2,128,768]{2,1,0:T(8,128)(2,1)S(1)} %get-tuple-element.131), channel_id=1, source_target_pairs={{0,1},{1,0},{2,3},{3,2},{4,5},{5,4},{6,7},{7,6},{8,9},{9,8},{10,11... | collective-permute-start | bytes 1179656 | tf_op jit(solution)/shard_map/ppermute | solution.py:43
  109.2 16.6 %collective-permute-start.28 = (bf16[4,128,512]{2,1,0:T(8,128)(2,1)S(1)}, bf16[4,128,512]{2,1,0:T(8,128)(2,1)S(1)}, u32[]{:S(2)}, u32[]{:S(2)}) collective-permute-start(bf16[4,128,512]{2,1,0:T(8,128)(2,1)S(1)} %get-tuple-element.132), channel_id=1, source_target_pairs={{0,8},{4,12},{8,0},{12,4},{1,9},{5,13},{9,1},{13,5},{2,10},{6,14},... | collective-permute-start | bytes 1572872 | tf_op jit(solution)/shard_map/ppermute | solution.py:43
  111.7 7.1 %collective-permute-start.25 = (f32[128]{0:T(128)S(1)}, f32[128]{0:T(128)S(1)}, u32[]{:S(2)}, u32[]{:S(2)}) collective-permute-start(f32[128]{0:T(128)S(1)} %add.34), channel_id=1, source_target_pairs={{0,2},{1,3},{2,0},{3,1},{4,6},{5,7},{6,4},{7,5},{8,10},{9,11},{10,... | collective-permute-start | bytes 1544 | tf_op jit(solution)/shard_map/ppermute | solution.py:43
  118.8 15.4 %collective-permute-start.29 = (bf16[1,128,1024]{2,1,0:T(8,128)(2,1)S(1)}, bf16[1,128,1024]{2,1,0:T(8,128)(2,1)S(1)}, u32[]{:S(2)}, u32[]{:S(2)}) collective-permute-start(bf16[1,128,1024]{2,1,0:T(8,128)(2,1)S(1)} %get-tuple-element.136), channel_id=1, source_target_pairs={{0,2},{1,3},{2,0},{3,1},{4,6},{5,7},{6,4},{7,5},{8,10},{9,11},{10,... | collective-permute-start | bytes 786440 | tf_op jit(solution)/shard_map/ppermute | solution.py:43
  119.2 15.1 %collective-permute-start.30 = (bf16[2,128,512]{2,1,0:T(8,128)(2,1)S(1)}, bf16[2,128,512]{2,1,0:T(8,128)(2,1)S(1)}, u32[]{:S(2)}, u32[]{:S(2)}) collective-permute-start(bf16[2,128,512]{2,1,0:T(8,128)(2,1)S(1)} %get-tuple-element.137), channel_id=1, source_target_pairs={{0,1},{1,0},{2,3},{3,2},{4,5},{5,4},{6,7},{7,6},{8,9},{9,8},{10,11... | collective-permute-start | bytes 786440 | tf_op jit(solution)/shard_map/ppermute | solution.py:43
  120.8 13.4 %collective-permute-start.31 = (bf16[4,128,256]{2,1,0:T(8,128)(2,1)S(1)}, bf16[4,128,256]{2,1,0:T(8,128)(2,1)S(1)}, u32[]{:S(2)}, u32[]{:S(2)}) collective-permute-start(bf16[4,128,256]{2,1,0:T(8,128)(2,1)S(1)} %get-tuple-element.138), channel_id=1, source_target_pairs={{0,8},{4,12},{8,0},{12,4},{1,9},{5,13},{9,1},{13,5},{2,10},{6,14},... | collective-permute-start | bytes 786440 | tf_op jit(solution)/shard_map/ppermute | solution.py:43
  129.9 9.0 %collective-permute-start.32 = (bf16[1,128,768]{2,1,0:T(8,128)(2,1)S(1)}, bf16[1,128,768]{2,1,0:T(8,128)(2,1)S(1)}, u32[]{:S(2)}, u32[]{:S(2)}) collective-permute-start(bf16[1,128,768]{2,1,0:T(8,128)(2,1)S(1)} %get-tuple-element.141), channel_id=1, source_target_pairs={{0,2},{1,3},{2,0},{3,1},{4,6},{5,7},{6,4},{7,5},{8,10},{9,11},{10,... | collective-permute-start | bytes 589832 | tf_op jit(solution)/shard_map/ppermute | solution.py:43
  132.6 5.3 %copy-start.3 = (bf16[2,128,128]{2,1,0:T(8,128)(2,1)S(1)}, bf16[2,128,128]{2,1,0:T(8,128)(2,1)}, u32[]{:S(2)}) copy-start(bf16[2,128,128]{2,1,0:T(8,128)(2,1)} %get-tuple-element.158) | copy-start | bytes 196612
  132.6 5.3 %copy-start.4 = (bf16[2,128,128]{2,1,0:T(8,128)(2,1)S(1)}, bf16[2,128,128]{2,1,0:T(8,128)(2,1)}, u32[]{:S(2)}) copy-start(bf16[2,128,128]{2,1,0:T(8,128)(2,1)} %get-tuple-element.159) | copy-start | bytes 196612
  132.6 13.0 %copy-start.2 = (f32[2048]{0:T(1024)S(1)}, f32[2048]{0:T(1024)}, u32[]{:S(2)}) copy-start(f32[2048]{0:T(1024)} %param.12) | copy-start | bytes 24580
  132.6 10.1 %collective-permute-start.33 = (bf16[2,128,512]{2,1,0:T(8,128)(2,1)S(1)}, bf16[2,128,512]{2,1,0:T(8,128)(2,1)S(1)}, u32[]{:S(2)}, u32[]{:S(2)}) collective-permute-start(bf16[2,128,512]{2,1,0:T(8,128)(2,1)S(1)} %get-tuple-element.142), channel_id=1, source_target_pairs={{0,1},{1,0},{2,3},{3,2},{4,5},{5,4},{6,7},{7,6},{8,9},{9,8},{10,11... | collective-permute-start | bytes 786440 | tf_op jit(solution)/shard_map/ppermute | solution.py:43
  137.4 8.1 %collective-permute-start.34 = (bf16[2,128,256]{2,1,0:T(8,128)(2,1)S(1)}, bf16[2,128,256]{2,1,0:T(8,128)(2,1)S(1)}, u32[]{:S(2)}, u32[]{:S(2)}) collective-permute-start(bf16[2,128,256]{2,1,0:T(8,128)(2,1)S(1)} %get-tuple-element.143), channel_id=1, source_target_pairs={{0,1},{1,0},{2,3},{3,2},{4,5},{5,4},{6,7},{7,6},{8,9},{9,8},{10,11... | collective-permute-start | bytes 393224 | tf_op jit(solution)/shard_map/ppermute | solution.py:43
  138.6 13.5 %collective-permute-start.35 = (bf16[1,128,512]{2,1,0:T(8,128)(2,1)S(1)}, bf16[1,128,512]{2,1,0:T(8,128)(2,1)S(1)}, u32[]{:S(2)}, u32[]{:S(2)}) collective-permute-start(bf16[1,128,512]{2,1,0:T(8,128)(2,1)S(1)} %get-tuple-element.146), channel_id=1, source_target_pairs={{0,2},{1,3},{2,0},{3,1},{4,6},{5,7},{6,4},{7,5},{8,10},{9,11},{10,... | collective-permute-start | bytes 393224 | tf_op jit(solution)/shard_map/ppermute | solution.py:43
  149.1 5.7 %collective-permute-start.37 = (bf16[1,128,256]{2,1,0:T(8,128)(2,1)S(1)}, bf16[1,128,256]{2,1,0:T(8,128)(2,1)S(1)}, u32[]{:S(2)}, u32[]{:S(2)}) collective-permute-start(bf16[1,128,256]{2,1,0:T(8,128)(2,1)S(1)} %get-tuple-element.149), channel_id=1, source_target_pairs={{0,2},{1,3},{2,0},{3,1},{4,6},{5,7},{6,4},{7,5},{8,10},{9,11},{10,... | collective-permute-start | bytes 196616 | tf_op jit(solution)/shard_map/ppermute | solution.py:43
  149.9 6.3 %collective-permute-start.36 = (bf16[1,128,512]{2,1,0:T(8,128)(2,1)S(1)}, bf16[1,128,512]{2,1,0:T(8,128)(2,1)S(1)}, u32[]{:S(2)}, u32[]{:S(2)}) collective-permute-start(bf16[1,128,512]{2,1,0:T(8,128)(2,1)S(1)} %get-tuple-element.148), channel_id=1, source_target_pairs={{0,2},{1,3},{2,0},{3,1},{4,6},{5,7},{6,4},{7,5},{8,10},{9,11},{10,... | collective-permute-start | bytes 393224 | tf_op jit(solution)/shard_map/ppermute | solution.py:43

commit v4 on v3

--- a/solution.py
+++ b/solution.py
@@ -26,7 +26,7 @@
     ("dec", 0, 1, (0, 2, 4, 6, 8), False),
     ("enc", 0, 1, (1, 3, 5, 7, 9), False),
 )
-COST = 100
+COST = 30
 AHEAD = 16
 TOGETHER = 4096
 FIRST_SQUARES = 4

time: 160 us -> 159 us (level)
  other arithmetic: 4.24 us -> 1.49 us
  waiting for transfers between devices: 43.3 us -> 45 us
    ppermute x34, waiting for transfers between devices: 39.1 us -> 40.8 us  [swapped(): return lax.ppermute(value, axis, [(i, i ^ mask) for i in range(count)])]
  transfers between devices with their start and end apart: 38 -> 38, of which waited for: 11 -> 11; matrix products, arithmetic and copies ran while one was open for 3% -> 1% of each run, Pallas kernels for 35% -> 35%
where the time goes in v4:
time: 159 us; the launch traced here: 158 us
  Pallas kernels  64.2 us (40%)
  starting transfers between devices  45.8 us (29%)
  waiting for transfers between devices  45 us (28%)
    pallas_call x13, Pallas kernels, run_step(): pl.pallas_call(functools.partial(step_kernel, {'kinds': kinds, 'jobs': jo...  61.3 us
    ppermute x34, waiting for transfers between devices, swapped(): return lax.ppermute(value, axis, [(i, i ^ mask) for i in range(count)])  40.8 us
    ppermute x34, starting transfers between devices, swapped(): return lax.ppermute(value, axis, [(i, i ^ mask) for i in range(count)])  37.5 us
    ppermute x2, starting transfers between devices, shifted(): lax.ppermute(value, axis, [(i, (i + steps) % count) for i in range(count)])  5.75 us
    ppermute x2, waiting for transfers between devices, shifted(): lax.ppermute(value, axis, [(i, (i + steps) % count) for i in range(count)])  4.21 us
  transfers between devices with their start and end apart: 38, of which 11 were waited for; matrix products, arithmetic and copies ran while one was open for 1% of the time, Pallas kernels for 35%

profile of v4, /device:TPU:0, one launch (start us, length us, event | category | flops | bytes accessed | tf_op | source)
XLA Modules:
  0.0 158.3 jit_solution(3174532176078358912)
XLA Ops:
  0.6 1.3 collective-permute-start
  2.0 0.8 dynamic-slice_bitcast_fusion
  2.7 3.0 %collective-permute-start.1 = (bf16[2,128,128]{2,1,0:T(8,128)(2,1)S(1)}, bf16[2,128,128]{2,1,0:T(8,128)(2,1)S(1)}, u32[]{:S(2)}, u32[]{:S(2)}) collective-permute-start(bf16[2,128,128]{2,1,0:T(8,128)(2,1)S(1)} %pad_maximum_fusion.1.refs_0_), channel_id=1, source_target_pairs={{0,16},{16,0},{1,17},{17,1},{2,18},{18,2},{3,19},{19,3},{4,20},{20... | collective-permute-start | bytes 196616 | tf_op jit(solution)/shard_map/ppermute | solution.py:38
  5.8 4.2 %collective-permute-done.1.refs_1_ = bf16[2,128,128]{2,1,0:T(8,128)(2,1)S(1)} collective-permute-done((bf16[2,128,128]{2,1,0:T(8,128)(2,1)S(1)}, bf16[2,128,128]{2,1,0:T(8,128)(2,1)S(1)}, u32[]{:S(2)}, u32[]{:S(2)}) %collective-permute-start.1) | collective-permute-done | bytes 65568 | tf_op jit(solution)/shard_map/ppermute | solution.py:38
  10.0 6.6 %shard_map.102 = (bf16[8,128,512]{2,1,0:T(8,128)(2,1)}, bf16[8,128,512]{2,1,0:T(8,128)(2,1)S(1)}) custom-call(bf16[128,512]{1,0:T(8,128)(2,1)S(1)} %broadcast_select_fusion.1.refs_0_, bf16[32768,512]{1,0:T(8,128)(2,1)} %refs_1_.22), custom_call_target="tpu_custom_call" | custom-call | flops 32212254720 | bytes 314572800 | tf_op jit(solution)/shard_map/pallas_call | solution.py:267
  16.7 2.9 %shard_map.103 = (bf16[128,512]{1,0:T(8,128)(2,1)S(1)}, bf16[128,512]{1,0:T(8,128)(2,1)}, f32[2,128,128]{2,1,0:T(8,128)S(1)}, f32[2,128,128]{2,1,0:T(8,128)S(1)}) custom-call(bf16[128,512]{1,0:T(8,128)(2,1)S(1)} %copy-done.1, bf16[128,512]{1,0:T(8,128)(2,1)S(1)} %copy-done, bf16[2,128,128]{2,1,0:T(8,128)(2,1)S(1)} %pad_maximum_fusion.1.refs_0_, ...), custom_call_target="tpu_custom_call" | custom-call | tf_op jit(solution)/shard_map/pallas_call | solution.py:333
  19.6 1.3 collective-permute-start.2
  20.9 2.7 %collective-permute-start.7 = (f32[2,128,128]{2,1,0:T(8,128)S(1)}, f32[2,128,128]{2,1,0:T(8,128)S(1)}, u32[]{:S(2)}, u32[]{:S(2)}) collective-permute-start(f32[2,128,128]{2,1,0:T(8,128)S(1)} %get-tuple-element.98), channel_id=1, source_target_pairs={{0,16},{16,0},{1,17},{17,1},{2,18},{18,2},{3,19},{19,3},{4,20},{20... | collective-permute-start | bytes 393224 | tf_op jit(solution)/shard_map/ppermute | solution.py:38
  23.6 6.7 %shard_map.104 = (bf16[4,128,512]{2,1,0:T(8,128)(2,1)S(1)}, bf16[8,128,1024]{2,1,0:T(8,128)(2,1)S(1)}) custom-call(bf16[128,512]{1,0:T(8,128)(2,1)S(1)} %broadcast_select_fusion.1.refs_0_, bf16[32768,512]{1,0:T(8,128)(2,1)} %refs_1_.22, bf16[8,128,512]{2,1,0:T(8,128)(2,1)S(1)} %collective-permute-done.3.refs_2_.refs_4_), custom_call_target="tpu_custom_call" | custom-call | flops 40265318400 | bytes 408944640 | tf_op jit(solution)/shard_map/pallas_call | solution.py:267
  30.4 2.4 %collective-permute-start.5 = (bf16[4,128,512]{2,1,0:T(8,128)(2,1)S(1)}, bf16[4,128,512]{2,1,0:T(8,128)(2,1)S(1)}, u32[]{:S(2)}, u32[]{:S(2)}) collective-permute-start(bf16[4,128,512]{2,1,0:T(8,128)(2,1)S(1)} %get-tuple-element.86), channel_id=1, source_target_pairs={{0,8},{4,12},{8,0},{12,4},{1,9},{5,13},{9,1},{13,5},{2,10},{6,14},... | collective-permute-start | bytes 1572872 | tf_op jit(solution)/shard_map/ppermute | solution.py:43
  33.1 5.7 %shard_map.105 = (bf16[4,128,512]{2,1,0:T(8,128)(2,1)S(1)}, bf16[8,128,768]{2,1,0:T(8,128)(2,1)S(1)}) custom-call(bf16[128,512]{1,0:T(8,128)(2,1)S(1)} %broadcast_select_fusion.1.refs_0_, bf16[32768,512]{1,0:T(8,128)(2,1)} %refs_1_.22, bf16[128,512]{1,0:T(8,128)(2,1)S(1)} %get-tuple-element.147.refs_2_.refs_0_, bf16[512,32768]{1,0:T(8,128)(2,1)} %refs_1_.25, ...), custom_call_target="tpu_custom_call" | custom-call | flops 32212254720 | bytes 330301440 | tf_op jit(solution)/shard_map/pallas_call | solution.py:267
  38.8 1.6 %collective-permute-start.8 = (bf16[4,128,512]{2,1,0:T(8,128)(2,1)S(1)}, bf16[4,128,512]{2,1,0:T(8,128)(2,1)S(1)}, u32[]{:S(2)}, u32[]{:S(2)}) collective-permute-start(bf16[4,128,512]{2,1,0:T(8,128)(2,1)S(1)} %get-tuple-element.91), channel_id=1, source_target_pairs={{0,1},{1,0},{2,3},{3,2},{4,5},{5,4},{6,7},{7,6},{8,9},{9,8},{10,11... | collective-permute-start | bytes 1572872 | tf_op jit(solution)/shard_map/ppermute | solution.py:43
  40.5 4.8 %collective-permute-done.5.refs_5_ = bf16[4,128,512]{2,1,0:T(8,128)(2,1)S(1)} collective-permute-done((bf16[4,128,512]{2,1,0:T(8,128)(2,1)S(1)}, bf16[4,128,512]{2,1,0:T(8,128)(2,1)S(1)}, u32[]{:S(2)}, u32[]{:S(2)}) %collective-permute-start.5) | collective-permute-done | bytes 524320 | tf_op jit(solution)/shard_map/ppermute | solution.py:43
  45.3 6.4 %shard_map.106 = (bf16[2,128,512]{2,1,0:T(8,128)(2,1)S(1)}, bf16[4,128,1024]{2,1,0:T(8,128)(2,1)S(1)}, bf16[8,128,512]{2,1,0:T(8,128)(2,1)S(1)}) custom-call(bf16[128,512]{1,0:T(8,128)(2,1)S(1)} %broadcast_select_fusion.1.refs_0_, bf16[32768,512]{1,0:T(8,128)(2,1)} %refs_1_.22, bf16[128,512]{1,0:T(8,128)(2,1)S(1)} %get-tuple-element.147.refs_2_.refs_0_, ...), custom_call_target="tpu_custom_call" | custom-call | flops 36238786560 | bytes 401080320 | tf_op jit(solution)/shard_map/pallas_call | solution.py:267
  51.8 1.9 %collective-permute-start.10 = (f32[2,128,128]{2,1,0:T(8,128)S(1)}, f32[2,128,128]{2,1,0:T(8,128)S(1)}, u32[]{:S(2)}, u32[]{:S(2)}) collective-permute-start(f32[2,128,128]{2,1,0:T(8,128)S(1)} %add.30), channel_id=1, source_target_pairs={{0,1},{1,0},{2,3},{3,2},{4,5},{5,4},{6,7},{7,6},{8,9},{9,8},{10,11... | collective-permute-start | bytes 393224 | tf_op jit(solution)/shard_map/ppermute | solution.py:43
  53.9 1.7 %collective-permute-start.14 = (bf16[4,128,1024]{2,1,0:T(8,128)(2,1)S(1)}, bf16[4,128,1024]{2,1,0:T(8,128)(2,1)S(1)}, u32[]{:S(2)}, u32[]{:S(2)}) collective-permute-start(bf16[4,128,1024]{2,1,0:T(8,128)(2,1)S(1)} %get-tuple-element.108), channel_id=1, source_target_pairs={{0,8},{4,12},{8,0},{12,4},{1,9},{5,13},{9,1},{13,5},{2,10},{6,14},... | collective-permute-start | bytes 3145736 | tf_op jit(solution)/shard_map/ppermute | solution.py:43
  55.6 5.8 %shard_map.107 = (bf16[2,128,512]{2,1,0:T(8,128)(2,1)S(1)}, bf16[4,128,768]{2,1,0:T(8,128)(2,1)S(1)}, bf16[8,128,512]{2,1,0:T(8,128)(2,1)S(1)}) custom-call(bf16[128,512]{1,0:T(8,128)(2,1)S(1)} %broadcast_select_fusion.1.refs_0_, bf16[32768,512]{1,0:T(8,128)(2,1)} %refs_1_.22, bf16[128,512]{1,0:T(8,128)(2,1)S(1)} %get-tuple-element.147.refs_2_.refs_0_, ...), custom_call_target="tpu_custom_call" | custom-call | flops 32212254720 | bytes 353894400 | tf_op jit(solution)/shard_map/pallas_call | solution.py:267
  61.5 2.6 %collective-permute-start.17 = (bf16[2,128,512]{2,1,0:T(8,128)(2,1)S(1)}, bf16[2,128,512]{2,1,0:T(8,128)(2,1)S(1)}, u32[]{:S(2)}, u32[]{:S(2)}) collective-permute-start(bf16[2,128,512]{2,1,0:T(8,128)(2,1)S(1)} %get-tuple-element.102), channel_id=1, source_target_pairs={{0,2},{1,3},{2,0},{3,1},{4,6},{5,7},{6,4},{7,5},{8,10},{9,11},{10,... | collective-permute-start | bytes 786440 | tf_op jit(solution)/shard_map/ppermute | solution.py:43
  64.7 1.6 collective-permute-start.18
  66.2 13.7 %collective-permute-done.14.refs_8_.refs_9_.refs_5_ = bf16[4,128,1024]{2,1,0:T(8,128)(2,1)S(1)} collective-permute-done((bf16[4,128,1024]{2,1,0:T(8,128)(2,1)S(1)}, bf16[4,128,1024]{2,1,0:T(8,128)(2,1)S(1)}, u32[]{:S(2)}, u32[]{:S(2)}) %collective-permute-start.14) | collective-permute-done | bytes 1048608 | tf_op jit(solution)/shard_map/ppermute | solution.py:43
  79.9 2.8 %collective-permute-start.11 = (bf16[2,128,128]{2,1,0:T(8,128)(2,1)S(1)}, bf16[2,128,128]{2,1,0:T(8,128)(2,1)S(1)}, u32[]{:S(2)}, u32[]{:S(2)}) collective-permute-start(bf16[2,128,128]{2,1,0:T(8,128)(2,1)S(1)} %add.31), channel_id=1, source_target_pairs={{0,2},{1,3},{2,0},{3,1},{4,6},{5,7},{6,4},{7,5},{8,10},{9,11},{10,... | collective-permute-start | bytes 196616 | tf_op jit(solution)/shard_map/ppermute | solution.py:43
  82.8 6.3 %shard_map.108 = (bf16[1,128,512]{2,1,0:T(8,128)(2,1)S(1)}, bf16[2,128,1024]{2,1,0:T(8,128)(2,1)S(1)}, bf16[4,128,512]{2,1,0:T(8,128)(2,1)S(1)}, bf16[8,128,256]{2,1,0:T(8,128)(2,1)S(1)}) custom-call(bf16[128,512]{1,0:T(8,128)(2,1)S(1)} %broadcast_select_fusion.1.refs_0_, bf16[32768,512]{1,0:T(8,128)(2,1)} %refs_1_.22, ...), custom_call_target="tpu_custom_call" | custom-call | flops 26172456960 | bytes 314572800 | tf_op jit(solution)/shard_map/pallas_call | solution.py:267
  89.2 1.8 %collective-permute-start.20 = (f32[128]{0:T(128)S(1)}, f32[128]{0:T(128)S(1)}, u32[]{:S(2)}, u32[]{:S(2)}) collective-permute-start(f32[128]{0:T(128)S(1)} %add.33), channel_id=1, source_target_pairs={{0,1},{1,0},{2,3},{3,2},{4,5},{5,4},{6,7},{7,6},{8,9},{9,8},{10,11... | collective-permute-start | bytes 1544 | tf_op jit(solution)/shard_map/ppermute | solution.py:43
  91.4 4.5 %collective-permute-done.18.refs_8_.refs_9_.refs_3_ = bf16[4,128,768]{2,1,0:T(8,128)(2,1)S(1)} collective-permute-done((bf16[4,128,768]{2,1,0:T(8,128)(2,1)S(1)}, bf16[4,128,768]{2,1,0:T(8,128)(2,1)S(1)}, u32[]{:S(2)}, u32[]{:S(2)}) %collective-permute-start.18) | collective-permute-done | bytes 786464 | tf_op jit(solution)/shard_map/ppermute | solution.py:43
  95.9 1.6 %collective-permute-start.23 = (bf16[4,128,512]{2,1,0:T(8,128)(2,1)S(1)}, bf16[4,128,512]{2,1,0:T(8,128)(2,1)S(1)}, u32[]{:S(2)}, u32[]{:S(2)}) collective-permute-start(bf16[4,128,512]{2,1,0:T(8,128)(2,1)S(1)} %get-tuple-element.124), channel_id=1, source_target_pairs={{0,8},{4,12},{8,0},{12,4},{1,9},{5,13},{9,1},{13,5},{2,10},{6,14},... | collective-permute-start | bytes 1572872 | tf_op jit(solution)/shard_map/ppermute | solution.py:43
  97.5 4.5 %shard_map.109 = (bf16[1,128,512]{2,1,0:T(8,128)(2,1)S(1)}, bf16[2,128,768]{2,1,0:T(8,128)(2,1)S(1)}, bf16[4,128,512]{2,1,0:T(8,128)(2,1)S(1)}) custom-call(bf16[128,512]{1,0:T(8,128)(2,1)S(1)} %broadcast_select_fusion.1.refs_0_, bf16[32768,512]{1,0:T(8,128)(2,1)} %refs_1_.22, bf16[128,512]{1,0:T(8,128)(2,1)S(1)} %get-tuple-element.147.refs_2_.refs_0_, ...), custom_call_target="tpu_custom_call" | custom-call | flops 16106127360 | bytes 208404480 | tf_op jit(solution)/shard_map/pallas_call | solution.py:267
  102.5 1.7 %collective-permute-start.27 = (bf16[2,128,768]{2,1,0:T(8,128)(2,1)S(1)}, bf16[2,128,768]{2,1,0:T(8,128)(2,1)S(1)}, u32[]{:S(2)}, u32[]{:S(2)}) collective-permute-start(bf16[2,128,768]{2,1,0:T(8,128)(2,1)S(1)} %get-tuple-element.131), channel_id=1, source_target_pairs={{0,1},{1,0},{2,3},{3,2},{4,5},{5,4},{6,7},{7,6},{8,9},{9,8},{10,11... | collective-permute-start | bytes 1179656 | tf_op jit(solution)/shard_map/ppermute | solution.py:43
  104.2 3.5 %collective-permute-done.22.refs_10_.refs_6_ = bf16[2,128,1024]{2,1,0:T(8,128)(2,1)S(1)} collective-permute-done((bf16[2,128,1024]{2,1,0:T(8,128)(2,1)S(1)}, bf16[2,128,1024]{2,1,0:T(8,128)(2,1)S(1)}, u32[]{:S(2)}, u32[]{:S(2)}) %collective-permute-start.22) | collective-permute-done | bytes 524320 | tf_op jit(solution)/shard_map/ppermute | solution.py:43
  107.7 1.5 collective-permute-start.28
  109.1 1.6 %collective-permute-done.23.refs_12_.refs_9_.refs_3_ = bf16[4,128,512]{2,1,0:T(8,128)(2,1)S(1)} collective-permute-done((bf16[4,128,512]{2,1,0:T(8,128)(2,1)S(1)}, bf16[4,128,512]{2,1,0:T(8,128)(2,1)S(1)}, u32[]{:S(2)}, u32[]{:S(2)}) %collective-permute-start.23) | collective-permute-done | bytes 524320 | tf_op jit(solution)/shard_map/ppermute | solution.py:43
  110.8 2.7 %collective-permute-start.25 = (f32[128]{0:T(128)S(1)}, f32[128]{0:T(128)S(1)}, u32[]{:S(2)}, u32[]{:S(2)}) collective-permute-start(f32[128]{0:T(128)S(1)} %add.34), channel_id=1, source_target_pairs={{0,2},{1,3},{2,0},{3,1},{4,6},{5,7},{6,4},{7,5},{8,10},{9,11},{10,... | collective-permute-start | bytes 1544 | tf_op jit(solution)/shard_map/ppermute | solution.py:43
  113.5 4.4 %shard_map.110 = (f32[1,128,512]{2,1,0:T(8,128)S(1)}, bf16[1,128,1024]{2,1,0:T(8,128)(2,1)S(1)}, bf16[2,128,512]{2,1,0:T(8,128)(2,1)S(1)}, bf16[4,128,256]{2,1,0:T(8,128)(2,1)S(1)}) custom-call(bf16[128,512]{1,0:T(8,128)(2,1)S(1)} %broadcast_select_fusion.1.refs_0_, bf16[32768,512]{1,0:T(8,128)(2,1)} %refs_1_.22, ...), custom_call_target="tpu_custom_call" | custom-call | flops 14092861440 | bytes 200540160 | tf_op jit(solution)/shard_map/pallas_call | solution.py:267
  118.2 1.7 %collective-permute-start.30 = (bf16[2,128,512]{2,1,0:T(8,128)(2,1)S(1)}, bf16[2,128,512]{2,1,0:T(8,128)(2,1)S(1)}, u32[]{:S(2)}, u32[]{:S(2)}) collective-permute-start(bf16[2,128,512]{2,1,0:T(8,128)(2,1)S(1)} %get-tuple-element.137), channel_id=1, source_target_pairs={{0,1},{1,0},{2,3},{3,2},{4,5},{5,4},{6,7},{7,6},{8,9},{9,8},{10,11... | collective-permute-start | bytes 786440 | tf_op jit(solution)/shard_map/ppermute | solution.py:43
  119.9 1.5 collective-permute-start.31
  121.4 3.4 %collective-permute-done.28.refs_12_.refs_7_.refs_3_ = bf16[4,128,512]{2,1,0:T(8,128)(2,1)S(1)} collective-permute-done((bf16[4,128,512]{2,1,0:T(8,128)(2,1)S(1)}, bf16[4,128,512]{2,1,0:T(8,128)(2,1)S(1)}, u32[]{:S(2)}, u32[]{:S(2)}) %collective-permute-start.28) | collective-permute-done | bytes 524320 | tf_op jit(solution)/shard_map/ppermute | solution.py:43
  124.8 4.1 %shard_map.111 = (f32[1,128,512]{2,1,0:T(8,128)S(1)}, bf16[1,128,768]{2,1,0:T(8,128)(2,1)S(1)}, bf16[2,128,512]{2,1,0:T(8,128)(2,1)S(1)}) custom-call(bf16[128,512]{1,0:T(8,128)(2,1)S(1)} %broadcast_select_fusion.1.refs_0_, bf16[32768,512]{1,0:T(8,128)(2,1)} %refs_1_.22, bf16[128,512]{1,0:T(8,128)(2,1)S(1)} %get-tuple-element.147.refs_2_.refs_0_, ...), custom_call_target="tpu_custom_call" | custom-call | flops 9059696640 | bytes 137625600 | tf_op jit(solution)/shard_map/pallas_call | solution.py:267
  128.9 2.7 %collective-permute-start.32 = (bf16[1,128,768]{2,1,0:T(8,128)(2,1)S(1)}, bf16[1,128,768]{2,1,0:T(8,128)(2,1)S(1)}, u32[]{:S(2)}, u32[]{:S(2)}) collective-permute-start(bf16[1,128,768]{2,1,0:T(8,128)(2,1)S(1)} %get-tuple-element.141), channel_id=1, source_target_pairs={{0,2},{1,3},{2,0},{3,1},{4,6},{5,7},{6,4},{7,5},{8,10},{9,11},{10,... | collective-permute-start | bytes 589832 | tf_op jit(solution)/shard_map/ppermute | solution.py:43
  131.7 1.6 collective-permute-start.33
  133.3 3.2 %shard_map.112 = (f32[1,128,1024]{2,1,0:T(8,128)S(1)}, bf16[1,128,512]{2,1,0:T(8,128)(2,1)S(1)}, bf16[2,128,256]{2,1,0:T(8,128)(2,1)S(1)}) custom-call(bf16[128,512]{1,0:T(8,128)(2,1)S(1)} %broadcast_select_fusion.1.refs_0_, bf16[32768,512]{1,0:T(8,128)(2,1)} %refs_1_.22, bf16[128,512]{1,0:T(8,128)(2,1)S(1)} %get-tuple-element.147.refs_2_.refs_0_, ...), custom_call_target="tpu_custom_call" | custom-call | flops 8053063680 | bytes 129761280 | tf_op jit(solution)/shard_map/pallas_call | solution.py:267
  137.9 3.9 %collective-permute-done.33.refs_8_.refs_4_ = bf16[2,128,512]{2,1,0:T(8,128)(2,1)S(1)} collective-permute-done((bf16[2,128,512]{2,1,0:T(8,128)(2,1)S(1)}, bf16[2,128,512]{2,1,0:T(8,128)(2,1)S(1)}, u32[]{:S(2)}, u32[]{:S(2)}) %collective-permute-start.33) | collective-permute-done | bytes 262176 | tf_op jit(solution)/shard_map/ppermute | solution.py:43
  141.8 2.8 %collective-permute-done.34.refs_11_.refs_8_ = bf16[2,128,256]{2,1,0:T(8,128)(2,1)S(1)} collective-permute-done((bf16[2,128,256]{2,1,0:T(8,128)(2,1)S(1)}, bf16[2,128,256]{2,1,0:T(8,128)(2,1)S(1)}, u32[]{:S(2)}, u32[]{:S(2)}) %collective-permute-start.34) | collective-permute-done | bytes 131104 | tf_op jit(solution)/shard_map/ppermute | solution.py:43
  144.7 3.5 %shard_map.113 = (f32[1,1,768]{2,1,0:T(1,128)S(1)}, bf16[1,128,512]{2,1,0:T(8,128)(2,1)S(1)}, bf16[1,128,256]{2,1,0:T(8,128)(2,1)S(1)}) custom-call(bf16[128,512]{1,0:T(8,128)(2,1)S(1)} %get-tuple-element.147.refs_2_.refs_0_, bf16[512,32768]{1,0:T(8,128)(2,1)} %refs_1_.25, bf16[8,128,768]{2,1,0:T(8,128)(2,1)S(1)} %collective-permute-done.9.refs_6_.refs_7_.refs_8_.refs_2_, ...), custom_call_target="tpu_custom_call" | custom-call | flops 6039797760 | bytes 100270080 | tf_op jit(solution)/shard_map/pallas_call | solution.py:267
  148.2 0.8 collective-permute-start.37
  149.0 2.2 %collective-permute-start.36 = (bf16[1,128,512]{2,1,0:T(8,128)(2,1)S(1)}, bf16[1,128,512]{2,1,0:T(8,128)(2,1)S(1)}, u32[]{:S(2)}, u32[]{:S(2)}) collective-permute-start(bf16[1,128,512]{2,1,0:T(8,128)(2,1)S(1)} %get-tuple-element.148), channel_id=1, source_target_pairs={{0,2},{1,3},{2,0},{3,1},{4,6},{5,7},{6,4},{7,5},{8,10},{9,11},{10,... | collective-permute-start | bytes 393224 | tf_op jit(solution)/shard_map/ppermute | solution.py:43
  151.2 1.6 %shard_map.114 = f32[1,1,512]{2,1,0:T(1,128)S(1)} custom-call(bf16[128,512]{1,0:T(8,128)(2,1)S(1)} %get-tuple-element.147.refs_2_.refs_0_, bf16[512,32768]{1,0:T(8,128)(2,1)} %refs_1_.25, bf16[8,128,512]{2,1,0:T(8,128)(2,1)S(1)} %collective-permute-done.15.refs_9_.refs_11_.refs_8_.refs_2_, ...), custom_call_target="tpu_custom_call" | custom-call | flops 2013265920 | bytes 35389440 | tf_op jit(solution)/shard_map/pallas_call | solution.py:267
  152.8 1.1 collective-permute-done.37.refs_9_
  153.9 1.4 collective-permute-done.36.refs_5_
  155.3 2.4 %shard_map.115 = (f32[1,1,512]{2,1,0:T(1,128)S(1)}, f32[1,1,256]{2,1,0:T(1,128)S(1)}) custom-call(bf16[128,512]{1,0:T(8,128)(2,1)S(1)} %get-tuple-element.147.refs_2_.refs_0_, bf16[512,32768]{1,0:T(8,128)(2,1)} %refs_1_.25, bf16[8,128,512]{2,1,0:T(8,128)(2,1)S(1)} %collective-permute-done.19.refs_9_.refs_11_.refs_6_.refs_2_, ...), custom_call_target="tpu_custom_call" | custom-call | flops 3019898880 | bytes 53084160 | tf_op jit(solution)/shard_map/pallas_call | solution.py:267
  (62 shorter events, 4.8 us)
Async XLA Ops:
  0.6 9.4 %collective-permute-start = (bf16[128,512]{1,0:T(8,128)(2,1)}, bf16[128,512]{1,0:T(8,128)(2,1)S(1)}, u32[]{:S(2)}, u32[]{:S(2)}) collective-permute-start(bf16[128,512]{1,0:T(8,128)(2,1)} %out_grad.1), channel_id=1, source_target_pairs={{16,0},{17,1},{18,2},{19,3},{20,4},{21,5},{22,6},{23,7},{24,8},{25... | collective-permute-start | bytes 393224 | tf_op jit(solution)/shard_map/ppermute | solution.py:54
  2.7 7.2 %collective-permute-start.1 = (bf16[2,128,128]{2,1,0:T(8,128)(2,1)S(1)}, bf16[2,128,128]{2,1,0:T(8,128)(2,1)S(1)}, u32[]{:S(2)}, u32[]{:S(2)}) collective-permute-start(bf16[2,128,128]{2,1,0:T(8,128)(2,1)S(1)} %pad_maximum_fusion.1.refs_0_), channel_id=1, source_target_pairs={{0,16},{16,0},{1,17},{17,1},{2,18},{18,2},{3,19},{19,3},{4,20},{20... | collective-permute-start | bytes 196616 | tf_op jit(solution)/shard_map/ppermute | solution.py:38
  10.0 6.7 %copy-start = (bf16[128,512]{1,0:T(8,128)(2,1)S(1)}, bf16[128,512]{1,0:T(8,128)(2,1)}, u32[]{:S(2)}) copy-start(bf16[128,512]{1,0:T(8,128)(2,1)} %out_grad.1) | copy-start | bytes 393220
  10.0 6.7 %copy-start.1 = (bf16[128,512]{1,0:T(8,128)(2,1)S(1)}, bf16[128,512]{1,0:T(8,128)(2,1)}, u32[]{:S(2)}) copy-start(bf16[128,512]{1,0:T(8,128)(2,1)} %queries) | copy-start | bytes 393220
  16.6 7.0 %collective-permute-start.3 = (bf16[8,128,512]{2,1,0:T(8,128)(2,1)}, bf16[8,128,512]{2,1,0:T(8,128)(2,1)S(1)}, u32[]{:S(2)}, u32[]{:S(2)}) collective-permute-start(bf16[8,128,512]{2,1,0:T(8,128)(2,1)} %get-tuple-element.79), channel_id=1, source_target_pairs={{0,4},{4,0},{8,12},{12,8},{1,5},{5,1},{9,13},{13,9},{2,6},{6,2},{1... | collective-permute-start | bytes 3145736 | tf_op jit(solution)/shard_map/ppermute | solution.py:43
  19.6 13.1 %collective-permute-start.2 = (bf16[128,512]{1,0:T(8,128)(2,1)S(1)}, bf16[128,512]{1,0:T(8,128)(2,1)S(1)}, u32[]{:S(2)}, u32[]{:S(2)}) collective-permute-start(bf16[128,512]{1,0:T(8,128)(2,1)S(1)} %get-tuple-element.88), channel_id=1, source_target_pairs={{16,0},{17,1},{18,2},{19,3},{20,4},{21,5},{22,6},{23,7},{24,8},{25... | collective-permute-start | bytes 393224 | tf_op jit(solution)/shard_map/ppermute | solution.py:54
  20.9 30.9 %collective-permute-start.7 = (f32[2,128,128]{2,1,0:T(8,128)S(1)}, f32[2,128,128]{2,1,0:T(8,128)S(1)}, u32[]{:S(2)}, u32[]{:S(2)}) collective-permute-start(f32[2,128,128]{2,1,0:T(8,128)S(1)} %get-tuple-element.98), channel_id=1, source_target_pairs={{0,16},{16,0},{1,17},{17,1},{2,18},{18,2},{3,19},{19,3},{4,20},{20... | collective-permute-start | bytes 393224 | tf_op jit(solution)/shard_map/ppermute | solution.py:38
  23.6 9.5 %collective-permute-start.4 = (bf16[8,128,512]{2,1,0:T(8,128)(2,1)S(1)}, bf16[8,128,512]{2,1,0:T(8,128)(2,1)S(1)}, u32[]{:S(2)}, u32[]{:S(2)}) collective-permute-start(bf16[8,128,512]{2,1,0:T(8,128)(2,1)S(1)} %get-tuple-element.90), channel_id=1, source_target_pairs={{0,4},{4,0},{8,12},{12,8},{1,5},{5,1},{9,13},{13,9},{2,6},{6,2},{1... | collective-permute-start | bytes 3145736 | tf_op jit(solution)/shard_map/ppermute | solution.py:43
  30.4 15.0 %collective-permute-start.5 = (bf16[4,128,512]{2,1,0:T(8,128)(2,1)S(1)}, bf16[4,128,512]{2,1,0:T(8,128)(2,1)S(1)}, u32[]{:S(2)}, u32[]{:S(2)}) collective-permute-start(bf16[4,128,512]{2,1,0:T(8,128)(2,1)S(1)} %get-tuple-element.86), channel_id=1, source_target_pairs={{0,8},{4,12},{8,0},{12,4},{1,9},{5,13},{9,1},{13,5},{2,10},{6,14},... | collective-permute-start | bytes 1572872 | tf_op jit(solution)/shard_map/ppermute | solution.py:43
  32.9 12.5 %collective-permute-start.6 = (bf16[8,128,1024]{2,1,0:T(8,128)(2,1)S(1)}, bf16[8,128,1024]{2,1,0:T(8,128)(2,1)S(1)}, u32[]{:S(2)}, u32[]{:S(2)}) collective-permute-start(bf16[8,128,1024]{2,1,0:T(8,128)(2,1)S(1)} %get-tuple-element.94), channel_id=1, source_target_pairs={{0,4},{4,0},{8,12},{12,8},{1,5},{5,1},{9,13},{13,9},{2,6},{6,2},{1... | collective-permute-start | bytes 6291464 | tf_op jit(solution)/shard_map/ppermute | solution.py:43
  38.8 15.1 %collective-permute-start.8 = (bf16[4,128,512]{2,1,0:T(8,128)(2,1)S(1)}, bf16[4,128,512]{2,1,0:T(8,128)(2,1)S(1)}, u32[]{:S(2)}, u32[]{:S(2)}) collective-permute-start(bf16[4,128,512]{2,1,0:T(8,128)(2,1)S(1)} %get-tuple-element.91), channel_id=1, source_target_pairs={{0,1},{1,0},{2,3},{3,2},{4,5},{5,4},{6,7},{7,6},{8,9},{9,8},{10,11... | collective-permute-start | bytes 1572872 | tf_op jit(solution)/shard_map/ppermute | solution.py:43
  40.5 21.0 %collective-permute-start.12 = (f32[128]{0:T(128)S(1)}, f32[128]{0:T(128)S(1)}, u32[]{:S(2)}, u32[]{:S(2)}) collective-permute-start(f32[128]{0:T(128)S(1)} %get-tuple-element.154), channel_id=1, source_target_pairs={{0,4},{4,0},{8,12},{12,8},{1,5},{5,1},{9,13},{13,9},{2,6},{6,2},{1... | collective-permute-start | bytes 1544 | tf_op jit(solution)/shard_map/ppermute | solution.py:43
  45.3 10.3 %collective-permute-start.9 = (bf16[8,128,768]{2,1,0:T(8,128)(2,1)S(1)}, bf16[8,128,768]{2,1,0:T(8,128)(2,1)S(1)}, u32[]{:S(2)}, u32[]{:S(2)}) collective-permute-start(bf16[8,128,768]{2,1,0:T(8,128)(2,1)S(1)} %get-tuple-element.101), channel_id=1, source_target_pairs={{0,4},{4,0},{8,12},{12,8},{1,5},{5,1},{9,13},{13,9},{2,6},{6,2},{1... | collective-permute-start | bytes 4718600 | tf_op jit(solution)/shard_map/ppermute | solution.py:43
  51.8 12.3 %collective-permute-start.10 = (f32[2,128,128]{2,1,0:T(8,128)S(1)}, f32[2,128,128]{2,1,0:T(8,128)S(1)}, u32[]{:S(2)}, u32[]{:S(2)}) collective-permute-start(f32[2,128,128]{2,1,0:T(8,128)S(1)} %add.30), channel_id=1, source_target_pairs={{0,1},{1,0},{2,3},{3,2},{4,5},{5,4},{6,7},{7,6},{8,9},{9,8},{10,11... | collective-permute-start | bytes 393224 | tf_op jit(solution)/shard_map/ppermute | solution.py:43
  53.7 11.0 %collective-permute-start.13 = (bf16[2,128,512]{2,1,0:T(8,128)(2,1)S(1)}, bf16[2,128,512]{2,1,0:T(8,128)(2,1)S(1)}, u32[]{:S(2)}, u32[]{:S(2)}) collective-permute-start(bf16[2,128,512]{2,1,0:T(8,128)(2,1)S(1)} %get-tuple-element.95), channel_id=1, source_target_pairs={{0,1},{1,0},{2,3},{3,2},{4,5},{5,4},{6,7},{7,6},{8,9},{9,8},{10,11... | collective-permute-start | bytes 786440 | tf_op jit(solution)/shard_map/ppermute | solution.py:43
  53.9 26.0 %collective-permute-start.14 = (bf16[4,128,1024]{2,1,0:T(8,128)(2,1)S(1)}, bf16[4,128,1024]{2,1,0:T(8,128)(2,1)S(1)}, u32[]{:S(2)}, u32[]{:S(2)}) collective-permute-start(bf16[4,128,1024]{2,1,0:T(8,128)(2,1)S(1)} %get-tuple-element.108), channel_id=1, source_target_pairs={{0,8},{4,12},{8,0},{12,4},{1,9},{5,13},{9,1},{13,5},{2,10},{6,14},... | collective-permute-start | bytes 3145736 | tf_op jit(solution)/shard_map/ppermute | solution.py:43
  55.6 24.3 %collective-permute-start.15 = (bf16[8,128,512]{2,1,0:T(8,128)(2,1)S(1)}, bf16[8,128,512]{2,1,0:T(8,128)(2,1)S(1)}, u32[]{:S(2)}, u32[]{:S(2)}) collective-permute-start(bf16[8,128,512]{2,1,0:T(8,128)(2,1)S(1)} %get-tuple-element.109), channel_id=1, source_target_pairs={{0,4},{4,0},{8,12},{12,8},{1,5},{5,1},{9,13},{13,9},{2,6},{6,2},{1... | collective-permute-start | bytes 3145736 | tf_op jit(solution)/shard_map/ppermute | solution.py:43
  61.5 29.6 %collective-permute-start.17 = (bf16[2,128,512]{2,1,0:T(8,128)(2,1)S(1)}, bf16[2,128,512]{2,1,0:T(8,128)(2,1)S(1)}, u32[]{:S(2)}, u32[]{:S(2)}) collective-permute-start(bf16[2,128,512]{2,1,0:T(8,128)(2,1)S(1)} %get-tuple-element.102), channel_id=1, source_target_pairs={{0,2},{1,3},{2,0},{3,1},{4,6},{5,7},{6,4},{7,5},{8,10},{9,11},{10,... | collective-permute-start | bytes 786440 | tf_op jit(solution)/shard_map/ppermute | solution.py:43
  64.1 24.9 %collective-permute-start.16 = (f32[128]{0:T(128)S(1)}, f32[128]{0:T(128)S(1)}, u32[]{:S(2)}, u32[]{:S(2)}) collective-permute-start(f32[128]{0:T(128)S(1)} %add.32), channel_id=1, source_target_pairs={{0,8},{4,12},{8,0},{12,4},{1,9},{5,13},{9,1},{13,5},{2,10},{6,14},... | collective-permute-start | bytes 1544 | tf_op jit(solution)/shard_map/ppermute | solution.py:43
  64.7 31.2 %collective-permute-start.18 = (bf16[4,128,768]{2,1,0:T(8,128)(2,1)S(1)}, bf16[4,128,768]{2,1,0:T(8,128)(2,1)S(1)}, u32[]{:S(2)}, u32[]{:S(2)}) collective-permute-start(bf16[4,128,768]{2,1,0:T(8,128)(2,1)S(1)} %get-tuple-element.116), channel_id=1, source_target_pairs={{0,8},{4,12},{8,0},{12,4},{1,9},{5,13},{9,1},{13,5},{2,10},{6,14},... | collective-permute-start | bytes 2359304 | tf_op jit(solution)/shard_map/ppermute | solution.py:43
  79.9 17.6 %collective-permute-start.19 = (bf16[8,128,512]{2,1,0:T(8,128)(2,1)S(1)}, bf16[8,128,512]{2,1,0:T(8,128)(2,1)S(1)}, u32[]{:S(2)}, u32[]{:S(2)}) collective-permute-start(bf16[8,128,512]{2,1,0:T(8,128)(2,1)S(1)} %get-tuple-element.117), channel_id=1, source_target_pairs={{0,4},{4,0},{8,12},{12,8},{1,5},{5,1},{9,13},{13,9},{2,6},{6,2},{1... | collective-permute-start | bytes 3145736 | tf_op jit(solution)/shard_map/ppermute | solution.py:43
  79.9 9.3 %collective-permute-start.11 = (bf16[2,128,128]{2,1,0:T(8,128)(2,1)S(1)}, bf16[2,128,128]{2,1,0:T(8,128)(2,1)S(1)}, u32[]{:S(2)}, u32[]{:S(2)}) collective-permute-start(bf16[2,128,128]{2,1,0:T(8,128)(2,1)S(1)} %add.31), channel_id=1, source_target_pairs={{0,2},{1,3},{2,0},{3,1},{4,6},{5,7},{6,4},{7,5},{8,10},{9,11},{10,... | collective-permute-start | bytes 196616 | tf_op jit(solution)/shard_map/ppermute | solution.py:43
  89.1 13.4 %collective-permute-start.21 = (bf16[1,128,512]{2,1,0:T(8,128)(2,1)S(1)}, bf16[1,128,512]{2,1,0:T(8,128)(2,1)S(1)}, u32[]{:S(2)}, u32[]{:S(2)}) collective-permute-start(bf16[1,128,512]{2,1,0:T(8,128)(2,1)S(1)} %get-tuple-element.110), channel_id=1, source_target_pairs={{0,2},{1,3},{2,0},{3,1},{4,6},{5,7},{6,4},{7,5},{8,10},{9,11},{10,... | collective-permute-start | bytes 393224 | tf_op jit(solution)/shard_map/ppermute | solution.py:43
  89.2 12.7 %collective-permute-start.20 = (f32[128]{0:T(128)S(1)}, f32[128]{0:T(128)S(1)}, u32[]{:S(2)}, u32[]{:S(2)}) collective-permute-start(f32[128]{0:T(128)S(1)} %add.33), channel_id=1, source_target_pairs={{0,1},{1,0},{2,3},{3,2},{4,5},{5,4},{6,7},{7,6},{8,9},{9,8},{10,11... | collective-permute-start | bytes 1544 | tf_op jit(solution)/shard_map/ppermute | solution.py:43
  91.1 16.6 %collective-permute-start.22 = (bf16[2,128,1024]{2,1,0:T(8,128)(2,1)S(1)}, bf16[2,128,1024]{2,1,0:T(8,128)(2,1)S(1)}, u32[]{:S(2)}, u32[]{:S(2)}) collective-permute-start(bf16[2,128,1024]{2,1,0:T(8,128)(2,1)S(1)} %get-tuple-element.123), channel_id=1, source_target_pairs={{0,1},{1,0},{2,3},{3,2},{4,5},{5,4},{6,7},{7,6},{8,9},{9,8},{10,11... | collective-permute-start | bytes 1572872 | tf_op jit(solution)/shard_map/ppermute | solution.py:43
  95.9 14.9 %collective-permute-start.23 = (bf16[4,128,512]{2,1,0:T(8,128)(2,1)S(1)}, bf16[4,128,512]{2,1,0:T(8,128)(2,1)S(1)}, u32[]{:S(2)}, u32[]{:S(2)}) collective-permute-start(bf16[4,128,512]{2,1,0:T(8,128)(2,1)S(1)} %get-tuple-element.124), channel_id=1, source_target_pairs={{0,8},{4,12},{8,0},{12,4},{1,9},{5,13},{9,1},{13,5},{2,10},{6,14},... | collective-permute-start | bytes 1572872 | tf_op jit(solution)/shard_map/ppermute | solution.py:43
  97.5 16.0 %collective-permute-start.24 = (bf16[8,128,256]{2,1,0:T(8,128)(2,1)S(1)}, bf16[8,128,256]{2,1,0:T(8,128)(2,1)S(1)}, u32[]{:S(2)}, u32[]{:S(2)}) collective-permute-start(bf16[8,128,256]{2,1,0:T(8,128)(2,1)S(1)} %get-tuple-element.125), channel_id=1, source_target_pairs={{0,4},{4,0},{8,12},{12,8},{1,5},{5,1},{9,13},{13,9},{2,6},{6,2},{1... | collective-permute-start | bytes 1572872 | tf_op jit(solution)/shard_map/ppermute | solution.py:43
  102.0 17.9 %collective-permute-start.26 = (bf16[1,128,512]{2,1,0:T(8,128)(2,1)S(1)}, bf16[1,128,512]{2,1,0:T(8,128)(2,1)S(1)}, u32[]{:S(2)}, u32[]{:S(2)}) collective-permute-start(bf16[1,128,512]{2,1,0:T(8,128)(2,1)S(1)} %get-tuple-element.118), channel_id=1, source_target_pairs={{0,8},{4,12},{8,0},{12,4},{1,9},{5,13},{9,1},{13,5},{2,10},{6,14},... | collective-permute-start | bytes 393224 | tf_op jit(solution)/shard_map/ppermute | solution.py:43
  102.5 18.9 %collective-permute-start.27 = (bf16[2,128,768]{2,1,0:T(8,128)(2,1)S(1)}, bf16[2,128,768]{2,1,0:T(8,128)(2,1)S(1)}, u32[]{:S(2)}, u32[]{:S(2)}) collective-permute-start(bf16[2,128,768]{2,1,0:T(8,128)(2,1)S(1)} %get-tuple-element.131), channel_id=1, source_target_pairs={{0,1},{1,0},{2,3},{3,2},{4,5},{5,4},{6,7},{7,6},{8,9},{9,8},{10,11... | collective-permute-start | bytes 1179656 | tf_op jit(solution)/shard_map/ppermute | solution.py:43
  107.7 17.2 %collective-permute-start.28 = (bf16[4,128,512]{2,1,0:T(8,128)(2,1)S(1)}, bf16[4,128,512]{2,1,0:T(8,128)(2,1)S(1)}, u32[]{:S(2)}, u32[]{:S(2)}) collective-permute-start(bf16[4,128,512]{2,1,0:T(8,128)(2,1)S(1)} %get-tuple-element.132), channel_id=1, source_target_pairs={{0,8},{4,12},{8,0},{12,4},{1,9},{5,13},{9,1},{13,5},{2,10},{6,14},... | collective-permute-start | bytes 1572872 | tf_op jit(solution)/shard_map/ppermute | solution.py:43
  110.8 7.1 %collective-permute-start.25 = (f32[128]{0:T(128)S(1)}, f32[128]{0:T(128)S(1)}, u32[]{:S(2)}, u32[]{:S(2)}) collective-permute-start(f32[128]{0:T(128)S(1)} %add.34), channel_id=1, source_target_pairs={{0,2},{1,3},{2,0},{3,1},{4,6},{5,7},{6,4},{7,5},{8,10},{9,11},{10,... | collective-permute-start | bytes 1544 | tf_op jit(solution)/shard_map/ppermute | solution.py:43
  117.9 15.4 %collective-permute-start.29 = (bf16[1,128,1024]{2,1,0:T(8,128)(2,1)S(1)}, bf16[1,128,1024]{2,1,0:T(8,128)(2,1)S(1)}, u32[]{:S(2)}, u32[]{:S(2)}) collective-permute-start(bf16[1,128,1024]{2,1,0:T(8,128)(2,1)S(1)} %get-tuple-element.136), channel_id=1, source_target_pairs={{0,2},{1,3},{2,0},{3,1},{4,6},{5,7},{6,4},{7,5},{8,10},{9,11},{10,... | collective-permute-start | bytes 786440 | tf_op jit(solution)/shard_map/ppermute | solution.py:43
  118.2 15.1 %collective-permute-start.30 = (bf16[2,128,512]{2,1,0:T(8,128)(2,1)S(1)}, bf16[2,128,512]{2,1,0:T(8,128)(2,1)S(1)}, u32[]{:S(2)}, u32[]{:S(2)}) collective-permute-start(bf16[2,128,512]{2,1,0:T(8,128)(2,1)S(1)} %get-tuple-element.137), channel_id=1, source_target_pairs={{0,1},{1,0},{2,3},{3,2},{4,5},{5,4},{6,7},{7,6},{8,9},{9,8},{10,11... | collective-permute-start | bytes 786440 | tf_op jit(solution)/shard_map/ppermute | solution.py:43
  119.9 13.4 %collective-permute-start.31 = (bf16[4,128,256]{2,1,0:T(8,128)(2,1)S(1)}, bf16[4,128,256]{2,1,0:T(8,128)(2,1)S(1)}, u32[]{:S(2)}, u32[]{:S(2)}) collective-permute-start(bf16[4,128,256]{2,1,0:T(8,128)(2,1)S(1)} %get-tuple-element.138), channel_id=1, source_target_pairs={{0,8},{4,12},{8,0},{12,4},{1,9},{5,13},{9,1},{13,5},{2,10},{6,14},... | collective-permute-start | bytes 786440 | tf_op jit(solution)/shard_map/ppermute | solution.py:43
  128.9 9.0 %collective-permute-start.32 = (bf16[1,128,768]{2,1,0:T(8,128)(2,1)S(1)}, bf16[1,128,768]{2,1,0:T(8,128)(2,1)S(1)}, u32[]{:S(2)}, u32[]{:S(2)}) collective-permute-start(bf16[1,128,768]{2,1,0:T(8,128)(2,1)S(1)} %get-tuple-element.141), channel_id=1, source_target_pairs={{0,2},{1,3},{2,0},{3,1},{4,6},{5,7},{6,4},{7,5},{8,10},{9,11},{10,... | collective-permute-start | bytes 589832 | tf_op jit(solution)/shard_map/ppermute | solution.py:43
  131.7 13.0 %copy-start.2 = (f32[2048]{0:T(1024)S(1)}, f32[2048]{0:T(1024)}, u32[]{:S(2)}) copy-start(f32[2048]{0:T(1024)} %param.12) | copy-start | bytes 24580
  131.7 10.1 %collective-permute-start.33 = (bf16[2,128,512]{2,1,0:T(8,128)(2,1)S(1)}, bf16[2,128,512]{2,1,0:T(8,128)(2,1)S(1)}, u32[]{:S(2)}, u32[]{:S(2)}) collective-permute-start(bf16[2,128,512]{2,1,0:T(8,128)(2,1)S(1)} %get-tuple-element.142), channel_id=1, source_target_pairs={{0,1},{1,0},{2,3},{3,2},{4,5},{5,4},{6,7},{7,6},{8,9},{9,8},{10,11... | collective-permute-start | bytes 786440 | tf_op jit(solution)/shard_map/ppermute | solution.py:43
  136.5 8.1 %collective-permute-start.34 = (bf16[2,128,256]{2,1,0:T(8,128)(2,1)S(1)}, bf16[2,128,256]{2,1,0:T(8,128)(2,1)S(1)}, u32[]{:S(2)}, u32[]{:S(2)}) collective-permute-start(bf16[2,128,256]{2,1,0:T(8,128)(2,1)S(1)} %get-tuple-element.143), channel_id=1, source_target_pairs={{0,1},{1,0},{2,3},{3,2},{4,5},{5,4},{6,7},{7,6},{8,9},{9,8},{10,11... | collective-permute-start | bytes 393224 | tf_op jit(solution)/shard_map/ppermute | solution.py:43
  137.7 13.5 %collective-permute-start.35 = (bf16[1,128,512]{2,1,0:T(8,128)(2,1)S(1)}, bf16[1,128,512]{2,1,0:T(8,128)(2,1)S(1)}, u32[]{:S(2)}, u32[]{:S(2)}) collective-permute-start(bf16[1,128,512]{2,1,0:T(8,128)(2,1)S(1)} %get-tuple-element.146), channel_id=1, source_target_pairs={{0,2},{1,3},{2,0},{3,1},{4,6},{5,7},{6,4},{7,5},{8,10},{9,11},{10,... | collective-permute-start | bytes 393224 | tf_op jit(solution)/shard_map/ppermute | solution.py:43
  148.2 5.7 %collective-permute-start.37 = (bf16[1,128,256]{2,1,0:T(8,128)(2,1)S(1)}, bf16[1,128,256]{2,1,0:T(8,128)(2,1)S(1)}, u32[]{:S(2)}, u32[]{:S(2)}) collective-permute-start(bf16[1,128,256]{2,1,0:T(8,128)(2,1)S(1)} %get-tuple-element.149), channel_id=1, source_target_pairs={{0,2},{1,3},{2,0},{3,1},{4,6},{5,7},{6,4},{7,5},{8,10},{9,11},{10,... | collective-permute-start | bytes 196616 | tf_op jit(solution)/shard_map/ppermute | solution.py:43
  149.0 6.3 %collective-permute-start.36 = (bf16[1,128,512]{2,1,0:T(8,128)(2,1)S(1)}, bf16[1,128,512]{2,1,0:T(8,128)(2,1)S(1)}, u32[]{:S(2)}, u32[]{:S(2)}) collective-permute-start(bf16[1,128,512]{2,1,0:T(8,128)(2,1)S(1)} %get-tuple-element.148), channel_id=1, source_target_pairs={{0,2},{1,3},{2,0},{3,1},{4,6},{5,7},{6,4},{7,5},{8,10},{9,11},{10,... | collective-permute-start | bytes 393224 | tf_op jit(solution)/shard_map/ppermute | solution.py:43
